TPU v7x, 32 devices: a whole 2x2x4 slice. The times are simulated.
32 devices in a mesh: wave: 4 (over y, x), row: 8 (over z, core).
Axes of the slice: x: 2, y: 2, z: 4, core: 2. Of those that a mesh axis runs over, the one named last changes fastest.
Arguments:
- plane_waves: float32 [2, 4, 2048, 2048], P(None, 'wave', 'row'), may hold values from -6 to 6
- transmission: float32 [1, 2, 2048, 2048], P(None, None, 'row')
- wave_index: int32 [4, 2], P('wave'), may hold values from -32 to 31
- wave_weight: float32 [4], P('wave'), may hold values from 0.3 to 3
- wave_phase: float32 [4], P('wave'), may hold values from -3.140625 to 3.140625
- probe_pos: int32 [64, 2], replicated, may hold values from 0 to 2047, as said below
Outputs:
- diffraction: float32 [64, 128, 128], P('row', 'wave')
Inputs may be any that keep to these rules, and one draw needn't show every extreme that they name: `probe_pos`: the probes numbered j * 8 to (j + 1) * 8 - 1 have their grid row (first entry) in j * 256 to (j + 1) * 256 - 1; the second entry is the grid column.
All inputs are finite; a program needn't handle non-finite values.
Results may differ from a plain program's by a relative error of at most 0.0003.
Values sent between devices are 32-bit elements; how exact they have to be, the bound alone decides.
No kernel may reach another device: no remote copies, remote signals or barrier semaphores. Data moves between devices by JAX's collectives and lax.ppermute only.
A program may use at most 128 MiB of HBM per device.

v0:
```python
import functools
import math

import jax
import jax.numpy as jnp
import numpy as np
from jax import lax
from jax.experimental import pallas as pl
from jax.experimental.pallas import tpu as pltpu
from jax.sharding import PartitionSpec as P

GRID = 2048
FACTOR = 16
WINDOW = 128
HALF = 64
FRESNEL = 0.1

BAND = math.isqrt(GRID * GRID // 9)
FOLD = GRID // 2
BLOCKS = 3
LANES = 128
PAIR = 2 * LANES
DEPTH = BLOCKS * PAIR
FREQS = BLOCKS * LANES
FINE = 64
COL_TILES = FOLD // PAIR


def angles_of(first, second):
    return (2.0 * math.pi / GRID) * (np.outer(first, second) % GRID)


def cos_sin(first, second):
    angle = angles_of(first, second)
    return np.stack([np.cos(angle), np.sin(angle)]).astype(np.float32)


def freqs(parity):
    return 2 * np.arange(FREQS) + parity


def both(function):
    return np.stack([function(freqs(0)), function(freqs(1))])


def halves_of(value):
    high = value.astype(jnp.bfloat16)
    return high, (value - high.astype(jnp.float32)).astype(jnp.bfloat16)


def dot3(left, right):
    def term(first, second):
        return jnp.dot(first, second, preferred_element_type=jnp.float32)

    return term(left[0], right[0]) + term(left[0], right[1]) + term(left[1], right[0])


def turn(first, second):
    return (
        first[0] * second[0] - first[1] * second[1],
        first[1] * second[0] + first[0] * second[1],
    )


def put(refs, place, value):
    high, low = halves_of(value)
    refs[0][place] = high
    refs[1][place] = low


def split_kernel(sign_ref, wave_ref, trans_ref, mine_ref, theirs_ref):
    wave_re, wave_im = wave_ref[0, 0], wave_ref[1, 0]
    trans_re, trans_im = trans_ref[0, 0], trans_ref[0, 1]
    sign = sign_ref[0]
    for part, value in enumerate(
        (wave_re * trans_re - wave_im * trans_im, wave_re * trans_im + wave_im * trans_re)
    ):
        low, high = value[:, :FOLD], sign * value[:, FOLD:]
        mine_ref[part] = low + high
        theirs_ref[part] = low - high


def split_columns(sign, plane_waves, transmission):
    rows = plane_waves.shape[2]
    step = 32
    out = jax.ShapeDtypeStruct((2, rows, FOLD), jnp.float32)
    out_spec = pl.BlockSpec((2, step, FOLD), lambda i, *_: (0, i, 0))
    return pl.pallas_call(
        split_kernel,
        out_shape=(out, out),
        grid_spec=pltpu.PrefetchScalarGridSpec(
            num_scalar_prefetch=1,
            grid=(rows // step,),
            in_specs=[
                pl.BlockSpec((2, 1, step, GRID), lambda i, *_: (0, 0, i, 0)),
                pl.BlockSpec((1, 2, step, GRID), lambda i, *_: (0, 0, i, 0)),
            ],
            out_specs=(out_spec, out_spec),
        ),
        cost_estimate=pl.CostEstimate(
            flops=20 * rows * GRID, bytes_accessed=24 * rows * GRID, transcendentals=0
        ),
        name="split_columns",
    )(sign, plane_waves, transmission)


def column_forward_kernel(parity_ref, field_ref, fine_ref, coarse_ref, out_ref, *scratch):
    field, table = scratch[:2], scratch[2:]
    rows = field_ref.shape[1]

    @pl.when(pl.program_id(0) == 0)
    def _():
        for part in (0, 1):
            put(field, slice(part * rows, (part + 1) * rows), field_ref[part])

    fine = fine_ref[0, 0], fine_ref[0, 1]
    for step in range(FOLD // FINE):
        place = slice(step, step + 1)
        value = turn((coarse_ref[0, 0, place], coarse_ref[0, 1, place]), fine)
        rows_here = slice(step * FINE, (step + 1) * FINE)
        put(table, (rows_here, slice(0, LANES)), value[0])
        put(table, (rows_here, slice(LANES, PAIR)), value[1])
    result = dot3((field[0][...], field[1][...]), (table[0][...], table[1][...]))
    for part in (0, 1):
        out_ref[part] = result[part * rows : (part + 1) * rows]


def column_forward(parity, field):
    rows = field.shape[1]
    fine = both(lambda freq: cos_sin(np.arange(FINE), freq))
    coarse = both(lambda freq: cos_sin(np.arange(0, FOLD, FINE), freq))
    half = functools.partial(pltpu.VMEM, dtype=jnp.bfloat16)
    return pl.pallas_call(
        column_forward_kernel,
        out_shape=jax.ShapeDtypeStruct((2, rows, DEPTH), jnp.float32),
        grid_spec=pltpu.PrefetchScalarGridSpec(
            num_scalar_prefetch=1,
            grid=(BLOCKS,),
            in_specs=[
                pl.BlockSpec((2, rows, FOLD), lambda j, *_: (0, 0, 0)),
                pl.BlockSpec((1, 2, FINE, LANES), lambda j, c: (c[0], 0, 0, j)),
                pl.BlockSpec((1, 2, FOLD // FINE, LANES), lambda j, c: (c[0], 0, 0, j)),
            ],
            out_specs=pl.BlockSpec((2, rows, PAIR), lambda j, *_: (0, 0, j)),
            scratch_shapes=[half((2 * rows, FOLD))] * 2 + [half((FOLD, PAIR))] * 2,
        ),
        cost_estimate=pl.CostEstimate(
            flops=12 * rows * FOLD * DEPTH,
            bytes_accessed=8 * rows * (FOLD + DEPTH),
            transcendentals=0,
        ),
        name="column_forward",
    )(parity, field, jnp.asarray(fine), jnp.asarray(coarse))


def row_forward_kernel(
    parity_ref, mine_ref, theirs_ref, fine_ref, coarse_ref, down_ref, along_ref,
    out_hi, out_lo, table_hi, table_lo,
):
    tables = (table_hi, table_lo)

    @pl.when(pl.program_id(0) == 0)
    def _():
        for block in range(2 * BLOCKS):
            freq = slice(block * LANES, (block + 1) * LANES)
            fine = fine_ref[0, freq], fine_ref[1, freq]
            for step in range(coarse_ref.shape[3]):
                place = slice(step, step + 1)
                value = turn((coarse_ref[0, 0, freq, place], coarse_ref[0, 1, freq, place]), fine)
                cols = slice(step * LANES, (step + 1) * LANES)
                for kind in (0, 1):
                    start = block * PAIR + kind * LANES
                    put(tables, (slice(start, start + LANES), cols), value[kind])

    parts = [
        halves_of(jnp.concatenate([mine_ref[part], theirs_ref[part]])) for part in (0, 1)
    ]
    cos_x, sin_x, square_x = (along_ref[0, i : i + 1] for i in range(3))

    def blocks(parity, count):
        rows = slice(parity * DEPTH, parity * DEPTH + count * PAIR)
        table = table_hi[rows], table_lo[rows]
        real_part, imag_part = dot3(table, parts[0]), dot3(table, parts[1])
        cos_y, sin_y, square_y = (down_ref[rows, i : i + 1] for i in range(3))
        inside = 9.0 * (square_y + square_x) <= GRID * GRID
        prop_re = jnp.where(inside, cos_y * cos_x - sin_y * sin_x, 0.0)
        prop_im = jnp.where(inside, -(sin_y * cos_x + cos_y * sin_x), 0.0)
        outs = (out_hi, out_lo)
        put(outs, (0, rows), prop_re * real_part - prop_im * imag_part)
        put(outs, (1, rows), prop_re * imag_part + prop_im * real_part)

    last = pl.program_id(0) == BLOCKS - 1
    for parity in (0, 1):
        pl.when(last)(functools.partial(blocks, parity, BLOCKS - 1))
        pl.when(jnp.logical_not(last))(functools.partial(blocks, parity, BLOCKS))


def axis_factors(freq):
    angle = freq.astype(np.float64) ** 2 * (math.pi * FRESNEL / GRID)
    weight = np.where(freq == 0, 1.0, 2.0) / GRID
    return [np.cos(angle) * weight, np.sin(angle) * weight, freq.astype(np.float64) ** 2]


def paired(values):
    blocks = values.reshape(values.shape[:-1] + (-1, 1, LANES))
    return np.concatenate([blocks, blocks], -2).reshape(values.shape[:-1] + (-1,))


def row_forward(parity, mine, theirs):
    rows = mine.shape[1]
    all_freqs = np.concatenate([freqs(0), freqs(1)])
    fine = cos_sin(all_freqs, np.arange(LANES))
    starts = np.arange(0, rows, LANES)
    coarse = np.stack(
        [
            cos_sin(all_freqs, np.concatenate([starts + rows * core, starts + rows * (1 - core)]))
            for core in (0, 1)
        ]
    )
    down = paired(np.stack(axis_factors(all_freqs))).T
    along = np.stack([paired(np.stack(axis_factors(freqs(core)))) for core in (0, 1)])
    down, along = down.astype(np.float32), along.astype(np.float32)
    tile = pl.BlockSpec((2, rows, PAIR), lambda j, *_: (0, 0, j))
    out = jax.ShapeDtypeStruct((2, 2 * DEPTH, DEPTH), jnp.bfloat16)
    out_spec = pl.BlockSpec((2, 2 * DEPTH, PAIR), lambda j, *_: (0, 0, j))
    return pl.pallas_call(
        row_forward_kernel,
        out_shape=(out, out),
        grid_spec=pltpu.PrefetchScalarGridSpec(
            num_scalar_prefetch=1,
            grid=(BLOCKS,),
            in_specs=[
                tile,
                tile,
                pl.BlockSpec(fine.shape, lambda j, *_: (0, 0, 0)),
                pl.BlockSpec((1,) + coarse.shape[1:], lambda j, c: (c[0], 0, 0, 0)),
                pl.BlockSpec(down.shape, lambda j, *_: (0, 0)),
                pl.BlockSpec((1, 3, PAIR), lambda j, c: (c[0], 0, j)),
            ],
            out_specs=(out_spec, out_spec),
            scratch_shapes=[pltpu.VMEM((2 * DEPTH, 2 * rows), jnp.bfloat16)] * 2,
        ),
        cost_estimate=pl.CostEstimate(
            flops=48 * rows * DEPTH * DEPTH,
            bytes_accessed=16 * rows * DEPTH + 16 * DEPTH * DEPTH,
            transcendentals=0,
        ),
        name="row_forward",
    )(
        parity, mine, theirs, jnp.asarray(fine), jnp.asarray(coarse), jnp.asarray(down),
        jnp.asarray(along),
    )


def row_inverse_kernel(steps, spec_hi, spec_lo, fine_ref, coarse_ref, out_hi, out_lo, *tables):
    count = len(steps) * FINE

    @pl.when(pl.program_id(0) == 0)
    def _():
        for block in range(2 * BLOCKS):
            freq = slice(block * LANES, (block + 1) * LANES)
            fine = fine_ref[0, :, freq], fine_ref[1, :, freq]
            for index, step in enumerate(steps):
                place = slice(step, step + 1)
                value = turn((coarse_ref[0, place, freq], coarse_ref[1, place, freq]), fine)
                rows = slice(index * FINE, (index + 1) * FINE)
                for kind in (0, 1):
                    start = block * PAIR + kind * LANES
                    put(tables, (rows, slice(start, start + LANES)), value[kind])

    def blocks(depth):
        sums = []
        for parity in (0, 1):
            part = slice(parity * DEPTH, parity * DEPTH + depth * PAIR)
            sums.append(
                dot3((tables[0][:, part], tables[1][:, part]), (spec_hi[0, part], spec_lo[0, part]))
            )
        outs = (out_hi, out_lo)
        put(outs, (0, slice(0, count)), sums[0] + sums[1])
        put(outs, (0, slice(count, 2 * count)), sums[0] - sums[1])

    last = pl.program_id(0) % BLOCKS == BLOCKS - 1
    pl.when(last)(functools.partial(blocks, BLOCKS - 1))
    pl.when(jnp.logical_not(last))(functools.partial(blocks, BLOCKS))


def row_inverse(spectrum, steps):
    count = len(steps) * FINE
    all_freqs = np.concatenate([freqs(0), freqs(1)])
    fine = cos_sin(np.arange(FINE), all_freqs)
    coarse = cos_sin(np.arange(-HALF, FOLD + HALF, FINE), all_freqs)
    out = jax.ShapeDtypeStruct((2, 2 * count, DEPTH), jnp.bfloat16)
    tile = pl.BlockSpec((1, 2 * count, PAIR), lambda j: (j // BLOCKS, 0, j % BLOCKS))
    spec = pl.BlockSpec((1, 2 * DEPTH, PAIR), lambda j: (j // BLOCKS, 0, j % BLOCKS))
    return pl.pallas_call(
        functools.partial(row_inverse_kernel, steps),
        out_shape=(out, out),
        grid=(2 * BLOCKS,),
        in_specs=[
            spec,
            spec,
            pl.BlockSpec(fine.shape, lambda j: (0, 0, 0)),
            pl.BlockSpec(coarse.shape, lambda j: (0, 0, 0)),
        ],
        out_specs=(tile, tile),
        scratch_shapes=[pltpu.VMEM((count, 2 * DEPTH), jnp.bfloat16)] * 2,
        cost_estimate=pl.CostEstimate(
            flops=24 * count * DEPTH * DEPTH,
            bytes_accessed=16 * DEPTH * DEPTH + 16 * count * DEPTH,
            transcendentals=0,
        ),
        name="row_inverse",
    )(*spectrum, jnp.asarray(fine), jnp.asarray(coarse))


def column_inverse_kernel(
    layout, info_ref, slot_ref, pos_ref, re_ref, im_ref, sign_ref,
    rows_hi, rows_lo, fine_ref, coarse_ref, keep_ref, send_ref, field, table_hi, table_lo,
):
    chip_rows, chips, waves, own = layout
    step = pl.program_id(0)
    tile = step % COL_TILES
    tables = (table_hi, table_lo)

    @pl.when(step < COL_TILES)
    def _():
        for block in range(BLOCKS):
            freq = slice(block * LANES, (block + 1) * LANES)
            fine = fine_ref[0, 0, freq], fine_ref[0, 1, freq]
            for side in (0, 1):
                place = slice(side, side + 1)
                value = turn(
                    (coarse_ref[0, 0, 0, freq, place], coarse_ref[0, 0, 1, freq, place]), fine
                )
                cols = slice(side * LANES, (side + 1) * LANES)
                for kind in (0, 1):
                    start = block * PAIR + kind * LANES
                    put(tables, (tile, slice(start, start + LANES), cols), value[kind])

    @pl.when(step < 2 * COL_TILES)
    def _():
        part = step // COL_TILES
        value = dot3((rows_hi[0], rows_lo[0]), (table_hi[tile], table_lo[tile]))
        field[part, 2 * tile] = value[:, :LANES]
        field[part, 2 * tile + 1] = value[:, LANES:]

        @pl.when(tile == 0)
        def _():
            field[part, 2 * COL_TILES] = value[:, :LANES] * sign_ref[0]

    @pl.when(step == 2 * COL_TILES)
    def _():
        lane = lax.broadcasted_iota(jnp.int32, (WINDOW, WINDOW), 1)
        row_rank, wave_rank = info_ref[0], info_ref[1]
        far = chips // 2
        segments = far // 2

        def one(index, out_ref, place):
            target = row_rank ^ slot_ref[0, index]
            probe = (target * waves + (wave_rank ^ slot_ref[1, index])) * own + slot_ref[2, index]
            away = lax.rem(target // 2 - row_rank // 2 + chips, chips)
            segment = away // far * segments + lax.rem(away, far) // 2
            row = segment * (chip_rows + WINDOW) + lax.rem(pos_ref[0, probe], chip_rows)
            start = lax.rem(pos_ref[1, probe] + (GRID - HALF), GRID)
            col = lax.rem(start, FOLD)
            turned = jnp.where(start >= FOLD, sign_ref[0], 1.0)
            shift = lax.rem(col, LANES)
            back = lax.rem(LANES - shift, LANES)

            def cut(part):
                sides = [
                    pltpu.roll(field[part, col // LANES + side, pl.ds(row, WINDOW)], back, 1)
                    for side in (0, 1)
                ]
                return jnp.where(lane < LANES - shift, sides[0], sides[1])

            real_part, imag_part = cut(0), cut(1)
            weight_re, weight_im = re_ref[probe] * turned, im_ref[probe] * turned
            out_ref[place, 0] = weight_re * real_part - weight_im * imag_part
            out_ref[place, 1] = weight_re * imag_part + weight_im * real_part

        count = keep_ref.shape[0]

        @pl.loop(0, count)
        def _(place):
            one(place, keep_ref, place)
            one(count + place, send_ref, place)


def column_inverse(layout, rows, slots, info, positions, weights, sign):
    count = slots.shape[1] // 2
    height = rows[0].shape[1]
    fine = both(lambda freq: cos_sin(freq, np.arange(LANES)))
    coarse = both(
        lambda freq: np.stack(
            [cos_sin(freq, PAIR * tile + np.array([0, LANES])) for tile in range(COL_TILES)]
        )
    )
    last = 2 * COL_TILES - 1
    rows_spec = pl.BlockSpec(
        (1, height, DEPTH), lambda i, *_: (jnp.minimum(i, last) // COL_TILES, 0, 0)
    )
    out = jax.ShapeDtypeStruct((count, 2, WINDOW, WINDOW), jnp.float32)
    out_spec = pl.BlockSpec(
        (count, 2, WINDOW, WINDOW), lambda i, *_: (0, 0, 0, 0), pipeline_mode=pl.Buffered(1)
    )
    return pl.pallas_call(
        functools.partial(column_inverse_kernel, layout),
        out_shape=(out, out),
        grid_spec=pltpu.PrefetchScalarGridSpec(
            num_scalar_prefetch=6,
            grid=(2 * COL_TILES + 1,),
            in_specs=[
                rows_spec,
                rows_spec,
                pl.BlockSpec((1,) + fine.shape[1:], lambda i, info, *_: (info[2], 0, 0, 0)),
                pl.BlockSpec(
                    (1, 1) + coarse.shape[2:],
                    lambda i, info, *_: (info[2], jnp.minimum(i, COL_TILES - 1), 0, 0, 0),
                ),
            ],
            out_specs=(out_spec, out_spec),
            scratch_shapes=[
                pltpu.VMEM((2, 2 * COL_TILES + 1, height, WINDOW), jnp.float32),
                pltpu.VMEM((COL_TILES, DEPTH, PAIR), jnp.bfloat16),
                pltpu.VMEM((COL_TILES, DEPTH, PAIR), jnp.bfloat16),
            ],
        ),
        cost_estimate=pl.CostEstimate(
            flops=12 * height * DEPTH * FOLD,
            bytes_accessed=8 * height * DEPTH + 16 * count * WINDOW * WINDOW,
            transcendentals=0,
        ),
        name="column_inverse",
    )(
        info, jnp.asarray(slots), positions, *weights, sign, *rows, jnp.asarray(fine),
        jnp.asarray(coarse),
    )


def coefficients(positions, wave_index, wave_weight, wave_phase):
    turns = (FACTOR * (positions[0] * wave_index[0, 0] + positions[1] * wave_index[0, 1])) % GRID
    angles = wave_phase[0] - turns.astype(jnp.float32) * (2.0 * math.pi / GRID)
    return wave_weight[0] * jnp.cos(angles), wave_weight[0] * jnp.sin(angles)


def flip(block, axis, bit):
    count = lax.axis_size(axis)
    return lax.ppermute(block, axis, [(i, i ^ bit) for i in range(count)])


def exchange(parts, axis, bit):
    return parts[0] + flip(parts[1], axis, bit)


def shards(plane_waves, transmission, wave_index, wave_weight, wave_phase, probe_pos):
    rows_here = plane_waves.shape[2]
    row_count = lax.axis_size("row")
    wave_count = lax.axis_size("wave")
    row_rank = lax.axis_index("row")
    wave_rank = lax.axis_index("wave")
    core = row_rank % 2
    sign = (1.0 - 2.0 * core.astype(jnp.float32))[None]
    parity = core[None]
    info = jnp.stack([row_rank, wave_rank, core])
    chip_rows = 2 * rows_here
    chips = row_count // 2
    far = chips // 2
    own = probe_pos.shape[0] // (row_count * wave_count)

    mine, theirs = split_columns(sign, plane_waves, transmission)
    theirs = flip(theirs, "row", 1)
    positions = probe_pos.T
    weights = coefficients(positions, wave_index, wave_weight, wave_phase)
    mine = column_forward(parity, mine)
    mine, theirs = lax.optimization_barrier((mine, theirs))
    spectrum = row_forward(parity, mine, column_forward(parity, theirs))

    wave_bits = wave_count.bit_length() - 1
    orders = (list(range(wave_bits - 1, -1, -1)), list(range(wave_bits)))
    order_of = [orders[0 if index < far // 2 else 1] for index in range(far)]
    layout = (chip_rows, chips, wave_count, own)

    def slots_of(odd):
        slots = []
        for core_bit in (0, 1):
            for index in range(far):
                for digits in range(wave_count):
                    wave = 0
                    for place, bit in enumerate(order_of[index]):
                        wave |= (digits >> (wave_bits - 1 - place) & 1) << bit
                    for probe in range(own):
                        slots.append(((index * 2 + odd) * 2 + core_bit, wave, probe))
        return np.array(slots, np.int32).T

    def steps_of(odd):
        steps = []
        for away in range(odd, far, 2):
            first = chip_rows * away // FINE
            steps += range(first, first + (chip_rows + WINDOW) // FINE)
        return tuple(steps)

    def by_half(parts):
        return [
            parts[half * (far // 2) : (half + 1) * (far // 2)].reshape(
                (far // 2, wave_count, own, 2, WINDOW, WINDOW)
            )
            for half in (0, 1)
        ]

    def column_part(odd, rows):
        keep, send = column_inverse(layout, rows, slots_of(odd), info, positions, weights, sign)
        return keep, flip(send, "row", 1)

    def add_core(keep, arrived):
        shape = (far, wave_count, own, 2, WINDOW, WINDOW)
        keep, arrived = by_half(keep.reshape(shape)), by_half(arrived.reshape(shape))
        middle = wave_count // 2
        return [
            (a[:, :middle] + b[:, :middle], a[:, middle:] + b[:, middle:])
            for a, b in zip(keep, arrived)
        ]

    def over_waves(halves):
        sums = []
        for (stay, send), order in zip(halves, orders):
            for place, bit in enumerate(order):
                arrived = flip(send, "wave", 1 << bit)
                middle = stay.shape[1] // 2
                if place + 1 < wave_bits:
                    stay, send = (
                        stay[:, :middle] + arrived[:, :middle],
                        stay[:, middle:] + arrived[:, middle:],
                    )
                else:
                    stay = stay + arrived
            sums.append(stay[:, 0])
        return sums

    rows_odd = row_inverse(spectrum, steps_of(1))
    keep_odd, arrived_odd = column_part(1, rows_odd)
    spectrum, keep_odd = lax.optimization_barrier((spectrum, keep_odd))
    rows_even = row_inverse(spectrum, steps_of(0))
    halves_odd = add_core(keep_odd, arrived_odd)
    rows_even, halves_odd = lax.optimization_barrier((rows_even, halves_odd))
    sums_odd = over_waves(halves_odd)
    sums_even = over_waves(add_core(*column_part(0, rows_even)))
    parts = [even + flip(odd, "row", 2) for even, odd in zip(sums_even, sums_odd)]
    bit = row_count // 2
    parts = exchange(parts, "row", bit)
    while bit > 4:
        bit //= 2
        parts = exchange(parts.reshape((2, -1) + parts.shape[1:]), "row", bit)
    window = parts[0]

    angle = angles_of(np.arange(WINDOW), FACTOR * np.arange(WINDOW))
    cos_t = jnp.asarray(np.cos(angle).astype(np.float32))
    sin_t = jnp.asarray(np.sin(angle).astype(np.float32))

    def one_dft(formula, halves):
        def term(table, value):
            return jnp.einsum(formula, table, value, precision=lax.Precision.HIGHEST)

        return (
            term(cos_t, halves[0]) + term(sin_t, halves[1]),
            term(cos_t, halves[1]) - term(sin_t, halves[0]),
        )

    halves = one_dft("ki,pij->pkj", (window[:, 0], window[:, 1]))
    halves = one_dft("kj,pij->pik", halves)
    total_waves = plane_waves.shape[1] * wave_count
    power = (halves[0] * halves[0] + halves[1] * halves[1]) / (WINDOW * WINDOW * total_waves)
    return lax.all_to_all(power, "wave", split_axis=1, concat_axis=0, tiled=True)


def solution(mesh):
    return jax.shard_map(
        shards,
        mesh=mesh,
        in_specs=(
            P(None, "wave", "row", None),
            P(None, None, "row", None),
            P("wave", None),
            P("wave"),
            P("wave"),
            P(),
        ),
        out_specs=P("row", "wave", None),
        check_vma=False,
    )
```

profile of v0, /device:TPU:0, one launch (start us, length us, event | category | flops | bytes accessed | tf_op | source)
XLA Modules:
  0.0 215.0 jit_solution(9024267351557307369)
XLA Ops:
  0.0 7.8 %split_columns.1 = (f32[2,256,1024]{2,1,0:T(8,128)}, f32[2,256,1024]{2,1,0:T(8,128)}) custom-call(f32[1]{0:T(128)} %bitcast.9.sign_ref, f32[2,1,256,2048]{3,2,1,0:T(8,128)} %wave_ref.1, f32[1,2,256,2048]{3,2,1,0:T(8,128)} %trans_ref.1), custom_call_target="tpu_custom_call" | custom-call | flops 10485760 | bytes 12582912 | tf_op jit(solution)/shard_map/split_columns/pallas_call | solution.py:88
  10.7 1.8 sine_multiply_fusion
  13.1 6.3 %column_forward.2.mine_ref = f32[2,256,768]{2,1,0:T(8,128)} custom-call(s32[1]{0:T(128)} %bitcast.2.parity_ref, f32[2,256,1024]{2,1,0:T(8,128)} %get-tuple-element.28.field_ref, f32[2,2,64,384]{3,2,1,0:T(8,128)} %constant.74.clone.fine_ref, f32[2,2,16,384]{3,2,1,0:T(8,128)} %constant.75.clone.coarse_ref), custom_call_target="tpu_custom_call" | custom-call | flops 2415919104 | bytes 3670016 | tf_op jit(solution)/shard_map/column_forward/pallas_call | solution.py:133
  20.8 6.3 %column_forward.3.theirs_ref = f32[2,256,768]{2,1,0:T(8,128)} custom-call(s32[1]{0:T(128)} %bitcast.2.parity_ref, f32[2,256,1024]{2,1,0:T(8,128)} %copy-done.9, f32[2,2,64,384]{3,2,1,0:T(8,128)} %constant.74.clone.fine_ref, f32[2,2,16,384]{3,2,1,0:T(8,128)} %constant.75.clone.coarse_ref), custom_call_target="tpu_custom_call" | custom-call | flops 2415919104 | bytes 3670016 | tf_op jit(solution)/shard_map/column_forward/pallas_call | solution.py:133
  27.1 14.7 %row_forward.1 = (bf16[2,1536,768]{2,1,0:T(8,128)(2,1)}, bf16[2,1536,768]{2,1,0:T(8,128)(2,1)}) custom-call(s32[1]{0:T(128)} %bitcast.2.parity_ref, f32[2,256,768]{2,1,0:T(8,128)} %column_forward.2.mine_ref, f32[2,256,768]{2,1,0:T(8,128)} %column_forward.3.theirs_ref, f32[2,768,128]{2,1,0:T(8,128)} %constant.76.clone.fine_ref, ...), custom_call_target="tpu_custom_call" | custom-call | flops 7247757312 | bytes 12582912 | tf_op jit(solution)/shard_map/row_forward/pallas_call | solution.py:226
  41.8 14.0 %row_inverse.2 = (bf16[2,1280,768]{2,1,0:T(8,128)(2,1)}, bf16[2,1280,768]{2,1,0:T(8,128)(2,1)}) custom-call(bf16[2,1536,768]{2,1,0:T(8,128)(2,1)} %get-tuple-element.37.spec_hi, bf16[2,1536,768]{2,1,0:T(8,128)(2,1)} %get-tuple-element.38.spec_lo, f32[2,64,768]{2,1,0:T(8,128)} %constant.80.clone.fine_ref, f32[2,18,768]{2,1,0:T(8,128)} %constant.81.clone.coarse_ref), custom_call_target="tpu_custom_call" | custom-call | flops 9059696640 | bytes 17301504 | tf_op jit(solution)/shard_map/row_inverse/pallas_call | solution.py:295
  55.7 24.5 %column_inverse.2 = (f32[16,2,128,128]{3,2,1,0:T(8,128)}, f32[16,2,128,128]{3,2,1,0:T(8,128)}) custom-call(s32[3]{0:T(128)} %pad_add_fusion.info_ref, s32[3,32]{1,0:T(4,128)} %constant.82.clone.slot_ref, s32[2,64]{1,0:T(2,128)} %bitcast.80, f32[64]{0:T(128)} %cosine_multiply_fusion.re_ref, f32[64]{0:T(128)} %get-tuple-element.51.im_ref, f32[1]{0:T(128)} %bitcast.9.sign_ref, ...), custom_call_target="tpu_custom_call" | custom-call | flops 12079595520 | bytes 12058624 | tf_op jit(solution)/shard_map/column_inverse/pallas_call | solution.py:407
  80.2 1.7 fusion.28
  82.9 14.0 %row_inverse.3 = (bf16[2,1280,768]{2,1,0:T(8,128)(2,1)}, bf16[2,1280,768]{2,1,0:T(8,128)(2,1)}) custom-call(bf16[2,1536,768]{2,1,0:T(8,128)(2,1)} %get-tuple-element.37.spec_hi, bf16[2,1536,768]{2,1,0:T(8,128)(2,1)} %get-tuple-element.38.spec_lo, f32[2,64,768]{2,1,0:T(8,128)} %constant.80.clone.fine_ref, f32[2,18,768]{2,1,0:T(8,128)} %constant.81.clone.coarse_ref), custom_call_target="tpu_custom_call" | custom-call | flops 9059696640 | bytes 17301504 | tf_op jit(solution)/shard_map/row_inverse/pallas_call | solution.py:295
  96.9 1.7 fusion.27
  99.7 2.1 copy.77
  104.1 2.1 copy.79
  106.2 2.1 copy.75
  110.2 24.4 %column_inverse.3 = (f32[16,2,128,128]{3,2,1,0:T(8,128)}, f32[16,2,128,128]{3,2,1,0:T(8,128)}) custom-call(s32[3]{0:T(128)} %pad_add_fusion.info_ref, s32[3,32]{1,0:T(4,128)} %constant.85.clone.slot_ref, s32[2,64]{1,0:T(2,128)} %bitcast.81, f32[64]{0:T(128)} %cosine_multiply_fusion.re_ref, f32[64]{0:T(128)} %get-tuple-element.51.im_ref, f32[1]{0:T(128)} %bitcast.9.sign_ref, ...), custom_call_target="tpu_custom_call" | custom-call | flops 12079595520 | bytes 12058624 | tf_op jit(solution)/shard_map/column_inverse/pallas_call | solution.py:407
  135.0 2.5 %collective-permute-start.5 = (f32[1,2,2,2,128,128]{4,5,2,3,1,0:T(8,128)}, f32[1,2,2,2,128,128]{4,5,2,3,1,0:T(8,128)}, u32[]{:S(2)}, u32[]{:S(2)}) collective-permute-start(f32[1,2,2,2,128,128]{4,5,2,3,1,0:T(8,128)} %add.99), channel_id=1, source_target_pairs={{0,16},{8,24},{16,0},{24,8},{1,17},{9,25},{17,1},{25,9},{2,18},{10... | collective-permute-start | bytes 1572872 | tf_op jit(solution)/shard_map/ppermute | solution.py:449
  144.0 2.1 copy.84
  148.6 1.9 collective-permute-done.5
  151.5 1.8 collective-permute-start.6
  153.2 1.7 fusion.25
  156.0 2.0 copy.89
  158.0 2.1 add.112
  160.5 1.7 collective-permute-done.10
  162.2 1.7 slice_add_fusion
  166.2 1.9 add.103
  168.1 2.0 collective-permute-start.3
  170.1 2.0 collective-permute-done.11
  172.1 1.8 fusion.7
  180.7 1.9 collective-permute-start.7
  185.6 2.1 collective-permute-done.9
  188.8 2.6 %collective-permute-start.13 = (f32[1,2,2,128,128]{3,4,1,2,0:T(8,128)S(1)}, f32[1,2,2,128,128]{3,4,1,2,0:T(8,128)S(1)}, u32[]{:S(2)}, u32[]{:S(2)}) collective-permute-start(f32[1,2,2,128,128]{3,4,1,2,0:T(8,128)S(1)} %fusion.10), channel_id=1, source_target_pairs={{0,4},{1,5},{2,6},{3,7},{4,0},{5,1},{6,2},{7,3},{8,12},{9,13},{10,... | collective-permute-start | bytes 786440 | tf_op jit(solution)/shard_map/ppermute | solution.py:449
  191.5 11.4 %collective-permute-done.13 = f32[1,2,2,128,128]{3,4,1,2,0:T(8,128)S(1)} collective-permute-done((f32[1,2,2,128,128]{3,4,1,2,0:T(8,128)S(1)}, f32[1,2,2,128,128]{3,4,1,2,0:T(8,128)S(1)}, u32[]{:S(2)}, u32[]{:S(2)}) %collective-permute-start.13) | collective-permute-done | bytes 262176 | tf_op jit(solution)/shard_map/ppermute | solution.py:449
  206.8 7.6 %all_to_all.18 = f32[2,128,128]{2,0,1:T(2,128)S(1)} all-to-all(f32[2,128,128]{2,0,1:T(2,128)S(1)} %copy.68), channel_id=1, replica_groups=mesh['wave'=4,'row'=8] {'wave'}, dimensions={1} | all-to-all | bytes 262144 | tf_op jit(solution)/shard_map/all_to_all | solution.py:573
  (83 shorter events, 39.4 us)
Async XLA Ops:
  0.0 10.1 %copy-start.7 = (s32[1,2]{1,0:T(1,128)S(1)}, s32[1,2]{1,0:T(1,128)}, u32[]{:S(2)}) copy-start(s32[1,2]{1,0:T(1,128)} %param.28) | copy-start | bytes 28
  0.0 10.7 %copy-start.8 = (s32[64,2]{0,1:T(2,128)S(1)}, s32[64,2]{0,1:T(2,128)}, u32[]{:S(2)}) copy-start(s32[64,2]{0,1:T(2,128)} %param.31) | copy-start | bytes 1540
  7.8 11.6 %collective-permute-start = (f32[2,256,1024]{2,1,0:T(8,128)}, f32[2,256,1024]{2,1,0:T(8,128)S(1)}, u32[]{:S(2)}, u32[]{:S(2)}) collective-permute-start(f32[2,256,1024]{2,1,0:T(8,128)} %get-tuple-element.29), channel_id=1, source_target_pairs={{0,1},{1,0},{2,3},{3,2},{4,5},{5,4},{6,7},{7,6},{8,9},{9,8},{10,11... | collective-permute-start | bytes 6291464 | tf_op jit(solution)/shard_map/ppermute | solution.py:449
  19.4 1.4 copy-start.9
  80.2 16.7 %collective-permute-start.1 = (f32[16,2,128,128]{3,2,1,0:T(8,128)}, f32[16,2,128,128]{3,2,1,0:T(8,128)}, u32[]{:S(2)}, u32[]{:S(2)}) collective-permute-start(f32[16,2,128,128]{3,2,1,0:T(8,128)} %get-tuple-element.42), channel_id=1, source_target_pairs={{0,1},{1,0},{2,3},{3,2},{4,5},{5,4},{6,7},{7,6},{8,9},{9,8},{10,11... | collective-permute-start | bytes 6291464 | tf_op jit(solution)/shard_map/ppermute | solution.py:449
  102.8 5.4 %copy-start = (f32[1,2,2,2,128,128]{4,5,2,3,1,0:T(8,128)S(1)}, f32[1,2,2,2,128,128]{4,5,2,3,1,0:T(8,128)}, u32[]{:S(2)}) copy-start(f32[1,2,2,2,128,128]{4,5,2,3,1,0:T(8,128)} %copy.77) | copy-start | bytes 1572868
  108.2 1.8 copy-start.1
  108.2 1.8 copy-start.2
  134.5 18.7 %collective-permute-start.2 = (f32[16,2,128,128]{3,2,1,0:T(8,128)}, f32[16,2,128,128]{3,2,1,0:T(8,128)}, u32[]{:S(2)}, u32[]{:S(2)}) collective-permute-start(f32[16,2,128,128]{3,2,1,0:T(8,128)} %get-tuple-element.46), channel_id=1, source_target_pairs={{0,1},{1,0},{2,3},{3,2},{4,5},{5,4},{6,7},{7,6},{8,9},{9,8},{10,11... | collective-permute-start | bytes 6291464 | tf_op jit(solution)/shard_map/ppermute | solution.py:449
  135.0 15.4 %collective-permute-start.5 = (f32[1,2,2,2,128,128]{4,5,2,3,1,0:T(8,128)}, f32[1,2,2,2,128,128]{4,5,2,3,1,0:T(8,128)}, u32[]{:S(2)}, u32[]{:S(2)}) collective-permute-start(f32[1,2,2,2,128,128]{4,5,2,3,1,0:T(8,128)} %add.99), channel_id=1, source_target_pairs={{0,16},{8,24},{16,0},{24,8},{1,17},{9,25},{17,1},{25,9},{2,18},{10... | collective-permute-start | bytes 1572872 | tf_op jit(solution)/shard_map/ppermute | solution.py:449
  142.6 3.4 %copy-start.4 = (f32[1,2,2,2,128,128]{5,4,3,2,1,0:T(8,128)S(1)}, f32[1,2,2,2,128,128]{5,4,3,2,1,0:T(8,128)}, u32[]{:S(2)}) copy-start(f32[1,2,2,2,128,128]{5,4,3,2,1,0:T(8,128)} %get-tuple-element.68) | copy-start | bytes 1572868
  147.1 15.1 %collective-permute-start.10 = (f32[1,2,2,2,128,128]{4,5,2,3,1,0:T(8,128)}, f32[1,2,2,2,128,128]{4,5,2,3,1,0:T(8,128)}, u32[]{:S(2)}, u32[]{:S(2)}) collective-permute-start(f32[1,2,2,2,128,128]{4,5,2,3,1,0:T(8,128)} %add.101), channel_id=1, source_target_pairs={{0,8},{8,0},{16,24},{24,16},{1,9},{9,1},{17,25},{25,17},{2,10},{10... | collective-permute-start | bytes 1572872 | tf_op jit(solution)/shard_map/ppermute | solution.py:449
  151.5 28.2 %collective-permute-start.6 = (f32[1,1,2,2,128,128]{4,5,2,3,1,0:T(8,128)S(1)}, f32[1,1,2,2,128,128]{4,5,2,3,1,0:T(8,128)}, u32[]{:S(2)}, u32[]{:S(2)}) collective-permute-start(f32[1,1,2,2,128,128]{4,5,2,3,1,0:T(8,128)S(1)} %slice_add_fusion.4), channel_id=1, source_target_pairs={{0,8},{8,0},{16,24},{24,16},{1,9},{9,1},{17,25},{25,17},{2,10},{10... | collective-permute-start | bytes 786440 | tf_op jit(solution)/shard_map/ppermute | solution.py:449
  160.1 18.2 %collective-permute-start.8 = (f32[1,2,2,2,128,128]{4,5,2,3,1,0:T(8,128)}, f32[1,2,2,2,128,128]{4,5,2,3,1,0:T(8,128)}, u32[]{:S(2)}, u32[]{:S(2)}) collective-permute-start(f32[1,2,2,2,128,128]{4,5,2,3,1,0:T(8,128)} %add.112), channel_id=1, source_target_pairs={{0,8},{8,0},{16,24},{24,16},{1,9},{9,1},{17,25},{25,17},{2,10},{10... | collective-permute-start | bytes 1572872 | tf_op jit(solution)/shard_map/ppermute | solution.py:449
  163.8 8.3 %collective-permute-start.11 = (f32[1,1,2,2,128,128]{4,5,2,3,1,0:T(8,128)}, f32[1,1,2,2,128,128]{4,5,2,3,1,0:T(8,128)}, u32[]{:S(2)}, u32[]{:S(2)}) collective-permute-start(f32[1,1,2,2,128,128]{4,5,2,3,1,0:T(8,128)} %slice_add_fusion), channel_id=1, source_target_pairs={{0,16},{8,24},{16,0},{24,8},{1,17},{9,25},{17,1},{25,9},{2,18},{10... | collective-permute-start | bytes 786440 | tf_op jit(solution)/shard_map/ppermute | solution.py:449
  168.1 15.0 %collective-permute-start.3 = (f32[1,2,2,2,128,128]{4,5,2,3,1,0:T(8,128)}, f32[1,2,2,2,128,128]{4,5,2,3,1,0:T(8,128)}, u32[]{:S(2)}, u32[]{:S(2)}) collective-permute-start(f32[1,2,2,2,128,128]{4,5,2,3,1,0:T(8,128)} %add.103), channel_id=1, source_target_pairs={{0,16},{8,24},{16,0},{24,8},{1,17},{9,25},{17,1},{25,9},{2,18},{10... | collective-permute-start | bytes 1572872 | tf_op jit(solution)/shard_map/ppermute | solution.py:449
  173.9 11.8 %collective-permute-start.12 = (f32[1,2,2,128,128]{3,4,1,2,0:T(8,128)}, f32[1,2,2,128,128]{3,4,1,2,0:T(8,128)}, u32[]{:S(2)}, u32[]{:S(2)}) collective-permute-start(f32[1,2,2,128,128]{3,4,1,2,0:T(8,128)} %fusion.7), channel_id=1, source_target_pairs={{0,2},{1,3},{2,0},{3,1},{4,6},{5,7},{6,4},{7,5},{8,10},{9,11},{10,... | collective-permute-start | bytes 786440 | tf_op jit(solution)/shard_map/ppermute | solution.py:449
  175.5 7.1 %copy-start.3 = (f32[1,2,2,2,128,128]{5,4,3,2,1,0:T(8,128)S(1)}, f32[1,2,2,2,128,128]{5,4,3,2,1,0:T(8,128)}, u32[]{:S(2)}) copy-start(f32[1,2,2,2,128,128]{5,4,3,2,1,0:T(8,128)} %get-tuple-element.61) | copy-start | bytes 1572868
  179.3 8.5 %collective-permute-start.9 = (f32[1,1,2,2,128,128]{4,5,2,3,1,0:T(8,128)S(1)}, f32[1,1,2,2,128,128]{4,5,2,3,1,0:T(8,128)S(1)}, u32[]{:S(2)}, u32[]{:S(2)}) collective-permute-start(f32[1,1,2,2,128,128]{4,5,2,3,1,0:T(8,128)S(1)} %slice_add_fusion.2), channel_id=1, source_target_pairs={{0,16},{8,24},{16,0},{24,8},{1,17},{9,25},{17,1},{25,9},{2,18},{10... | collective-permute-start | bytes 786440 | tf_op jit(solution)/shard_map/ppermute | solution.py:449
  180.7 10.8 %collective-permute-start.7 = (f32[1,2,2,128,128]{3,4,1,2,0:T(8,128)S(1)}, f32[1,2,2,128,128]{3,4,1,2,0:T(8,128)S(1)}, u32[]{:S(2)}, u32[]{:S(2)}) collective-permute-start(f32[1,2,2,128,128]{3,4,1,2,0:T(8,128)S(1)} %fusion.12), channel_id=1, source_target_pairs={{0,2},{1,3},{2,0},{3,1},{4,6},{5,7},{6,4},{7,5},{8,10},{9,11},{10,... | collective-permute-start | bytes 786440 | tf_op jit(solution)/shard_map/ppermute | solution.py:449
  182.8 21.1 %copy-start.5 = (f32[128,128,1]{1,0,2:T(8,128)S(1)}, f32[128,128,1]{1,0,2:T(8,128)}, u32[]{:S(2)}) copy-start(f32[128,128,1]{1,0,2:T(8,128)} %constant.93) | copy-start | bytes 196612
  182.8 21.7 %copy-start.6 = (f32[128,128,1]{1,0,2:T(8,128)S(1)}, f32[128,128,1]{1,0,2:T(8,128)}, u32[]{:S(2)}) copy-start(f32[128,128,1]{1,0,2:T(8,128)} %constant.92) | copy-start | bytes 196612
  184.1 7.4 %collective-permute-start.4 = (f32[1,1,2,2,128,128]{4,5,2,3,1,0:T(8,128)S(1)}, f32[1,1,2,2,128,128]{4,5,2,3,1,0:T(8,128)S(1)}, u32[]{:S(2)}, u32[]{:S(2)}) collective-permute-start(f32[1,1,2,2,128,128]{4,5,2,3,1,0:T(8,128)S(1)} %slice_add_fusion.6), channel_id=1, source_target_pairs={{0,8},{8,0},{16,24},{24,16},{1,9},{9,1},{17,25},{25,17},{2,10},{10... | collective-permute-start | bytes 786440 | tf_op jit(solution)/shard_map/ppermute | solution.py:449
  188.8 14.1 %collective-permute-start.13 = (f32[1,2,2,128,128]{3,4,1,2,0:T(8,128)S(1)}, f32[1,2,2,128,128]{3,4,1,2,0:T(8,128)S(1)}, u32[]{:S(2)}, u32[]{:S(2)}) collective-permute-start(f32[1,2,2,128,128]{3,4,1,2,0:T(8,128)S(1)} %fusion.10), channel_id=1, source_target_pairs={{0,4},{1,5},{2,6},{3,7},{4,0},{5,1},{6,2},{7,3},{8,12},{9,13},{10,... | collective-permute-start | bytes 786440 | tf_op jit(solution)/shard_map/ppermute | solution.py:449
where the time goes:
time: 217 us; the launch traced here: 215 us
  Pallas kernels  112 us (52%)
  local copies, waits for them, and re-layouts  34.8 us (16%)
  waiting for transfers between devices  20.8 us (10%)
  other arithmetic  18.5 us (9%)
  starting transfers between devices  17.2 us (8%)
  blocking collectives  7.59 us (3%)
  matrix products  2.66 us (1%)
    pallas_call x2, Pallas kernels, column_inverse(): pl.pallas_call(functools.partial(column_inverse_kernel, layout), out_shap...  48.9 us
    pallas_call x2, Pallas kernels, row_inverse(): pl.pallas_call(functools.partial(row_inverse_kernel, steps), out_shape=(o...  27.9 us
    ppermute x14, waiting for transfers between devices, flip(): return lax.ppermute(block, axis, [(i, i ^ bit) for i in range(count)])  20.8 us
    unnamed x36, local copies, waits for them, and re-layouts  20.1 us
    ppermute x14, starting transfers between devices, flip(): return lax.ppermute(block, axis, [(i, i ^ bit) for i in range(count)])  17.2 us
    pallas_call x1, Pallas kernels, row_forward(): pl.pallas_call(row_forward_kernel, out_shape=(out, out), grid_spec=pltpu....  14.7 us
    pallas_call x2, Pallas kernels, column_forward(): pl.pallas_call(column_forward_kernel, out_shape=jax.ShapeDtypeStruct((2,...  12.6 us
    pallas_call x1, Pallas kernels, split_columns(): pl.pallas_call(split_kernel, out_shape=(out, out), grid_spec=pltpu.Prefet...  7.76 us
  transfers between devices with their start and end apart: 14, of which 7 were waited for; matrix products, arithmetic and copies ran while one was open for 17% of the time, Pallas kernels for 9%

commit v1 on v0

--- a/solution.py
+++ b/solution.py
@@ -317,7 +317,8 @@
     layout, info_ref, slot_ref, pos_ref, re_ref, im_ref, sign_ref,
     rows_hi, rows_lo, fine_ref, coarse_ref, keep_ref, send_ref, field, table_hi, table_lo,
 ):
-    chip_rows, chips, waves, own = layout
+    chip_rows, waves, own, segments = layout
+    height = chip_rows + WINDOW
     step = pl.program_id(0)
     tile = step % COL_TILES
     tables = (table_hi, table_lo)
@@ -337,30 +338,28 @@
                     start = block * PAIR + kind * LANES
                     put(tables, (tile, slice(start, start + LANES), cols), value[kind])
 
-    @pl.when(step < 2 * COL_TILES)
+    @pl.when(step < 2 * segments * COL_TILES)
     def _():
-        part = step // COL_TILES
+        part = step // COL_TILES % 2
+        start = pl.multiple_of(step // (2 * COL_TILES) * height, LANES)
+        rows = pl.ds(start, height)
         value = dot3((rows_hi[0], rows_lo[0]), (table_hi[tile], table_lo[tile]))
-        field[part, 2 * tile] = value[:, :LANES]
-        field[part, 2 * tile + 1] = value[:, LANES:]
+        field[part, 2 * tile, rows] = value[:, :LANES]
+        field[part, 2 * tile + 1, rows] = value[:, LANES:]
 
         @pl.when(tile == 0)
         def _():
-            field[part, 2 * COL_TILES] = value[:, :LANES] * sign_ref[0]
-
-    @pl.when(step == 2 * COL_TILES)
+            field[part, 2 * COL_TILES, rows] = value[:, :LANES] * sign_ref[0]
+
+    @pl.when(step == 2 * segments * COL_TILES)
     def _():
         lane = lax.broadcasted_iota(jnp.int32, (WINDOW, WINDOW), 1)
         row_rank, wave_rank = info_ref[0], info_ref[1]
-        far = chips // 2
-        segments = far // 2
 
         def one(index, out_ref, place):
             target = row_rank ^ slot_ref[0, index]
             probe = (target * waves + (wave_rank ^ slot_ref[1, index])) * own + slot_ref[2, index]
-            away = lax.rem(target // 2 - row_rank // 2 + chips, chips)
-            segment = away // far * segments + lax.rem(away, far) // 2
-            row = segment * (chip_rows + WINDOW) + lax.rem(pos_ref[0, probe], chip_rows)
+            row = slot_ref[3, index] * height + lax.rem(pos_ref[0, probe], chip_rows)
             start = lax.rem(pos_ref[1, probe] + (GRID - HALF), GRID)
             col = lax.rem(start, FOLD)
             turned = jnp.where(start >= FOLD, sign_ref[0], 1.0)
@@ -383,23 +382,27 @@
 
         @pl.loop(0, count)
         def _(place):
+            one(count + place, send_ref, place)
             one(place, keep_ref, place)
-            one(count + place, send_ref, place)
 
 
 def column_inverse(layout, rows, slots, info, positions, weights, sign):
+    chip_rows, _, _, segments = layout
     count = slots.shape[1] // 2
-    height = rows[0].shape[1]
+    height = chip_rows + WINDOW
     fine = both(lambda freq: cos_sin(freq, np.arange(LANES)))
     coarse = both(
         lambda freq: np.stack(
             [cos_sin(freq, PAIR * tile + np.array([0, LANES])) for tile in range(COL_TILES)]
         )
     )
-    last = 2 * COL_TILES - 1
-    rows_spec = pl.BlockSpec(
-        (1, height, DEPTH), lambda i, *_: (jnp.minimum(i, last) // COL_TILES, 0, 0)
-    )
+    last = 2 * segments * COL_TILES - 1
+
+    def rows_map(i, info, *_):
+        i = jnp.minimum(i, last)
+        return i // COL_TILES % 2, info[3 + i // (2 * COL_TILES)], 0
+
+    rows_spec = pl.BlockSpec((1, height, DEPTH), rows_map)
     out = jax.ShapeDtypeStruct((count, 2, WINDOW, WINDOW), jnp.float32)
     out_spec = pl.BlockSpec(
         (count, 2, WINDOW, WINDOW), lambda i, *_: (0, 0, 0, 0), pipeline_mode=pl.Buffered(1)
@@ -409,7 +412,7 @@
         out_shape=(out, out),
         grid_spec=pltpu.PrefetchScalarGridSpec(
             num_scalar_prefetch=6,
-            grid=(2 * COL_TILES + 1,),
+            grid=(last + 2,),
             in_specs=[
                 rows_spec,
                 rows_spec,
@@ -421,14 +424,14 @@
             ],
             out_specs=(out_spec, out_spec),
             scratch_shapes=[
-                pltpu.VMEM((2, 2 * COL_TILES + 1, height, WINDOW), jnp.float32),
+                pltpu.VMEM((2, 2 * COL_TILES + 1, segments * height, WINDOW), jnp.float32),
                 pltpu.VMEM((COL_TILES, DEPTH, PAIR), jnp.bfloat16),
                 pltpu.VMEM((COL_TILES, DEPTH, PAIR), jnp.bfloat16),
             ],
         ),
         cost_estimate=pl.CostEstimate(
-            flops=12 * height * DEPTH * FOLD,
-            bytes_accessed=8 * height * DEPTH + 16 * count * WINDOW * WINDOW,
+            flops=12 * segments * height * DEPTH * FOLD,
+            bytes_accessed=8 * segments * height * DEPTH + 16 * count * WINDOW * WINDOW,
             transcendentals=0,
         ),
         name="column_inverse",
@@ -438,6 +441,75 @@
     )
 
 
+def sum_kernel(count, *refs):
+    total = refs[0][...]
+    for ref in refs[1:count]:
+        total += ref[...]
+    if len(refs) == count + 1:
+        refs[count][...] = total
+    else:
+        refs[count][...] = total[0]
+        refs[count + 1][...] = total[1]
+
+
+def sum_of(terms, halve):
+    count, tail = terms[0].shape[0], terms[0].shape[1:]
+    zeros = (0,) * len(tail)
+    if halve:
+        count //= 2
+        terms = [term.reshape((2, count) + tail) for term in terms]
+        step = max(1, count // 2)
+        in_spec = pl.BlockSpec((2, step) + tail, lambda i: (0, i) + zeros)
+    else:
+        step = max(1, count // 2)
+        in_spec = pl.BlockSpec((step,) + tail, lambda i: (i,) + zeros)
+    out = jax.ShapeDtypeStruct((count,) + tail, jnp.float32)
+    out_spec = pl.BlockSpec((step,) + tail, lambda i: (i,) + zeros)
+    size = count * 4 * math.prod(tail) * (2 if halve else 1)
+    result = pl.pallas_call(
+        functools.partial(sum_kernel, len(terms)),
+        out_shape=(out, out) if halve else out,
+        grid=(count // step,),
+        in_specs=[in_spec] * len(terms),
+        out_specs=(out_spec, out_spec) if halve else out_spec,
+        cost_estimate=pl.CostEstimate(
+            flops=size, bytes_accessed=(len(terms) + 1) * size, transcendentals=0
+        ),
+        name="sum_of",
+    )(*terms)
+    return result
+
+
+def power_kernel(count, scale, *refs):
+    terms, (down_ref, along_ref, out_ref) = refs[:count], refs[count:]
+    down, along = halves_of(down_ref[...]), halves_of(along_ref[...])
+    for probe in range(out_ref.shape[0]):
+        total = terms[0][probe]
+        for term in terms[1:]:
+            total += term[probe]
+        value = dot3(down, halves_of(jnp.concatenate([total[0], total[1]], axis=1)))
+        cos_part, sin_part = value[:WINDOW], value[WINDOW:]
+        real_part = cos_part[:, :WINDOW] + sin_part[:, WINDOW:]
+        imag_part = cos_part[:, WINDOW:] - sin_part[:, :WINDOW]
+        value = dot3(halves_of(jnp.concatenate([real_part, imag_part])), along)
+        real_part = value[:WINDOW, :WINDOW] + value[WINDOW:, WINDOW:]
+        imag_part = value[WINDOW:, :WINDOW] - value[:WINDOW, WINDOW:]
+        out_ref[probe] = (real_part * real_part + imag_part * imag_part) * scale
+
+
+def power_of(terms, scale):
+    count = terms[0].shape[0]
+    table = cos_sin(np.arange(WINDOW), FACTOR * np.arange(WINDOW))
+    return pl.pallas_call(
+        functools.partial(power_kernel, len(terms), scale),
+        out_shape=jax.ShapeDtypeStruct((count, WINDOW, WINDOW), jnp.float32),
+        name="power_of",
+    )(
+        *terms, jnp.asarray(np.concatenate(list(table))),
+        jnp.asarray(np.concatenate(list(table), axis=1)),
+    )
+
+
 def coefficients(positions, wave_index, wave_weight, wave_phase):
     turns = (FACTOR * (positions[0] * wave_index[0, 0] + positions[1] * wave_index[0, 1])) % GRID
     angles = wave_phase[0] - turns.astype(jnp.float32) * (2.0 * math.pi / GRID)
@@ -447,10 +519,6 @@
 def flip(block, axis, bit):
     count = lax.axis_size(axis)
     return lax.ppermute(block, axis, [(i, i ^ bit) for i in range(count)])
-
-
-def exchange(parts, axis, bit):
-    return parts[0] + flip(parts[1], axis, bit)
 
 
 def shards(plane_waves, transmission, wave_index, wave_weight, wave_phase, probe_pos):
@@ -462,7 +530,6 @@
     core = row_rank % 2
     sign = (1.0 - 2.0 * core.astype(jnp.float32))[None]
     parity = core[None]
-    info = jnp.stack([row_rank, wave_rank, core])
     chip_rows = 2 * rows_here
     chips = row_count // 2
     far = chips // 2
@@ -478,20 +545,29 @@
 
     wave_bits = wave_count.bit_length() - 1
     orders = (list(range(wave_bits - 1, -1, -1)), list(range(wave_bits)))
-    order_of = [orders[0 if index < far // 2 else 1] for index in range(far)]
-    layout = (chip_rows, chips, wave_count, own)
-
-    def slots_of(odd):
+    segments = far // 2
+    layout = (chip_rows, wave_count, own, segments)
+
+    def slots_of(odd, half):
         slots = []
         for core_bit in (0, 1):
-            for index in range(far):
-                for digits in range(wave_count):
-                    wave = 0
-                    for place, bit in enumerate(order_of[index]):
-                        wave |= (digits >> (wave_bits - 1 - place) & 1) << bit
-                    for probe in range(own):
-                        slots.append(((index * 2 + odd) * 2 + core_bit, wave, probe))
+            for digits in range(wave_count):
+                wave = 0
+                for place, bit in enumerate(orders[half]):
+                    wave |= (digits >> (wave_bits - 1 - place) & 1) << bit
+                for index in range(segments):
+                    row = ((half * segments + index) * 2 + odd) * 2 + core_bit
+                    slots += [(row, wave, probe, index) for probe in range(own)]
         return np.array(slots, np.int32).T
+
+    def info_of(odd, half):
+        chip = row_rank // 2
+        info = [row_rank, wave_rank, core]
+        for index in range(segments):
+            target = chip ^ ((half * segments + index) * 2 + odd)
+            away = (target - chip) % chips
+            info.append(away // far * segments + away % far // 2)
+        return jnp.stack(info)
 
     def steps_of(odd):
         steps = []
@@ -500,76 +576,75 @@
             steps += range(first, first + (chip_rows + WINDOW) // FINE)
         return tuple(steps)
 
-    def by_half(parts):
-        return [
-            parts[half * (far // 2) : (half + 1) * (far // 2)].reshape(
-                (far // 2, wave_count, own, 2, WINDOW, WINDOW)
-            )
-            for half in (0, 1)
-        ]
-
-    def column_part(odd, rows):
-        keep, send = column_inverse(layout, rows, slots_of(odd), info, positions, weights, sign)
+    def cut(odd, half, rows):
+        keep, send = column_inverse(
+            layout, rows, slots_of(odd, half), info_of(odd, half), positions, weights, sign
+        )
         return keep, flip(send, "row", 1)
 
-    def add_core(keep, arrived):
-        shape = (far, wave_count, own, 2, WINDOW, WINDOW)
-        keep, arrived = by_half(keep.reshape(shape)), by_half(arrived.reshape(shape))
-        middle = wave_count // 2
-        return [
-            (a[:, :middle] + b[:, :middle], a[:, middle:] + b[:, middle:])
-            for a, b in zip(keep, arrived)
-        ]
-
-    def over_waves(halves):
-        sums = []
-        for (stay, send), order in zip(halves, orders):
-            for place, bit in enumerate(order):
-                arrived = flip(send, "wave", 1 << bit)
-                middle = stay.shape[1] // 2
-                if place + 1 < wave_bits:
-                    stay, send = (
-                        stay[:, :middle] + arrived[:, :middle],
-                        stay[:, middle:] + arrived[:, middle:],
-                    )
-                else:
-                    stay = stay + arrived
-            sums.append(stay[:, 0])
-        return sums
-
+    def wave_stage(half, place, terms):
+        stay, send = sum_of(terms, True)
+        return stay, flip(send, "wave", 1 << orders[half][place])
+
+    def later(value, *before):
+        return lax.optimization_barrier((value,) + before)
+
+    upper, lower = 1, 0
     rows_odd = row_inverse(spectrum, steps_of(1))
-    keep_odd, arrived_odd = column_part(1, rows_odd)
-    spectrum, keep_odd = lax.optimization_barrier((spectrum, keep_odd))
+    odd_upper = cut(1, upper, rows_odd)
+    rows_odd, keep = later(rows_odd, odd_upper[0])
+    odd_upper = (keep, odd_upper[1])
+    odd_lower = cut(1, lower, rows_odd)
+
+    stages = {(1, upper): [odd_upper, 0], (1, lower): [odd_lower, 0]}
+
+    def advance(value, *keys):
+        for key in keys:
+            terms, place = stages[key]
+            if place == wave_bits:
+                continue
+            stay, send = sum_of(terms, True)
+            value, stay, send = later(value, stay, send)
+            stages[key] = [
+                (stay, flip(send, "wave", 1 << orders[key[1]][place])), place + 1
+            ]
+        return value
+
+    spectrum = later(spectrum, odd_lower[0])
+    spectrum, keep = spectrum
+    stages[1, lower] = [(keep, odd_lower[1]), 0]
+    spectrum = advance(spectrum, (1, upper))
     rows_even = row_inverse(spectrum, steps_of(0))
-    halves_odd = add_core(keep_odd, arrived_odd)
-    rows_even, halves_odd = lax.optimization_barrier((rows_even, halves_odd))
-    sums_odd = over_waves(halves_odd)
-    sums_even = over_waves(add_core(*column_part(0, rows_even)))
-    parts = [even + flip(odd, "row", 2) for even, odd in zip(sums_even, sums_odd)]
+    rows_even = advance(rows_even, (1, upper), (1, lower))
+    even_upper = cut(0, upper, rows_even)
+    rows_even, keep = later(rows_even, even_upper[0])
+    stages[0, upper] = [(keep, even_upper[1]), 0]
+    rows_even = advance(rows_even, (1, lower))
+    near_upper = None
+    if stages[1, upper][1] == wave_bits:
+        total = sum_of(stages[1, upper][0], False)
+        rows_even, total = later(rows_even, total)
+        near_upper = flip(total, "row", 2)
+    stages[0, lower] = [cut(0, lower, rows_even), 0]
+
+    def finish(key):
+        while stages[key][1] < wave_bits:
+            terms, place = stages[key]
+            stages[key] = [wave_stage(key[1], place, terms), place + 1]
+        return list(stages[key][0])
+
+    if near_upper is None:
+        near_upper = flip(sum_of(finish((1, upper)), False), "row", 2)
+    near_lower = flip(sum_of(finish((1, lower)), False), "row", 2)
     bit = row_count // 2
-    parts = exchange(parts, "row", bit)
+    send = sum_of(finish((0, upper)) + [near_upper], False)
+    terms = finish((0, lower)) + [near_lower, flip(send, "row", bit)]
     while bit > 4:
         bit //= 2
-        parts = exchange(parts.reshape((2, -1) + parts.shape[1:]), "row", bit)
-    window = parts[0]
-
-    angle = angles_of(np.arange(WINDOW), FACTOR * np.arange(WINDOW))
-    cos_t = jnp.asarray(np.cos(angle).astype(np.float32))
-    sin_t = jnp.asarray(np.sin(angle).astype(np.float32))
-
-    def one_dft(formula, halves):
-        def term(table, value):
-            return jnp.einsum(formula, table, value, precision=lax.Precision.HIGHEST)
-
-        return (
-            term(cos_t, halves[0]) + term(sin_t, halves[1]),
-            term(cos_t, halves[1]) - term(sin_t, halves[0]),
-        )
-
-    halves = one_dft("ki,pij->pkj", (window[:, 0], window[:, 1]))
-    halves = one_dft("kj,pij->pik", halves)
+        stay, send = sum_of(terms, True)
+        terms = [stay, flip(send, "row", bit)]
     total_waves = plane_waves.shape[1] * wave_count
-    power = (halves[0] * halves[0] + halves[1] * halves[1]) / (WINDOW * WINDOW * total_waves)
+    power = power_of(terms, 1.0 / (WINDOW * WINDOW * total_waves))
     return lax.all_to_all(power, "wave", split_axis=1, concat_axis=0, tiled=True)
 
 

time: 217 us -> 209 us (0.963)
  Pallas kernels: 112 us -> 150 us
  local copies, waits for them, and re-layouts: 34.8 us -> 12.2 us
  other arithmetic: 18.5 us -> 3.79 us
  waiting for transfers between devices: 20.8 us -> 15.4 us
  matrix products: 2.66 us -> 0 us
    pallas_call x0 -> x12, Pallas kernels: none -> 25.3 us  [the longest x11 22.5 us: sum_of(): pl.pallas_call(functools.partial(sum_kernel, len(terms)), out_shape=(out,...]
    slice x12 -> x0, local copies, waits for them, and re-layouts: 13.3 us -> none  [the longest x4 6.74 us: by_half(): parts[half * (far // 2):(half + 1) * (far // 2)]]
    pallas_call x2 -> x4, Pallas kernels: 48.9 us -> 61.2 us  [column_inverse(): pl.pallas_call(functools.partial(column_inverse_kernel, layout), out_shap...]
    add x13 -> x0, other arithmetic: 11.7 us -> none  [the longest x4 5.76 us: add_core(): a[:, middle:] + b[:, middle:]]
    unnamed x36 -> x40, local copies, waits for them, and re-layouts: 20.1 us -> 9.95 us
    ppermute x14 -> x16, waiting for transfers between devices: 20.8 us -> 15.4 us  [flip(): return lax.ppermute(block, axis, [(i, i ^ bit) for i in range(count)])]
    squeeze x3 -> x0, other arithmetic: 3.87 us -> none  [the longest x2 2.84 us: over_waves(): sums.append(stay[:, 0])]
    dot_general x8 -> x0, matrix products: 2.66 us -> none  [term(): return jnp.einsum(formula, table, value, precision=lax.Precision.HIGHEST)]
  transfers between devices with their start and end apart: 14 -> 16, of which waited for: 7 -> 5; matrix products, arithmetic and copies ran while one was open for 17% -> 2% of each run, Pallas kernels for 9% -> 42%
where the time goes in v1:
time: 209 us; the launch traced here: 207 us
  Pallas kernels  150 us (72%)
  starting transfers between devices  17.3 us (8%)
  waiting for transfers between devices  15.4 us (7%)
  local copies, waits for them, and re-layouts  12.2 us (6%)
  blocking collectives  7.59 us (4%)
  other arithmetic  3.79 us (2%)
    pallas_call x4, Pallas kernels, column_inverse(): pl.pallas_call(functools.partial(column_inverse_kernel, layout), out_shap...  61.2 us
    pallas_call x2, Pallas kernels, row_inverse(): pl.pallas_call(functools.partial(row_inverse_kernel, steps), out_shape=(o...  28 us
    pallas_call x11, Pallas kernels, sum_of(): pl.pallas_call(functools.partial(sum_kernel, len(terms)), out_shape=(out,...  22.5 us
    ppermute x16, starting transfers between devices, flip(): return lax.ppermute(block, axis, [(i, i ^ bit) for i in range(count)])  17.3 us
    ppermute x16, waiting for transfers between devices, flip(): return lax.ppermute(block, axis, [(i, i ^ bit) for i in range(count)])  15.4 us
    pallas_call x1, Pallas kernels, row_forward(): pl.pallas_call(row_forward_kernel, out_shape=(out, out), grid_spec=pltpu....  14.7 us
    pallas_call x2, Pallas kernels, column_forward(): pl.pallas_call(column_forward_kernel, out_shape=jax.ShapeDtypeStruct((2,...  12.6 us
    unnamed x40, local copies, waits for them, and re-layouts  9.95 us
  transfers between devices with their start and end apart: 16, of which 5 were waited for; matrix products, arithmetic and copies ran while one was open for 2% of the time, Pallas kernels for 42%

profile of v1, /device:TPU:0, one launch (start us, length us, event | category | flops | bytes accessed | tf_op | source)
XLA Modules:
  0.0 207.3 jit_solution(7900496367108340747)
XLA Ops:
  0.0 7.8 %split_columns.1 = (f32[2,256,1024]{2,1,0:T(8,128)}, f32[2,256,1024]{2,1,0:T(8,128)}) custom-call(f32[1]{0:T(128)} %bitcast.9.sign_ref, f32[2,1,256,2048]{3,2,1,0:T(8,128)} %wave_ref.1, f32[1,2,256,2048]{3,2,1,0:T(8,128)} %trans_ref.1), custom_call_target="tpu_custom_call" | custom-call | flops 10485760 | bytes 12582912 | tf_op jit(solution)/shard_map/split_columns/pallas_call | solution.py:88
  10.9 1.9 sine_multiply_fusion
  14.0 6.3 %column_forward.2.mine_ref = f32[2,256,768]{2,1,0:T(8,128)} custom-call(s32[1]{0:T(128)} %bitcast.2.parity_ref, f32[2,256,1024]{2,1,0:T(8,128)} %get-tuple-element.67.field_ref, f32[2,2,64,384]{3,2,1,0:T(8,128)} %constant.234.clone.fine_ref, f32[2,2,16,384]{3,2,1,0:T(8,128)} %constant.235.clone.coarse_ref), custom_call_target="tpu_custom_call" | custom-call | flops 2415919104 | bytes 3670016 | tf_op jit(solution)/shard_map/column_forward/pallas_call | solution.py:133
  20.4 6.3 %column_forward.3.theirs_ref = f32[2,256,768]{2,1,0:T(8,128)} custom-call(s32[1]{0:T(128)} %bitcast.2.parity_ref, f32[2,256,1024]{2,1,0:T(8,128)} %collective-permute-done.field_ref, f32[2,2,64,384]{3,2,1,0:T(8,128)} %constant.234.clone.fine_ref, f32[2,2,16,384]{3,2,1,0:T(8,128)} %constant.235.clone.coarse_ref), custom_call_target="tpu_custom_call" | custom-call | flops 2415919104 | bytes 3670016 | tf_op jit(solution)/shard_map/column_forward/pallas_call | solution.py:133
  26.7 14.7 %row_forward.1 = (bf16[2,1536,768]{2,1,0:T(8,128)(2,1)}, bf16[2,1536,768]{2,1,0:T(8,128)(2,1)}) custom-call(s32[1]{0:T(128)} %bitcast.2.parity_ref, f32[2,256,768]{2,1,0:T(8,128)} %column_forward.2.mine_ref, f32[2,256,768]{2,1,0:T(8,128)} %column_forward.3.theirs_ref, f32[2,768,128]{2,1,0:T(8,128)} %constant.236.clone.fine_ref, ...), custom_call_target="tpu_custom_call" | custom-call | flops 7247757312 | bytes 12582912 | tf_op jit(solution)/shard_map/row_forward/pallas_call | solution.py:226
  41.3 14.0 %row_inverse.2 = (bf16[2,1280,768]{2,1,0:T(8,128)(2,1)}, bf16[2,1280,768]{2,1,0:T(8,128)(2,1)}) custom-call(bf16[2,1536,768]{2,1,0:T(8,128)(2,1)} %get-tuple-element.85.spec_hi, bf16[2,1536,768]{2,1,0:T(8,128)(2,1)} %get-tuple-element.86.spec_lo, f32[2,64,768]{2,1,0:T(8,128)} %constant.240.clone.fine_ref, f32[2,18,768]{2,1,0:T(8,128)} %constant.241.clone.coarse_ref), custom_call_target="tpu_custom_call" | custom-call | flops 9059696640 | bytes 17301504 | tf_op jit(solution)/shard_map/row_inverse/pallas_call | solution.py:295
  55.3 15.5 %column_inverse.4 = (f32[8,2,128,128]{3,2,1,0:T(8,128)}, f32[8,2,128,128]{3,2,1,0:T(8,128)}) custom-call(s32[4]{0:T(128)} %get-tuple-element.133.info_ref, s32[4,16]{1,0:T(4,128)} %constant.242.clone.slot_ref, s32[2,64]{1,0:T(2,128)} %bitcast.55, f32[64]{0:T(128)} %cosine_multiply_fusion.re_ref, f32[64]{0:T(128)} %get-tuple-element.131.im_ref, ...), custom_call_target="tpu_custom_call" | custom-call | flops 6039797760 | bytes 6029312 | tf_op jit(solution)/shard_map/column_inverse/pallas_call | solution.py:410
  70.8 15.2 %column_inverse.5 = (f32[8,2,128,128]{3,2,1,0:T(8,128)}, f32[8,2,128,128]{3,2,1,0:T(8,128)}) custom-call(s32[4]{0:T(128)} %get-tuple-element.134.info_ref, s32[4,16]{1,0:T(4,128)} %constant.245.clone.slot_ref, s32[2,64]{1,0:T(2,128)} %bitcast.56, f32[64]{0:T(128)} %cosine_multiply_fusion.re_ref, f32[64]{0:T(128)} %get-tuple-element.131.im_ref, ...), custom_call_target="tpu_custom_call" | custom-call | flops 6039797760 | bytes 6029312 | tf_op jit(solution)/shard_map/column_inverse/pallas_call | solution.py:410
  87.5 2.4 %sum_of.11 = (f32[4,2,128,128]{3,2,1,0:T(8,128)}, f32[4,2,128,128]{3,2,1,0:T(8,128)}) custom-call(f32[2,4,2,128,128]{4,3,2,1,0:T(8,128)} %bitcast.42, f32[2,4,2,128,128]{4,3,2,1,0:T(8,128)} %bitcast.45), custom_call_target="tpu_custom_call" | custom-call | flops 1048576 | bytes 3145728 | tf_op jit(solution)/shard_map/sum_of/pallas_call | solution.py:469
  89.9 2.5 %collective-permute-start.2 = (f32[4,2,128,128]{3,2,1,0:T(8,128)}, f32[4,2,128,128]{3,2,1,0:T(8,128)S(1)}, u32[]{:S(2)}, u32[]{:S(2)}) collective-permute-start(f32[4,2,128,128]{3,2,1,0:T(8,128)} %get-tuple-element.90), channel_id=1, source_target_pairs={{0,8},{8,0},{16,24},{24,16},{1,9},{9,1},{17,25},{25,17},{2,10},{10... | collective-permute-start | bytes 1572872 | tf_op jit(solution)/shard_map/ppermute | solution.py:521
  93.3 2.4 %sum_of.13 = (f32[4,2,128,128]{3,2,1,0:T(8,128)}, f32[4,2,128,128]{3,2,1,0:T(8,128)}) custom-call(f32[2,4,2,128,128]{4,3,2,1,0:T(8,128)} %bitcast.41, f32[2,4,2,128,128]{4,3,2,1,0:T(8,128)} %bitcast.43), custom_call_target="tpu_custom_call" | custom-call | flops 1048576 | bytes 3145728 | tf_op jit(solution)/shard_map/sum_of/pallas_call | solution.py:469
  95.7 14.0 %row_inverse.3 = (bf16[2,1280,768]{2,1,0:T(8,128)(2,1)}, bf16[2,1280,768]{2,1,0:T(8,128)(2,1)}) custom-call(bf16[2,1536,768]{2,1,0:T(8,128)(2,1)} %get-tuple-element.85.spec_hi, bf16[2,1536,768]{2,1,0:T(8,128)(2,1)} %get-tuple-element.86.spec_lo, f32[2,64,768]{2,1,0:T(8,128)} %constant.240.clone.fine_ref, f32[2,18,768]{2,1,0:T(8,128)} %constant.241.clone.coarse_ref), custom_call_target="tpu_custom_call" | custom-call | flops 9059696640 | bytes 17301504 | tf_op jit(solution)/shard_map/row_inverse/pallas_call | solution.py:295
  110.5 1.9 sum_of.12
  112.5 1.5 collective-permute-start.5
  114.5 15.3 %column_inverse.6 = (f32[8,2,128,128]{3,2,1,0:T(8,128)}, f32[8,2,128,128]{3,2,1,0:T(8,128)}) custom-call(s32[4]{0:T(128)} %get-tuple-element.129.info_ref, s32[4,16]{1,0:T(4,128)} %constant.246.clone.slot_ref, s32[2,64]{1,0:T(2,128)} %bitcast.57, f32[64]{0:T(128)} %cosine_multiply_fusion.re_ref, f32[64]{0:T(128)} %get-tuple-element.131.im_ref, ...), custom_call_target="tpu_custom_call" | custom-call | flops 6039797760 | bytes 6029312 | tf_op jit(solution)/shard_map/column_inverse/pallas_call | solution.py:410
  130.4 1.8 sum_of.15
  133.1 1.9 sum_of.14
  135.0 15.3 %column_inverse.7 = (f32[8,2,128,128]{3,2,1,0:T(8,128)}, f32[8,2,128,128]{3,2,1,0:T(8,128)}) custom-call(s32[4]{0:T(128)} %get-tuple-element.135.info_ref, s32[4,16]{1,0:T(4,128)} %constant.247.clone.slot_ref, s32[2,64]{1,0:T(2,128)} %bitcast.58, f32[64]{0:T(128)} %cosine_multiply_fusion.re_ref, f32[64]{0:T(128)} %get-tuple-element.131.im_ref, ...), custom_call_target="tpu_custom_call" | custom-call | flops 6039797760 | bytes 6029312 | tf_op jit(solution)/shard_map/column_inverse/pallas_call | solution.py:410
  151.7 2.4 %sum_of.19 = (f32[4,2,128,128]{3,2,1,0:T(8,128)}, f32[4,2,128,128]{3,2,1,0:T(8,128)}) custom-call(f32[2,4,2,128,128]{4,3,2,1,0:T(8,128)} %bitcast.38, f32[2,4,2,128,128]{4,3,2,1,0:T(8,128)} %bitcast.39), custom_call_target="tpu_custom_call" | custom-call | flops 1048576 | bytes 3145728 | tf_op jit(solution)/shard_map/sum_of/pallas_call | solution.py:469
  155.2 2.4 %sum_of.16 = (f32[4,2,128,128]{3,2,1,0:T(8,128)}, f32[4,2,128,128]{3,2,1,0:T(8,128)}) custom-call(f32[2,4,2,128,128]{4,3,2,1,0:T(8,128)} %bitcast.40, f32[2,4,2,128,128]{4,3,2,1,0:T(8,128)} %bitcast.44), custom_call_target="tpu_custom_call" | custom-call | flops 1048576 | bytes 3145728 | tf_op jit(solution)/shard_map/sum_of/pallas_call | solution.py:469
  157.5 2.0 collective-permute-start.7
  159.5 1.6 collective-permute-start.14
  162.6 6.5 %collective-permute-done.12 = f32[4,2,128,128]{3,2,1,0:T(8,128)S(1)} collective-permute-done((f32[4,2,128,128]{3,2,1,0:T(8,128)}, f32[4,2,128,128]{3,2,1,0:T(8,128)S(1)}, u32[]{:S(2)}, u32[]{:S(2)}) %collective-permute-start.12) | collective-permute-done | bytes 524320 | tf_op jit(solution)/shard_map/ppermute | solution.py:521
  169.8 1.9 sum_of.20
  174.5 1.8 sum_of.18
  176.3 1.6 collective-permute-start.10
  179.3 1.9 sum_of.21
  181.2 2.6 %collective-permute-start.15 = (f32[2,2,128,128]{3,2,1,0:T(8,128)}, f32[2,2,128,128]{3,2,1,0:T(8,128)S(1)}, u32[]{:S(2)}, u32[]{:S(2)}) collective-permute-start(f32[2,2,128,128]{3,2,1,0:T(8,128)} %sum_of.21), channel_id=1, source_target_pairs={{0,4},{1,5},{2,6},{3,7},{4,0},{5,1},{6,2},{7,3},{8,12},{9,13},{10,... | collective-permute-start | bytes 786440 | tf_op jit(solution)/shard_map/ppermute | solution.py:521
  184.6 1.9 sum_of.17
  187.1 7.5 %collective-permute-done.15.refs_3_ = f32[2,2,128,128]{3,2,1,0:T(8,128)S(1)} collective-permute-done((f32[2,2,128,128]{3,2,1,0:T(8,128)}, f32[2,2,128,128]{3,2,1,0:T(8,128)S(1)}, u32[]{:S(2)}, u32[]{:S(2)}) %collective-permute-start.15) | collective-permute-done | bytes 262176 | tf_op jit(solution)/shard_map/ppermute | solution.py:521
  195.3 2.8 %power_of.1 = f32[2,128,128]{2,1,0:T(8,128)} custom-call(f32[2,2,128,128]{3,2,1,0:T(8,128)} %get-tuple-element.118.refs_0_, f32[2,2,128,128]{3,2,1,0:T(8,128)} %copy-done.15, f32[2,2,128,128]{3,2,1,0:T(8,128)} %copy-done.11, f32[2,2,128,128]{3,2,1,0:T(8,128)} %copy-done.13, f32[256,128]{1,0:T(8,128)} %constant.248.clone.refs_4_, ...), custom_call_target="tpu_custom_call" | custom-call | tf_op jit(solution)/shard_map/power_of/pallas_call | solution.py:503
  199.1 7.6 %all_to_all.18 = f32[2,128,128]{2,0,1:T(2,128)S(1)} all-to-all(f32[2,128,128]{2,0,1:T(2,128)S(1)} %copy.34), channel_id=1, replica_groups=mesh['wave'=4,'row'=8] {'wave'}, dimensions={1} | all-to-all | bytes 262144 | tf_op jit(solution)/shard_map/all_to_all | solution.py:648
  (70 shorter events, 21.1 us)
Async XLA Ops:
  0.0 10.3 %copy-start.16 = (s32[1,2]{1,0:T(1,128)S(1)}, s32[1,2]{1,0:T(1,128)}, u32[]{:S(2)}) copy-start(s32[1,2]{1,0:T(1,128)} %param.34) | copy-start | bytes 28
  0.0 10.9 %copy-start.17 = (s32[64,2]{0,1:T(2,128)S(1)}, s32[64,2]{0,1:T(2,128)}, u32[]{:S(2)}) copy-start(s32[64,2]{0,1:T(2,128)} %param.37) | copy-start | bytes 1540
  7.8 12.5 %collective-permute-start = (f32[2,256,1024]{2,1,0:T(8,128)}, f32[2,256,1024]{2,1,0:T(8,128)}, u32[]{:S(2)}, u32[]{:S(2)}) collective-permute-start(f32[2,256,1024]{2,1,0:T(8,128)} %get-tuple-element.68), channel_id=1, source_target_pairs={{0,1},{1,0},{2,3},{3,2},{4,5},{5,4},{6,7},{7,6},{8,9},{9,8},{10,11... | collective-permute-start | bytes 6291464 | tf_op jit(solution)/shard_map/ppermute | solution.py:521
  70.8 15.7 %collective-permute-start.1 = (f32[8,2,128,128]{3,2,1,0:T(8,128)}, f32[8,2,128,128]{3,2,1,0:T(8,128)S(1)}, u32[]{:S(2)}, u32[]{:S(2)}) collective-permute-start(f32[8,2,128,128]{3,2,1,0:T(8,128)} %get-tuple-element.82), channel_id=1, source_target_pairs={{0,1},{1,0},{2,3},{3,2},{4,5},{5,4},{6,7},{7,6},{8,9},{9,8},{10,11... | collective-permute-start | bytes 3145736 | tf_op jit(solution)/shard_map/ppermute | solution.py:521
  86.0 6.3 %collective-permute-start.3 = (f32[8,2,128,128]{3,2,1,0:T(8,128)}, f32[8,2,128,128]{3,2,1,0:T(8,128)S(1)}, u32[]{:S(2)}, u32[]{:S(2)}) collective-permute-start(f32[8,2,128,128]{3,2,1,0:T(8,128)} %get-tuple-element.96), channel_id=1, source_target_pairs={{0,1},{1,0},{2,3},{3,2},{4,5},{5,4},{6,7},{7,6},{8,9},{9,8},{10,11... | collective-permute-start | bytes 3145736 | tf_op jit(solution)/shard_map/ppermute | solution.py:521
  86.5 1.0 copy-start.3
  89.9 19.8 %collective-permute-start.2 = (f32[4,2,128,128]{3,2,1,0:T(8,128)}, f32[4,2,128,128]{3,2,1,0:T(8,128)S(1)}, u32[]{:S(2)}, u32[]{:S(2)}) collective-permute-start(f32[4,2,128,128]{3,2,1,0:T(8,128)} %get-tuple-element.90), channel_id=1, source_target_pairs={{0,8},{8,0},{16,24},{24,16},{1,9},{9,1},{17,25},{25,17},{2,10},{10... | collective-permute-start | bytes 1572872 | tf_op jit(solution)/shard_map/ppermute | solution.py:521
  92.4 1.0 copy-start.1
  95.7 18.3 %copy-start.18 = (f32[4,2,128,128]{3,2,1,0:T(8,128)S(1)}, f32[4,2,128,128]{3,2,1,0:T(8,128)}, u32[]{:S(2)}) copy-start(f32[4,2,128,128]{3,2,1,0:T(8,128)} %get-tuple-element.105) | copy-start | bytes 1572868
  109.7 0.8 copy-start.7
  112.5 17.3 %collective-permute-start.5 = (f32[2,2,128,128]{3,2,1,0:T(8,128)}, f32[2,2,128,128]{3,2,1,0:T(8,128)S(1)}, u32[]{:S(2)}, u32[]{:S(2)}) collective-permute-start(f32[2,2,128,128]{3,2,1,0:T(8,128)} %get-tuple-element.111), channel_id=1, source_target_pairs={{0,16},{8,24},{16,0},{24,8},{1,17},{9,25},{17,1},{25,9},{2,18},{10... | collective-permute-start | bytes 786440 | tf_op jit(solution)/shard_map/ppermute | solution.py:521
  114.0 18.3 %collective-permute-start.4 = (f32[4,2,128,128]{3,2,1,0:T(8,128)S(1)}, f32[4,2,128,128]{3,2,1,0:T(8,128)S(1)}, u32[]{:S(2)}, u32[]{:S(2)}) collective-permute-start(f32[4,2,128,128]{3,2,1,0:T(8,128)S(1)} %copy-done.18), channel_id=1, source_target_pairs={{0,16},{8,24},{16,0},{24,8},{1,17},{9,25},{17,1},{25,9},{2,18},{10... | collective-permute-start | bytes 1572872 | tf_op jit(solution)/shard_map/ppermute | solution.py:521
  129.7 21.0 %collective-permute-start.11 = (f32[8,2,128,128]{3,2,1,0:T(8,128)}, f32[8,2,128,128]{3,2,1,0:T(8,128)S(1)}, u32[]{:S(2)}, u32[]{:S(2)}) collective-permute-start(f32[8,2,128,128]{3,2,1,0:T(8,128)} %get-tuple-element.123), channel_id=1, source_target_pairs={{0,1},{1,0},{2,3},{3,2},{4,5},{5,4},{6,7},{7,6},{8,9},{9,8},{10,11... | collective-permute-start | bytes 3145736 | tf_op jit(solution)/shard_map/ppermute | solution.py:521
  132.3 0.8 copy-start.6
  150.3 9.2 %copy-start.8 = (f32[2,2,128,128]{3,2,1,0:T(8,128)S(1)}, f32[2,2,128,128]{3,2,1,0:T(8,128)}, u32[]{:S(2)}) copy-start(f32[2,2,128,128]{3,2,1,0:T(8,128)} %sum_of.15) | copy-start | bytes 786436
  150.3 10.8 %copy-start.19 = (f32[2,2,128,128]{3,2,1,0:T(8,128)S(1)}, f32[2,2,128,128]{3,2,1,0:T(8,128)}, u32[]{:S(2)}) copy-start(f32[2,2,128,128]{3,2,1,0:T(8,128)} %get-tuple-element.121) | copy-start | bytes 786436
  150.3 3.8 %collective-permute-start.6 = (f32[8,2,128,128]{3,2,1,0:T(8,128)}, f32[8,2,128,128]{3,2,1,0:T(8,128)S(1)}, u32[]{:S(2)}, u32[]{:S(2)}) collective-permute-start(f32[8,2,128,128]{3,2,1,0:T(8,128)} %get-tuple-element.115), channel_id=1, source_target_pairs={{0,1},{1,0},{2,3},{3,2},{4,5},{5,4},{6,7},{7,6},{8,9},{9,8},{10,11... | collective-permute-start | bytes 3145736 | tf_op jit(solution)/shard_map/ppermute | solution.py:521
  150.7 1.0 copy-start
  154.0 15.0 %collective-permute-start.12 = (f32[4,2,128,128]{3,2,1,0:T(8,128)}, f32[4,2,128,128]{3,2,1,0:T(8,128)S(1)}, u32[]{:S(2)}, u32[]{:S(2)}) collective-permute-start(f32[4,2,128,128]{3,2,1,0:T(8,128)} %get-tuple-element.125), channel_id=1, source_target_pairs={{0,8},{8,0},{16,24},{24,16},{1,9},{9,1},{17,25},{25,17},{2,10},{10... | collective-permute-start | bytes 1572872 | tf_op jit(solution)/shard_map/ppermute | solution.py:521
  154.2 1.0 copy-start.2
  157.5 26.3 %collective-permute-start.7 = (f32[4,2,128,128]{3,2,1,0:T(8,128)}, f32[4,2,128,128]{3,2,1,0:T(8,128)S(1)}, u32[]{:S(2)}, u32[]{:S(2)}) collective-permute-start(f32[4,2,128,128]{3,2,1,0:T(8,128)} %get-tuple-element.117), channel_id=1, source_target_pairs={{0,16},{8,24},{16,0},{24,8},{1,17},{9,25},{17,1},{25,9},{2,18},{10... | collective-permute-start | bytes 1572872 | tf_op jit(solution)/shard_map/ppermute | solution.py:521
  159.5 18.4 %collective-permute-start.14 = (f32[2,2,128,128]{3,2,1,0:T(8,128)S(1)}, f32[2,2,128,128]{3,2,1,0:T(8,128)S(1)}, u32[]{:S(2)}, u32[]{:S(2)}) collective-permute-start(f32[2,2,128,128]{3,2,1,0:T(8,128)S(1)} %copy-done.8), channel_id=1, source_target_pairs={{0,2},{1,3},{2,0},{3,1},{4,6},{5,7},{6,4},{7,5},{8,10},{9,11},{10,... | collective-permute-start | bytes 786440 | tf_op jit(solution)/shard_map/ppermute | solution.py:521
  161.1 12.7 %collective-permute-start.9 = (f32[2,2,128,128]{3,2,1,0:T(8,128)S(1)}, f32[2,2,128,128]{3,2,1,0:T(8,128)S(1)}, u32[]{:S(2)}, u32[]{:S(2)}) collective-permute-start(f32[2,2,128,128]{3,2,1,0:T(8,128)S(1)} %copy-done.19), channel_id=1, source_target_pairs={{0,8},{8,0},{16,24},{24,16},{1,9},{9,1},{17,25},{25,17},{2,10},{10... | collective-permute-start | bytes 786440 | tf_op jit(solution)/shard_map/ppermute | solution.py:521
  169.1 0.8 copy-start.5
  171.8 6.8 %collective-permute-start.13 = (f32[2,2,128,128]{3,2,1,0:T(8,128)}, f32[2,2,128,128]{3,2,1,0:T(8,128)S(1)}, u32[]{:S(2)}, u32[]{:S(2)}) collective-permute-start(f32[2,2,128,128]{3,2,1,0:T(8,128)} %get-tuple-element.127), channel_id=1, source_target_pairs={{0,16},{8,24},{16,0},{24,8},{1,17},{9,25},{17,1},{25,9},{2,18},{10... | collective-permute-start | bytes 786440 | tf_op jit(solution)/shard_map/ppermute | solution.py:521
  176.3 10.8 %collective-permute-start.10 = (f32[2,2,128,128]{3,2,1,0:T(8,128)}, f32[2,2,128,128]{3,2,1,0:T(8,128)S(1)}, u32[]{:S(2)}, u32[]{:S(2)}) collective-permute-start(f32[2,2,128,128]{3,2,1,0:T(8,128)} %sum_of.18), channel_id=1, source_target_pairs={{0,2},{1,3},{2,0},{3,1},{4,6},{5,7},{6,4},{7,5},{8,10},{9,11},{10,... | collective-permute-start | bytes 786440 | tf_op jit(solution)/shard_map/ppermute | solution.py:521
  177.9 0.8 copy-start.12
  181.2 13.3 %collective-permute-start.15 = (f32[2,2,128,128]{3,2,1,0:T(8,128)}, f32[2,2,128,128]{3,2,1,0:T(8,128)S(1)}, u32[]{:S(2)}, u32[]{:S(2)}) collective-permute-start(f32[2,2,128,128]{3,2,1,0:T(8,128)} %sum_of.21), channel_id=1, source_target_pairs={{0,4},{1,5},{2,6},{3,7},{4,0},{5,1},{6,2},{7,3},{8,12},{9,13},{10,... | collective-permute-start | bytes 786440 | tf_op jit(solution)/shard_map/ppermute | solution.py:521
  183.8 0.8 copy-start.4
  186.5 8.0 %collective-permute-start.8 = (f32[2,2,128,128]{3,2,1,0:T(8,128)}, f32[2,2,128,128]{3,2,1,0:T(8,128)S(1)}, u32[]{:S(2)}, u32[]{:S(2)}) collective-permute-start(f32[2,2,128,128]{3,2,1,0:T(8,128)} %get-tuple-element.119), channel_id=1, source_target_pairs={{0,8},{8,0},{16,24},{24,16},{1,9},{9,1},{17,25},{25,17},{2,10},{10... | collective-permute-start | bytes 786440 | tf_op jit(solution)/shard_map/ppermute | solution.py:521
  187.0 7.5 %copy-start.11 = (f32[2,2,128,128]{3,2,1,0:T(8,128)}, f32[2,2,128,128]{3,2,1,0:T(8,128)S(1)}, u32[]{:S(2)}) copy-start(f32[2,2,128,128]{3,2,1,0:T(8,128)S(1)} %collective-permute-done.10.refs_2_) | copy-start | bytes 786436
  194.5 0.8 copy-start.15
  (4 other events, 2.8 us)

commit v2 on v1

--- a/solution.py
+++ b/solution.py
@@ -22,7 +22,6 @@
 PAIR = 2 * LANES
 DEPTH = BLOCKS * PAIR
 FREQS = BLOCKS * LANES
-FINE = 64
 COL_TILES = FOLD // PAIR
 
 
@@ -32,7 +31,7 @@
 
 def cos_sin(first, second):
     angle = angles_of(first, second)
-    return np.stack([np.cos(angle), np.sin(angle)]).astype(np.float32)
+    return np.stack([np.cos(angle), np.sin(angle)])
 
 
 def freqs(parity):
@@ -55,11 +54,15 @@
     return term(left[0], right[0]) + term(left[0], right[1]) + term(left[1], right[0])
 
 
-def turn(first, second):
-    return (
-        first[0] * second[0] - first[1] * second[1],
-        first[1] * second[0] + first[0] * second[1],
-    )
+def paired(values):
+    blocks = values.reshape(values.shape[:-1] + (-1, LANES))
+    return np.moveaxis(blocks, 0, -2).reshape(values.shape[1:-1] + (-1,))
+
+
+def table_halves(table):
+    high = table.astype(jnp.bfloat16)
+    low = (table - high.astype(np.float64)).astype(jnp.bfloat16)
+    return jnp.asarray(high), jnp.asarray(low)
 
 
 def put(refs, place, value):
@@ -104,8 +107,7 @@
     )(sign, plane_waves, transmission)
 
 
-def column_forward_kernel(parity_ref, field_ref, fine_ref, coarse_ref, out_ref, *scratch):
-    field, table = scratch[:2], scratch[2:]
+def column_forward_kernel(parity_ref, field_ref, table_hi, table_lo, out_ref, *field):
     rows = field_ref.shape[1]
 
     @pl.when(pl.program_id(0) == 0)
@@ -113,23 +115,15 @@
         for part in (0, 1):
             put(field, slice(part * rows, (part + 1) * rows), field_ref[part])
 
-    fine = fine_ref[0, 0], fine_ref[0, 1]
-    for step in range(FOLD // FINE):
-        place = slice(step, step + 1)
-        value = turn((coarse_ref[0, 0, place], coarse_ref[0, 1, place]), fine)
-        rows_here = slice(step * FINE, (step + 1) * FINE)
-        put(table, (rows_here, slice(0, LANES)), value[0])
-        put(table, (rows_here, slice(LANES, PAIR)), value[1])
-    result = dot3((field[0][...], field[1][...]), (table[0][...], table[1][...]))
+    result = dot3((field[0][...], field[1][...]), (table_hi[0], table_lo[0]))
     for part in (0, 1):
         out_ref[part] = result[part * rows : (part + 1) * rows]
 
 
 def column_forward(parity, field):
     rows = field.shape[1]
-    fine = both(lambda freq: cos_sin(np.arange(FINE), freq))
-    coarse = both(lambda freq: cos_sin(np.arange(0, FOLD, FINE), freq))
-    half = functools.partial(pltpu.VMEM, dtype=jnp.bfloat16)
+    table = table_halves(both(lambda freq: paired(cos_sin(np.arange(FOLD), freq))))
+    table_spec = pl.BlockSpec((1, FOLD, PAIR), lambda j, c: (c[0], 0, j))
     return pl.pallas_call(
         column_forward_kernel,
         out_shape=jax.ShapeDtypeStruct((2, rows, DEPTH), jnp.float32),
@@ -138,11 +132,11 @@
             grid=(BLOCKS,),
             in_specs=[
                 pl.BlockSpec((2, rows, FOLD), lambda j, *_: (0, 0, 0)),
-                pl.BlockSpec((1, 2, FINE, LANES), lambda j, c: (c[0], 0, 0, j)),
-                pl.BlockSpec((1, 2, FOLD // FINE, LANES), lambda j, c: (c[0], 0, 0, j)),
+                table_spec,
+                table_spec,
             ],
             out_specs=pl.BlockSpec((2, rows, PAIR), lambda j, *_: (0, 0, j)),
-            scratch_shapes=[half((2 * rows, FOLD))] * 2 + [half((FOLD, PAIR))] * 2,
+            scratch_shapes=[pltpu.VMEM((2 * rows, FOLD), jnp.bfloat16)] * 2,
         ),
         cost_estimate=pl.CostEstimate(
             flops=12 * rows * FOLD * DEPTH,
@@ -150,44 +144,42 @@
             transcendentals=0,
         ),
         name="column_forward",
-    )(parity, field, jnp.asarray(fine), jnp.asarray(coarse))
+    )(parity, field, *table)
 
 
 def row_forward_kernel(
-    parity_ref, mine_ref, theirs_ref, fine_ref, coarse_ref, down_ref, along_ref,
-    out_hi, out_lo, table_hi, table_lo,
+    parity_ref, mine_ref, theirs_ref, table_hi, table_lo, down_ref, along_ref,
+    out_hi, out_lo, field_hi, field_lo,
 ):
-    tables = (table_hi, table_lo)
-
-    @pl.when(pl.program_id(0) == 0)
-    def _():
-        for block in range(2 * BLOCKS):
-            freq = slice(block * LANES, (block + 1) * LANES)
-            fine = fine_ref[0, freq], fine_ref[1, freq]
-            for step in range(coarse_ref.shape[3]):
-                place = slice(step, step + 1)
-                value = turn((coarse_ref[0, 0, freq, place], coarse_ref[0, 1, freq, place]), fine)
-                cols = slice(step * LANES, (step + 1) * LANES)
-                for kind in (0, 1):
-                    start = block * PAIR + kind * LANES
-                    put(tables, (slice(start, start + LANES), cols), value[kind])
-
-    parts = [
-        halves_of(jnp.concatenate([mine_ref[part], theirs_ref[part]])) for part in (0, 1)
-    ]
+    rows = mine_ref.shape[1]
+    field = (field_hi, field_lo)
+    core = parity_ref[0]
+    for place, ref in ((core, mine_ref), (1 - core, theirs_ref)):
+        start = pl.ds(pl.multiple_of(place * rows, LANES), rows)
+        for part in (0, 1):
+            put(field, (start, slice(part * PAIR, (part + 1) * PAIR)), ref[part])
     cos_x, sin_x, square_x = (along_ref[0, i : i + 1] for i in range(3))
+    outs = (out_hi, out_lo)
 
     def blocks(parity, count):
-        rows = slice(parity * DEPTH, parity * DEPTH + count * PAIR)
-        table = table_hi[rows], table_lo[rows]
-        real_part, imag_part = dot3(table, parts[0]), dot3(table, parts[1])
-        cos_y, sin_y, square_y = (down_ref[rows, i : i + 1] for i in range(3))
-        inside = 9.0 * (square_y + square_x) <= GRID * GRID
-        prop_re = jnp.where(inside, cos_y * cos_x - sin_y * sin_x, 0.0)
-        prop_im = jnp.where(inside, -(sin_y * cos_x + cos_y * sin_x), 0.0)
-        outs = (out_hi, out_lo)
-        put(outs, (0, rows), prop_re * real_part - prop_im * imag_part)
-        put(outs, (1, rows), prop_re * imag_part + prop_im * real_part)
+        first = parity * DEPTH
+        part = slice(first, first + count * PAIR)
+        result = dot3((table_hi[part], table_lo[part]), (field_hi[...], field_lo[...]))
+        for block in range(count):
+            freq = slice((parity * BLOCKS + block) * LANES, (parity * BLOCKS + block + 1) * LANES)
+            cos_y, sin_y, square_y = (down_ref[freq, i : i + 1] for i in range(3))
+            inside = 9.0 * (square_y + square_x) <= GRID * GRID
+            prop_re = jnp.where(inside, cos_y * cos_x - sin_y * sin_x, 0.0)
+            prop_im = jnp.where(inside, -(sin_y * cos_x + cos_y * sin_x), 0.0)
+            for kind in (0, 1):
+                start = block * PAIR + kind * LANES
+                place = slice(first + start, first + start + LANES)
+                for side in (0, 1):
+                    cols = slice(side * LANES, (side + 1) * LANES)
+                    real_part = result[start : start + LANES, cols]
+                    imag_part = result[start : start + LANES, slice(PAIR + side * LANES, PAIR + (side + 1) * LANES)]
+                    put(outs, (0, place, cols), prop_re * real_part - prop_im * imag_part)
+                    put(outs, (1, place, cols), prop_re * imag_part + prop_im * real_part)
 
     last = pl.program_id(0) == BLOCKS - 1
     for parity in (0, 1):
@@ -201,28 +193,16 @@
     return [np.cos(angle) * weight, np.sin(angle) * weight, freq.astype(np.float64) ** 2]
 
 
-def paired(values):
-    blocks = values.reshape(values.shape[:-1] + (-1, 1, LANES))
-    return np.concatenate([blocks, blocks], -2).reshape(values.shape[:-1] + (-1,))
-
-
 def row_forward(parity, mine, theirs):
     rows = mine.shape[1]
     all_freqs = np.concatenate([freqs(0), freqs(1)])
-    fine = cos_sin(all_freqs, np.arange(LANES))
-    starts = np.arange(0, rows, LANES)
-    coarse = np.stack(
-        [
-            cos_sin(all_freqs, np.concatenate([starts + rows * core, starts + rows * (1 - core)]))
-            for core in (0, 1)
-        ]
-    )
-    down = paired(np.stack(axis_factors(all_freqs))).T
-    along = np.stack([paired(np.stack(axis_factors(freqs(core)))) for core in (0, 1)])
-    down, along = down.astype(np.float32), along.astype(np.float32)
+    table = table_halves(paired(cos_sin(np.arange(2 * rows), all_freqs)).T)
+    down = np.stack(axis_factors(all_freqs)).T.astype(np.float32)
+    along = both(lambda freq: np.stack(axis_factors(freq))).astype(np.float32)
     tile = pl.BlockSpec((2, rows, PAIR), lambda j, *_: (0, 0, j))
     out = jax.ShapeDtypeStruct((2, 2 * DEPTH, DEPTH), jnp.bfloat16)
     out_spec = pl.BlockSpec((2, 2 * DEPTH, PAIR), lambda j, *_: (0, 0, j))
+    table_spec = pl.BlockSpec((2 * DEPTH, 2 * rows), lambda j, *_: (0, 0))
     return pl.pallas_call(
         row_forward_kernel,
         out_shape=(out, out),
@@ -232,13 +212,13 @@
             in_specs=[
                 tile,
                 tile,
-                pl.BlockSpec(fine.shape, lambda j, *_: (0, 0, 0)),
-                pl.BlockSpec((1,) + coarse.shape[1:], lambda j, c: (c[0], 0, 0, 0)),
+                table_spec,
+                table_spec,
                 pl.BlockSpec(down.shape, lambda j, *_: (0, 0)),
-                pl.BlockSpec((1, 3, PAIR), lambda j, c: (c[0], 0, j)),
+                pl.BlockSpec((1, 3, LANES), lambda j, c: (c[0], 0, j)),
             ],
             out_specs=(out_spec, out_spec),
-            scratch_shapes=[pltpu.VMEM((2 * DEPTH, 2 * rows), jnp.bfloat16)] * 2,
+            scratch_shapes=[pltpu.VMEM((2 * rows, 2 * PAIR), jnp.bfloat16)] * 2,
         ),
         cost_estimate=pl.CostEstimate(
             flops=48 * rows * DEPTH * DEPTH,
@@ -246,34 +226,18 @@
             transcendentals=0,
         ),
         name="row_forward",
-    )(
-        parity, mine, theirs, jnp.asarray(fine), jnp.asarray(coarse), jnp.asarray(down),
-        jnp.asarray(along),
-    )
-
-
-def row_inverse_kernel(steps, spec_hi, spec_lo, fine_ref, coarse_ref, out_hi, out_lo, *tables):
-    count = len(steps) * FINE
-
-    @pl.when(pl.program_id(0) == 0)
-    def _():
-        for block in range(2 * BLOCKS):
-            freq = slice(block * LANES, (block + 1) * LANES)
-            fine = fine_ref[0, :, freq], fine_ref[1, :, freq]
-            for index, step in enumerate(steps):
-                place = slice(step, step + 1)
-                value = turn((coarse_ref[0, place, freq], coarse_ref[1, place, freq]), fine)
-                rows = slice(index * FINE, (index + 1) * FINE)
-                for kind in (0, 1):
-                    start = block * PAIR + kind * LANES
-                    put(tables, (rows, slice(start, start + LANES)), value[kind])
+    )(parity, mine, theirs, *table, jnp.asarray(down), jnp.asarray(along))
+
+
+def row_inverse_kernel(spec_hi, spec_lo, table_hi, table_lo, out_hi, out_lo):
+    count = table_hi.shape[0]
 
     def blocks(depth):
         sums = []
         for parity in (0, 1):
             part = slice(parity * DEPTH, parity * DEPTH + depth * PAIR)
             sums.append(
-                dot3((tables[0][:, part], tables[1][:, part]), (spec_hi[0, part], spec_lo[0, part]))
+                dot3((table_hi[:, part], table_lo[:, part]), (spec_hi[0, part], spec_lo[0, part]))
             )
         outs = (out_hi, out_lo)
         put(outs, (0, slice(0, count)), sums[0] + sums[1])
@@ -284,66 +248,43 @@
     pl.when(jnp.logical_not(last))(functools.partial(blocks, BLOCKS))
 
 
-def row_inverse(spectrum, steps):
-    count = len(steps) * FINE
-    all_freqs = np.concatenate([freqs(0), freqs(1)])
-    fine = cos_sin(np.arange(FINE), all_freqs)
-    coarse = cos_sin(np.arange(-HALF, FOLD + HALF, FINE), all_freqs)
+def row_inverse(spectrum, rows):
+    count = len(rows)
+    table = table_halves(paired(cos_sin(rows, np.concatenate([freqs(0), freqs(1)]))))
     out = jax.ShapeDtypeStruct((2, 2 * count, DEPTH), jnp.bfloat16)
     tile = pl.BlockSpec((1, 2 * count, PAIR), lambda j: (j // BLOCKS, 0, j % BLOCKS))
     spec = pl.BlockSpec((1, 2 * DEPTH, PAIR), lambda j: (j // BLOCKS, 0, j % BLOCKS))
+    table_spec = pl.BlockSpec((count, 2 * DEPTH), lambda j: (0, 0))
     return pl.pallas_call(
-        functools.partial(row_inverse_kernel, steps),
+        row_inverse_kernel,
         out_shape=(out, out),
         grid=(2 * BLOCKS,),
-        in_specs=[
-            spec,
-            spec,
-            pl.BlockSpec(fine.shape, lambda j: (0, 0, 0)),
-            pl.BlockSpec(coarse.shape, lambda j: (0, 0, 0)),
-        ],
+        in_specs=[spec, spec, table_spec, table_spec],
         out_specs=(tile, tile),
-        scratch_shapes=[pltpu.VMEM((count, 2 * DEPTH), jnp.bfloat16)] * 2,
         cost_estimate=pl.CostEstimate(
             flops=24 * count * DEPTH * DEPTH,
             bytes_accessed=16 * DEPTH * DEPTH + 16 * count * DEPTH,
             transcendentals=0,
         ),
         name="row_inverse",
-    )(*spectrum, jnp.asarray(fine), jnp.asarray(coarse))
+    )(*spectrum, *table)
 
 
 def column_inverse_kernel(
     layout, info_ref, slot_ref, pos_ref, re_ref, im_ref, sign_ref,
-    rows_hi, rows_lo, fine_ref, coarse_ref, keep_ref, send_ref, field, table_hi, table_lo,
+    rows_hi, rows_lo, table_hi, table_lo, keep_ref, send_ref, field,
 ):
     chip_rows, waves, own, segments = layout
     height = chip_rows + WINDOW
     step = pl.program_id(0)
     tile = step % COL_TILES
-    tables = (table_hi, table_lo)
-
-    @pl.when(step < COL_TILES)
-    def _():
-        for block in range(BLOCKS):
-            freq = slice(block * LANES, (block + 1) * LANES)
-            fine = fine_ref[0, 0, freq], fine_ref[0, 1, freq]
-            for side in (0, 1):
-                place = slice(side, side + 1)
-                value = turn(
-                    (coarse_ref[0, 0, 0, freq, place], coarse_ref[0, 0, 1, freq, place]), fine
-                )
-                cols = slice(side * LANES, (side + 1) * LANES)
-                for kind in (0, 1):
-                    start = block * PAIR + kind * LANES
-                    put(tables, (tile, slice(start, start + LANES), cols), value[kind])
 
     @pl.when(step < 2 * segments * COL_TILES)
     def _():
         part = step // COL_TILES % 2
         start = pl.multiple_of(step // (2 * COL_TILES) * height, LANES)
         rows = pl.ds(start, height)
-        value = dot3((rows_hi[0], rows_lo[0]), (table_hi[tile], table_lo[tile]))
+        value = dot3((rows_hi[0], rows_lo[0]), (table_hi[0], table_lo[0]))
         field[part, 2 * tile, rows] = value[:, :LANES]
         field[part, 2 * tile + 1, rows] = value[:, LANES:]
 
@@ -390,11 +331,8 @@
     chip_rows, _, _, segments = layout
     count = slots.shape[1] // 2
     height = chip_rows + WINDOW
-    fine = both(lambda freq: cos_sin(freq, np.arange(LANES)))
-    coarse = both(
-        lambda freq: np.stack(
-            [cos_sin(freq, PAIR * tile + np.array([0, LANES])) for tile in range(COL_TILES)]
-        )
+    table = table_halves(
+        both(lambda freq: paired(cos_sin(np.arange(FOLD), freq)).T)
     )
     last = 2 * segments * COL_TILES - 1
 
@@ -403,6 +341,9 @@
         return i // COL_TILES % 2, info[3 + i // (2 * COL_TILES)], 0
 
     rows_spec = pl.BlockSpec((1, height, DEPTH), rows_map)
+    table_spec = pl.BlockSpec(
+        (1, DEPTH, PAIR), lambda i, info, *_: (info[2], 0, jnp.minimum(i, last) % COL_TILES)
+    )
     out = jax.ShapeDtypeStruct((count, 2, WINDOW, WINDOW), jnp.float32)
     out_spec = pl.BlockSpec(
         (count, 2, WINDOW, WINDOW), lambda i, *_: (0, 0, 0, 0), pipeline_mode=pl.Buffered(1)
@@ -416,17 +357,12 @@
             in_specs=[
                 rows_spec,
                 rows_spec,
-                pl.BlockSpec((1,) + fine.shape[1:], lambda i, info, *_: (info[2], 0, 0, 0)),
-                pl.BlockSpec(
-                    (1, 1) + coarse.shape[2:],
-                    lambda i, info, *_: (info[2], jnp.minimum(i, COL_TILES - 1), 0, 0, 0),
-                ),
+                table_spec,
+                table_spec,
             ],
             out_specs=(out_spec, out_spec),
             scratch_shapes=[
-                pltpu.VMEM((2, 2 * COL_TILES + 1, segments * height, WINDOW), jnp.float32),
-                pltpu.VMEM((COL_TILES, DEPTH, PAIR), jnp.bfloat16),
-                pltpu.VMEM((COL_TILES, DEPTH, PAIR), jnp.bfloat16),
+                pltpu.VMEM((2, 2 * COL_TILES + 1, segments * height, WINDOW), jnp.float32)
             ],
         ),
         cost_estimate=pl.CostEstimate(
@@ -436,8 +372,7 @@
         ),
         name="column_inverse",
     )(
-        info, jnp.asarray(slots), positions, *weights, sign, *rows, jnp.asarray(fine),
-        jnp.asarray(coarse),
+        info, jnp.asarray(slots), positions, *weights, sign, *rows, *table,
     )
 
 
@@ -505,8 +440,8 @@
         out_shape=jax.ShapeDtypeStruct((count, WINDOW, WINDOW), jnp.float32),
         name="power_of",
     )(
-        *terms, jnp.asarray(np.concatenate(list(table))),
-        jnp.asarray(np.concatenate(list(table), axis=1)),
+        *terms, jnp.asarray(np.concatenate(list(table)).astype(np.float32)),
+        jnp.asarray(np.concatenate(list(table), axis=1).astype(np.float32)),
     )
 
 
@@ -569,12 +504,13 @@
             info.append(away // far * segments + away % far // 2)
         return jnp.stack(info)
 
-    def steps_of(odd):
-        steps = []
-        for away in range(odd, far, 2):
-            first = chip_rows * away // FINE
-            steps += range(first, first + (chip_rows + WINDOW) // FINE)
-        return tuple(steps)
+    def rows_of(odd):
+        return np.concatenate(
+            [
+                chip_rows * away - HALF + np.arange(chip_rows + WINDOW)
+                for away in range(odd, far, 2)
+            ]
+        )
 
     def cut(odd, half, rows):
         keep, send = column_inverse(
@@ -590,7 +526,7 @@
         return lax.optimization_barrier((value,) + before)
 
     upper, lower = 1, 0
-    rows_odd = row_inverse(spectrum, steps_of(1))
+    rows_odd = row_inverse(spectrum, rows_of(1))
     odd_upper = cut(1, upper, rows_odd)
     rows_odd, keep = later(rows_odd, odd_upper[0])
     odd_upper = (keep, odd_upper[1])
@@ -614,7 +550,7 @@
     spectrum, keep = spectrum
     stages[1, lower] = [(keep, odd_lower[1]), 0]
     spectrum = advance(spectrum, (1, upper))
-    rows_even = row_inverse(spectrum, steps_of(0))
+    rows_even = row_inverse(spectrum, rows_of(0))
     rows_even = advance(rows_even, (1, upper), (1, lower))
     even_upper = cut(0, upper, rows_even)
     rows_even, keep = later(rows_even, even_upper[0])

time: 209 us -> 209 us (level)
  Pallas kernels: 150 us -> 147 us
    pallas_call x4, Pallas kernels: 61.2 us -> 58.9 us  [column_inverse(): pl.pallas_call(functools.partial(column_inverse_kernel, layout), out_shap...]
    unnamed x40 -> x42, local copies, waits for them, and re-layouts: 9.95 us -> 11.4 us
  transfers between devices with their start and end apart: 16 -> 16, of which waited for: 5 -> 5; matrix products, arithmetic and copies ran while one was open for 2% -> 2% of each run, Pallas kernels for 42% -> 41%
where the time goes in v2:
time: 209 us; the launch traced here: 207 us
  Pallas kernels  147 us (70%)
  starting transfers between devices  16.9 us (8%)
  waiting for transfers between devices  16.7 us (8%)
  local copies, waits for them, and re-layouts  13.7 us (7%)
  blocking collectives  7.61 us (4%)
  other arithmetic  3.7 us (2%)
    pallas_call x4, Pallas kernels, column_inverse(): pl.pallas_call(functools.partial(column_inverse_kernel, layout), out_shap...  58.9 us
    pallas_call x2, Pallas kernels, row_inverse(): pl.pallas_call(row_inverse_kernel, out_shape=(out, out), grid=(2 * BLOCKS...  28.3 us
    pallas_call x11, Pallas kernels, sum_of(): pl.pallas_call(functools.partial(sum_kernel, len(terms)), out_shape=(out,...  22.6 us
    ppermute x16, starting transfers between devices, flip(): return lax.ppermute(block, axis, [(i, i ^ bit) for i in range(count)])  16.9 us
    ppermute x16, waiting for transfers between devices, flip(): return lax.ppermute(block, axis, [(i, i ^ bit) for i in range(count)])  16.7 us
    pallas_call x1, Pallas kernels, row_forward(): pl.pallas_call(row_forward_kernel, out_shape=(out, out), grid_spec=pltpu....  13.7 us
    pallas_call x2, Pallas kernels, column_forward(): pl.pallas_call(column_forward_kernel, out_shape=jax.ShapeDtypeStruct((2,...  12.9 us
    unnamed x42, local copies, waits for them, and re-layouts  11.4 us
  transfers between devices with their start and end apart: 16, of which 5 were waited for; matrix products, arithmetic and copies ran while one was open for 2% of the time, Pallas kernels for 41%

profile of v2, /device:TPU:0, one launch (start us, length us, event | category | flops | bytes accessed | tf_op | source)
XLA Modules:
  0.0 206.9 jit_solution(552334745893557420)
XLA Ops:
  0.0 7.9 %split_columns.1 = (f32[2,256,1024]{2,1,0:T(8,128)}, f32[2,256,1024]{2,1,0:T(8,128)}) custom-call(f32[1]{0:T(128)} %bitcast.9.sign_ref, f32[2,1,256,2048]{3,2,1,0:T(8,128)} %wave_ref.1, f32[1,2,256,2048]{3,2,1,0:T(8,128)} %trans_ref.1), custom_call_target="tpu_custom_call" | custom-call | flops 10485760 | bytes 12582912 | tf_op jit(solution)/shard_map/split_columns/pallas_call | solution.py:91
  10.9 1.8 sine_multiply_fusion
  14.0 6.4 %column_forward.2.mine_ref = f32[2,256,768]{2,1,0:T(8,128)} custom-call(s32[1]{0:T(128)} %bitcast.2.parity_ref, f32[2,256,1024]{2,1,0:T(8,128)} %get-tuple-element.67.field_ref, bf16[2,1024,768]{2,1,0:T(8,128)(2,1)} %constant.238.clone.table_hi, bf16[2,1024,768]{2,1,0:T(8,128)(2,1)} %constant.239.clone.table_lo), custom_call_target="tpu_custom_call" | custom-call | flops 2415919104 | bytes 3670016 | tf_op jit(solution)/shard_map/column_forward/pallas_call | solution.py:127
  21.8 6.4 %column_forward.3.theirs_ref = f32[2,256,768]{2,1,0:T(8,128)} custom-call(s32[1]{0:T(128)} %bitcast.2.parity_ref, f32[2,256,1024]{2,1,0:T(8,128)} %copy-done, bf16[2,1024,768]{2,1,0:T(8,128)(2,1)} %constant.238.clone.table_hi, bf16[2,1024,768]{2,1,0:T(8,128)(2,1)} %constant.239.clone.table_lo), custom_call_target="tpu_custom_call" | custom-call | flops 2415919104 | bytes 3670016 | tf_op jit(solution)/shard_map/column_forward/pallas_call | solution.py:127
  28.2 13.7 %row_forward.1 = (bf16[2,1536,768]{2,1,0:T(8,128)(2,1)}, bf16[2,1536,768]{2,1,0:T(8,128)(2,1)}) custom-call(s32[1]{0:T(128)} %bitcast.2.parity_ref, f32[2,256,768]{2,1,0:T(8,128)} %column_forward.2.mine_ref, f32[2,256,768]{2,1,0:T(8,128)} %column_forward.3.theirs_ref, bf16[1536,512]{1,0:T(8,128)(2,1)} %constant.240.clone.table_hi, ...), custom_call_target="tpu_custom_call" | custom-call | flops 7247757312 | bytes 12582912 | tf_op jit(solution)/shard_map/row_forward/pallas_call | solution.py:206
  42.0 14.0 %row_inverse.2 = (bf16[2,1280,768]{2,1,0:T(8,128)(2,1)}, bf16[2,1280,768]{2,1,0:T(8,128)(2,1)}) custom-call(bf16[2,1536,768]{2,1,0:T(8,128)(2,1)} %get-tuple-element.85.spec_hi, bf16[2,1536,768]{2,1,0:T(8,128)(2,1)} %get-tuple-element.86.spec_lo, bf16[640,1536]{1,0:T(8,128)(2,1)} %constant.244.clone.table_hi, bf16[640,1536]{1,0:T(8,128)(2,1)} %constant.245.clone.table_lo), custom_call_target="tpu_custom_call" | custom-call | flops 9059696640 | bytes 17301504 | tf_op jit(solution)/shard_map/row_inverse/pallas_call | solution.py:258
  56.0 14.8 %column_inverse.4 = (f32[8,2,128,128]{3,2,1,0:T(8,128)}, f32[8,2,128,128]{3,2,1,0:T(8,128)}) custom-call(s32[4]{0:T(128)} %get-tuple-element.133.info_ref, s32[4,16]{1,0:T(4,128)} %constant.248.clone.slot_ref, s32[2,64]{1,0:T(2,128)} %bitcast.55, f32[64]{0:T(128)} %cosine_multiply_fusion.re_ref, f32[64]{0:T(128)} %get-tuple-element.131.im_ref, ...), custom_call_target="tpu_custom_call" | custom-call | flops 6039797760 | bytes 6029312 | tf_op jit(solution)/shard_map/column_inverse/pallas_call | solution.py:351
  70.8 14.7 %column_inverse.5 = (f32[8,2,128,128]{3,2,1,0:T(8,128)}, f32[8,2,128,128]{3,2,1,0:T(8,128)}) custom-call(s32[4]{0:T(128)} %get-tuple-element.134.info_ref, s32[4,16]{1,0:T(4,128)} %constant.249.clone.slot_ref, s32[2,64]{1,0:T(2,128)} %bitcast.56, f32[64]{0:T(128)} %cosine_multiply_fusion.re_ref, f32[64]{0:T(128)} %get-tuple-element.131.im_ref, ...), custom_call_target="tpu_custom_call" | custom-call | flops 6039797760 | bytes 6029312 | tf_op jit(solution)/shard_map/column_inverse/pallas_call | solution.py:351
  86.9 2.4 %sum_of.11 = (f32[4,2,128,128]{3,2,1,0:T(8,128)}, f32[4,2,128,128]{3,2,1,0:T(8,128)}) custom-call(f32[2,4,2,128,128]{4,3,2,1,0:T(8,128)} %bitcast.42, f32[2,4,2,128,128]{4,3,2,1,0:T(8,128)} %bitcast.45), custom_call_target="tpu_custom_call" | custom-call | flops 1048576 | bytes 3145728 | tf_op jit(solution)/shard_map/sum_of/pallas_call | solution.py:404
  89.3 2.5 %collective-permute-start.2 = (f32[4,2,128,128]{3,2,1,0:T(8,128)}, f32[4,2,128,128]{3,2,1,0:T(8,128)S(1)}, u32[]{:S(2)}, u32[]{:S(2)}) collective-permute-start(f32[4,2,128,128]{3,2,1,0:T(8,128)} %get-tuple-element.90), channel_id=1, source_target_pairs={{0,8},{8,0},{16,24},{24,16},{1,9},{9,1},{17,25},{25,17},{2,10},{10... | collective-permute-start | bytes 1572872 | tf_op jit(solution)/shard_map/ppermute | solution.py:456
  92.8 2.4 %sum_of.13 = (f32[4,2,128,128]{3,2,1,0:T(8,128)}, f32[4,2,128,128]{3,2,1,0:T(8,128)}) custom-call(f32[2,4,2,128,128]{4,3,2,1,0:T(8,128)} %bitcast.41, f32[2,4,2,128,128]{4,3,2,1,0:T(8,128)} %bitcast.43), custom_call_target="tpu_custom_call" | custom-call | flops 1048576 | bytes 3145728 | tf_op jit(solution)/shard_map/sum_of/pallas_call | solution.py:404
  95.2 14.2 %row_inverse.3 = (bf16[2,1280,768]{2,1,0:T(8,128)(2,1)}, bf16[2,1280,768]{2,1,0:T(8,128)(2,1)}) custom-call(bf16[2,1536,768]{2,1,0:T(8,128)(2,1)} %get-tuple-element.85.spec_hi, bf16[2,1536,768]{2,1,0:T(8,128)(2,1)} %get-tuple-element.86.spec_lo, bf16[640,1536]{1,0:T(8,128)(2,1)} %constant.250.clone.table_hi, bf16[640,1536]{1,0:T(8,128)(2,1)} %constant.251.clone.table_lo), custom_call_target="tpu_custom_call" | custom-call | flops 9059696640 | bytes 17301504 | tf_op jit(solution)/shard_map/row_inverse/pallas_call | solution.py:258
  110.2 1.9 sum_of.12
  112.1 1.5 collective-permute-start.5
  114.2 14.7 %column_inverse.6 = (f32[8,2,128,128]{3,2,1,0:T(8,128)}, f32[8,2,128,128]{3,2,1,0:T(8,128)}) custom-call(s32[4]{0:T(128)} %get-tuple-element.129.info_ref, s32[4,16]{1,0:T(4,128)} %constant.252.clone.slot_ref, s32[2,64]{1,0:T(2,128)} %bitcast.57, f32[64]{0:T(128)} %cosine_multiply_fusion.re_ref, f32[64]{0:T(128)} %get-tuple-element.131.im_ref, ...), custom_call_target="tpu_custom_call" | custom-call | flops 6039797760 | bytes 6029312 | tf_op jit(solution)/shard_map/column_inverse/pallas_call | solution.py:351
  129.6 1.8 sum_of.15
  132.8 1.9 sum_of.14
  134.7 14.7 %column_inverse.7 = (f32[8,2,128,128]{3,2,1,0:T(8,128)}, f32[8,2,128,128]{3,2,1,0:T(8,128)}) custom-call(s32[4]{0:T(128)} %get-tuple-element.135.info_ref, s32[4,16]{1,0:T(4,128)} %constant.253.clone.slot_ref, s32[2,64]{1,0:T(2,128)} %bitcast.58, f32[64]{0:T(128)} %cosine_multiply_fusion.re_ref, f32[64]{0:T(128)} %get-tuple-element.131.im_ref, ...), custom_call_target="tpu_custom_call" | custom-call | flops 6039797760 | bytes 6029312 | tf_op jit(solution)/shard_map/column_inverse/pallas_call | solution.py:351
  150.5 2.4 %sum_of.19 = (f32[4,2,128,128]{3,2,1,0:T(8,128)}, f32[4,2,128,128]{3,2,1,0:T(8,128)}) custom-call(f32[2,4,2,128,128]{4,3,2,1,0:T(8,128)} %bitcast.38, f32[2,4,2,128,128]{4,3,2,1,0:T(8,128)} %bitcast.39), custom_call_target="tpu_custom_call" | custom-call | flops 1048576 | bytes 3145728 | tf_op jit(solution)/shard_map/sum_of/pallas_call | solution.py:404
  154.2 2.4 %sum_of.16 = (f32[4,2,128,128]{3,2,1,0:T(8,128)}, f32[4,2,128,128]{3,2,1,0:T(8,128)}) custom-call(f32[2,4,2,128,128]{4,3,2,1,0:T(8,128)} %bitcast.40, f32[2,4,2,128,128]{4,3,2,1,0:T(8,128)} %bitcast.44), custom_call_target="tpu_custom_call" | custom-call | flops 1048576 | bytes 3145728 | tf_op jit(solution)/shard_map/sum_of/pallas_call | solution.py:404
  156.6 1.7 collective-permute-start.7
  158.3 1.6 collective-permute-start.14
  161.4 6.5 %collective-permute-done.12 = f32[4,2,128,128]{3,2,1,0:T(8,128)S(1)} collective-permute-done((f32[4,2,128,128]{3,2,1,0:T(8,128)}, f32[4,2,128,128]{3,2,1,0:T(8,128)S(1)}, u32[]{:S(2)}, u32[]{:S(2)}) %collective-permute-start.12) | collective-permute-done | bytes 524320 | tf_op jit(solution)/shard_map/ppermute | solution.py:456
  168.7 1.9 sum_of.20
  173.7 1.8 sum_of.18
  175.5 1.6 collective-permute-start.10
  178.9 1.9 sum_of.21
  180.8 2.6 %collective-permute-start.15 = (f32[2,2,128,128]{3,2,1,0:T(8,128)}, f32[2,2,128,128]{3,2,1,0:T(8,128)S(1)}, u32[]{:S(2)}, u32[]{:S(2)}) collective-permute-start(f32[2,2,128,128]{3,2,1,0:T(8,128)} %sum_of.21), channel_id=1, source_target_pairs={{0,4},{1,5},{2,6},{3,7},{4,0},{5,1},{6,2},{7,3},{8,12},{9,13},{10,... | collective-permute-start | bytes 786440 | tf_op jit(solution)/shard_map/ppermute | solution.py:456
  184.2 1.9 sum_of.17
  186.7 7.4 %collective-permute-done.15.refs_3_ = f32[2,2,128,128]{3,2,1,0:T(8,128)S(1)} collective-permute-done((f32[2,2,128,128]{3,2,1,0:T(8,128)}, f32[2,2,128,128]{3,2,1,0:T(8,128)S(1)}, u32[]{:S(2)}, u32[]{:S(2)}) %collective-permute-start.15) | collective-permute-done | bytes 262176 | tf_op jit(solution)/shard_map/ppermute | solution.py:456
  194.9 2.8 %power_of.1 = f32[2,128,128]{2,1,0:T(8,128)} custom-call(f32[2,2,128,128]{3,2,1,0:T(8,128)} %get-tuple-element.118.refs_0_, f32[2,2,128,128]{3,2,1,0:T(8,128)} %copy-done.16, f32[2,2,128,128]{3,2,1,0:T(8,128)} %copy-done.12, f32[2,2,128,128]{3,2,1,0:T(8,128)} %copy-done.14, f32[256,128]{1,0:T(8,128)} %constant.254.clone.refs_4_, ...), custom_call_target="tpu_custom_call" | custom-call | tf_op jit(solution)/shard_map/power_of/pallas_call | solution.py:438
  198.7 7.6 %all_to_all.18 = f32[2,128,128]{2,0,1:T(2,128)S(1)} all-to-all(f32[2,128,128]{2,0,1:T(2,128)S(1)} %copy.34), channel_id=1, replica_groups=mesh['wave'=4,'row'=8] {'wave'}, dimensions={1} | all-to-all | bytes 262144 | tf_op jit(solution)/shard_map/all_to_all | solution.py:584
  (72 shorter events, 23.7 us)
Async XLA Ops:
  0.0 10.3 %copy-start.17 = (s32[1,2]{1,0:T(1,128)S(1)}, s32[1,2]{1,0:T(1,128)}, u32[]{:S(2)}) copy-start(s32[1,2]{1,0:T(1,128)} %param.34) | copy-start | bytes 28
  0.0 10.9 %copy-start.18 = (s32[64,2]{0,1:T(2,128)S(1)}, s32[64,2]{0,1:T(2,128)}, u32[]{:S(2)}) copy-start(s32[64,2]{0,1:T(2,128)} %param.37) | copy-start | bytes 1540
  7.9 12.6 %collective-permute-start = (f32[2,256,1024]{2,1,0:T(8,128)}, f32[2,256,1024]{2,1,0:T(8,128)S(1)}, u32[]{:S(2)}, u32[]{:S(2)}) collective-permute-start(f32[2,256,1024]{2,1,0:T(8,128)} %get-tuple-element.68), channel_id=1, source_target_pairs={{0,1},{1,0},{2,3},{3,2},{4,5},{5,4},{6,7},{7,6},{8,9},{9,8},{10,11... | collective-permute-start | bytes 6291464 | tf_op jit(solution)/shard_map/ppermute | solution.py:456
  20.4 1.4 copy-start
  70.8 15.2 %collective-permute-start.1 = (f32[8,2,128,128]{3,2,1,0:T(8,128)}, f32[8,2,128,128]{3,2,1,0:T(8,128)S(1)}, u32[]{:S(2)}, u32[]{:S(2)}) collective-permute-start(f32[8,2,128,128]{3,2,1,0:T(8,128)} %get-tuple-element.82), channel_id=1, source_target_pairs={{0,1},{1,0},{2,3},{3,2},{4,5},{5,4},{6,7},{7,6},{8,9},{9,8},{10,11... | collective-permute-start | bytes 3145736 | tf_op jit(solution)/shard_map/ppermute | solution.py:456
  85.4 6.4 %collective-permute-start.3 = (f32[8,2,128,128]{3,2,1,0:T(8,128)}, f32[8,2,128,128]{3,2,1,0:T(8,128)S(1)}, u32[]{:S(2)}, u32[]{:S(2)}) collective-permute-start(f32[8,2,128,128]{3,2,1,0:T(8,128)} %get-tuple-element.96), channel_id=1, source_target_pairs={{0,1},{1,0},{2,3},{3,2},{4,5},{5,4},{6,7},{7,6},{8,9},{9,8},{10,11... | collective-permute-start | bytes 3145736 | tf_op jit(solution)/shard_map/ppermute | solution.py:456
  85.9 1.0 copy-start.4
  89.3 20.1 %collective-permute-start.2 = (f32[4,2,128,128]{3,2,1,0:T(8,128)}, f32[4,2,128,128]{3,2,1,0:T(8,128)S(1)}, u32[]{:S(2)}, u32[]{:S(2)}) collective-permute-start(f32[4,2,128,128]{3,2,1,0:T(8,128)} %get-tuple-element.90), channel_id=1, source_target_pairs={{0,8},{8,0},{16,24},{24,16},{1,9},{9,1},{17,25},{25,17},{2,10},{10... | collective-permute-start | bytes 1572872 | tf_op jit(solution)/shard_map/ppermute | solution.py:456
  91.8 1.0 copy-start.2
  95.2 18.5 %copy-start.19 = (f32[4,2,128,128]{3,2,1,0:T(8,128)S(1)}, f32[4,2,128,128]{3,2,1,0:T(8,128)}, u32[]{:S(2)}) copy-start(f32[4,2,128,128]{3,2,1,0:T(8,128)} %get-tuple-element.105) | copy-start | bytes 1572868
  109.4 0.8 copy-start.8
  112.1 16.7 %collective-permute-start.5 = (f32[2,2,128,128]{3,2,1,0:T(8,128)}, f32[2,2,128,128]{3,2,1,0:T(8,128)S(1)}, u32[]{:S(2)}, u32[]{:S(2)}) collective-permute-start(f32[2,2,128,128]{3,2,1,0:T(8,128)} %get-tuple-element.111), channel_id=1, source_target_pairs={{0,16},{8,24},{16,0},{24,8},{1,17},{9,25},{17,1},{25,9},{2,18},{10... | collective-permute-start | bytes 786440 | tf_op jit(solution)/shard_map/ppermute | solution.py:456
  113.7 18.4 %collective-permute-start.4 = (f32[4,2,128,128]{3,2,1,0:T(8,128)S(1)}, f32[4,2,128,128]{3,2,1,0:T(8,128)S(1)}, u32[]{:S(2)}, u32[]{:S(2)}) collective-permute-start(f32[4,2,128,128]{3,2,1,0:T(8,128)S(1)} %copy-done.19), channel_id=1, source_target_pairs={{0,16},{8,24},{16,0},{24,8},{1,17},{9,25},{17,1},{25,9},{2,18},{10... | collective-permute-start | bytes 1572872 | tf_op jit(solution)/shard_map/ppermute | solution.py:456
  128.9 20.6 %collective-permute-start.11 = (f32[8,2,128,128]{3,2,1,0:T(8,128)}, f32[8,2,128,128]{3,2,1,0:T(8,128)S(1)}, u32[]{:S(2)}, u32[]{:S(2)}) collective-permute-start(f32[8,2,128,128]{3,2,1,0:T(8,128)} %get-tuple-element.123), channel_id=1, source_target_pairs={{0,1},{1,0},{2,3},{3,2},{4,5},{5,4},{6,7},{7,6},{8,9},{9,8},{10,11... | collective-permute-start | bytes 3145736 | tf_op jit(solution)/shard_map/ppermute | solution.py:456
  132.0 0.8 copy-start.7
  149.4 8.9 %copy-start.9 = (f32[2,2,128,128]{3,2,1,0:T(8,128)S(1)}, f32[2,2,128,128]{3,2,1,0:T(8,128)}, u32[]{:S(2)}) copy-start(f32[2,2,128,128]{3,2,1,0:T(8,128)} %sum_of.15) | copy-start | bytes 786436
  149.4 10.5 %copy-start.20 = (f32[2,2,128,128]{3,2,1,0:T(8,128)S(1)}, f32[2,2,128,128]{3,2,1,0:T(8,128)}, u32[]{:S(2)}) copy-start(f32[2,2,128,128]{3,2,1,0:T(8,128)} %get-tuple-element.121) | copy-start | bytes 786436
  149.4 3.8 %collective-permute-start.6 = (f32[8,2,128,128]{3,2,1,0:T(8,128)}, f32[8,2,128,128]{3,2,1,0:T(8,128)S(1)}, u32[]{:S(2)}, u32[]{:S(2)}) collective-permute-start(f32[8,2,128,128]{3,2,1,0:T(8,128)} %get-tuple-element.115), channel_id=1, source_target_pairs={{0,1},{1,0},{2,3},{3,2},{4,5},{5,4},{6,7},{7,6},{8,9},{9,8},{10,11... | collective-permute-start | bytes 3145736 | tf_op jit(solution)/shard_map/ppermute | solution.py:456
  149.5 1.0 copy-start.1
  152.9 15.0 %collective-permute-start.12 = (f32[4,2,128,128]{3,2,1,0:T(8,128)}, f32[4,2,128,128]{3,2,1,0:T(8,128)S(1)}, u32[]{:S(2)}, u32[]{:S(2)}) collective-permute-start(f32[4,2,128,128]{3,2,1,0:T(8,128)} %get-tuple-element.125), channel_id=1, source_target_pairs={{0,8},{8,0},{16,24},{24,16},{1,9},{9,1},{17,25},{25,17},{2,10},{10... | collective-permute-start | bytes 1572872 | tf_op jit(solution)/shard_map/ppermute | solution.py:456
  153.2 1.0 copy-start.3
  156.6 26.8 %collective-permute-start.7 = (f32[4,2,128,128]{3,2,1,0:T(8,128)}, f32[4,2,128,128]{3,2,1,0:T(8,128)S(1)}, u32[]{:S(2)}, u32[]{:S(2)}) collective-permute-start(f32[4,2,128,128]{3,2,1,0:T(8,128)} %get-tuple-element.117), channel_id=1, source_target_pairs={{0,16},{8,24},{16,0},{24,8},{1,17},{9,25},{17,1},{25,9},{2,18},{10... | collective-permute-start | bytes 1572872 | tf_op jit(solution)/shard_map/ppermute | solution.py:456
  158.3 18.8 %collective-permute-start.14 = (f32[2,2,128,128]{3,2,1,0:T(8,128)S(1)}, f32[2,2,128,128]{3,2,1,0:T(8,128)S(1)}, u32[]{:S(2)}, u32[]{:S(2)}) collective-permute-start(f32[2,2,128,128]{3,2,1,0:T(8,128)S(1)} %copy-done.9), channel_id=1, source_target_pairs={{0,2},{1,3},{2,0},{3,1},{4,6},{5,7},{6,4},{7,5},{8,10},{9,11},{10,... | collective-permute-start | bytes 786440 | tf_op jit(solution)/shard_map/ppermute | solution.py:456
  159.9 13.1 %collective-permute-start.9 = (f32[2,2,128,128]{3,2,1,0:T(8,128)S(1)}, f32[2,2,128,128]{3,2,1,0:T(8,128)S(1)}, u32[]{:S(2)}, u32[]{:S(2)}) collective-permute-start(f32[2,2,128,128]{3,2,1,0:T(8,128)S(1)} %copy-done.20), channel_id=1, source_target_pairs={{0,8},{8,0},{16,24},{24,16},{1,9},{9,1},{17,25},{25,17},{2,10},{10... | collective-permute-start | bytes 786440 | tf_op jit(solution)/shard_map/ppermute | solution.py:456
  167.9 0.8 copy-start.6
  170.6 7.6 %collective-permute-start.13 = (f32[2,2,128,128]{3,2,1,0:T(8,128)}, f32[2,2,128,128]{3,2,1,0:T(8,128)S(1)}, u32[]{:S(2)}, u32[]{:S(2)}) collective-permute-start(f32[2,2,128,128]{3,2,1,0:T(8,128)} %get-tuple-element.127), channel_id=1, source_target_pairs={{0,16},{8,24},{16,0},{24,8},{1,17},{9,25},{17,1},{25,9},{2,18},{10... | collective-permute-start | bytes 786440 | tf_op jit(solution)/shard_map/ppermute | solution.py:456
  175.5 11.2 %collective-permute-start.10 = (f32[2,2,128,128]{3,2,1,0:T(8,128)}, f32[2,2,128,128]{3,2,1,0:T(8,128)S(1)}, u32[]{:S(2)}, u32[]{:S(2)}) collective-permute-start(f32[2,2,128,128]{3,2,1,0:T(8,128)} %sum_of.18), channel_id=1, source_target_pairs={{0,2},{1,3},{2,0},{3,1},{4,6},{5,7},{6,4},{7,5},{8,10},{9,11},{10,... | collective-permute-start | bytes 786440 | tf_op jit(solution)/shard_map/ppermute | solution.py:456
  177.1 1.1 copy-start.13
  180.8 13.3 %collective-permute-start.15 = (f32[2,2,128,128]{3,2,1,0:T(8,128)}, f32[2,2,128,128]{3,2,1,0:T(8,128)S(1)}, u32[]{:S(2)}, u32[]{:S(2)}) collective-permute-start(f32[2,2,128,128]{3,2,1,0:T(8,128)} %sum_of.21), channel_id=1, source_target_pairs={{0,4},{1,5},{2,6},{3,7},{4,0},{5,1},{6,2},{7,3},{8,12},{9,13},{10,... | collective-permute-start | bytes 786440 | tf_op jit(solution)/shard_map/ppermute | solution.py:456
  183.4 0.8 copy-start.5
  186.1 8.0 %collective-permute-start.8 = (f32[2,2,128,128]{3,2,1,0:T(8,128)}, f32[2,2,128,128]{3,2,1,0:T(8,128)S(1)}, u32[]{:S(2)}, u32[]{:S(2)}) collective-permute-start(f32[2,2,128,128]{3,2,1,0:T(8,128)} %get-tuple-element.119), channel_id=1, source_target_pairs={{0,8},{8,0},{16,24},{24,16},{1,9},{9,1},{17,25},{25,17},{2,10},{10... | collective-permute-start | bytes 786440 | tf_op jit(solution)/shard_map/ppermute | solution.py:456
  186.7 7.5 %copy-start.12 = (f32[2,2,128,128]{3,2,1,0:T(8,128)}, f32[2,2,128,128]{3,2,1,0:T(8,128)S(1)}, u32[]{:S(2)}) copy-start(f32[2,2,128,128]{3,2,1,0:T(8,128)S(1)} %collective-permute-done.10.refs_2_) | copy-start | bytes 786436
  (5 other events, 3.6 us)

commit v3 on v2

--- a/solution.py
+++ b/solution.py
@@ -229,52 +229,170 @@
     )(parity, mine, theirs, *table, jnp.asarray(down), jnp.asarray(along))
 
 
-def row_inverse_kernel(spec_hi, spec_lo, table_hi, table_lo, out_hi, out_lo):
-    count = table_hi.shape[0]
-
-    def blocks(depth):
+def cut_slots(layout, info_ref, slot_ref, pos_ref, re_ref, im_ref, sign_ref, field, outs):
+    chip_rows, waves, own, _ = layout
+    height = chip_rows + WINDOW
+    lane = lax.broadcasted_iota(jnp.int32, (WINDOW, WINDOW), 1)
+    row_rank, wave_rank = info_ref[0], info_ref[1]
+
+    def one(index, out_ref, place):
+        target = row_rank ^ slot_ref[0, index]
+        probe = (target * waves + (wave_rank ^ slot_ref[1, index])) * own + slot_ref[2, index]
+        row = slot_ref[3, index] * height + lax.rem(pos_ref[0, probe], chip_rows)
+        start = lax.rem(pos_ref[1, probe] + (GRID - HALF), GRID)
+        col = lax.rem(start, FOLD)
+        turned = jnp.where(start >= FOLD, sign_ref[0], 1.0)
+        shift = lax.rem(col, LANES)
+        back = lax.rem(LANES - shift, LANES)
+
+        def cut(part):
+            sides = [
+                pltpu.roll(field[part, col // LANES + side, pl.ds(row, WINDOW)], back, 1)
+                for side in (0, 1)
+            ]
+            return jnp.where(lane < LANES - shift, sides[0], sides[1])
+
+        real_part, imag_part = cut(0), cut(1)
+        weight_re, weight_im = re_ref[probe] * turned, im_ref[probe] * turned
+        out_ref[place, 0] = weight_re * real_part - weight_im * imag_part
+        out_ref[place, 1] = weight_re * imag_part + weight_im * real_part
+
+    keep_ref, send_ref = outs
+    count = keep_ref.shape[0]
+
+    @pl.loop(0, count)
+    def _(place):
+        one(count + place, send_ref, place)
+        one(place, keep_ref, place)
+
+
+def inverse_kernel(
+    layout, cuts, info_ref, slot_ref, pos_ref, re_ref, im_ref, sign_ref,
+    spec_hi, spec_lo, row_hi, row_lo, col_hi, col_lo, *refs,
+):
+    chip_rows, _, _, segments = layout
+    height = chip_rows + WINDOW
+    refs = list(refs)
+    outs = refs[:2]
+    exports = refs[2:4] if len(refs) > 5 else None
+    rows, field = refs[-3:-1], refs[-1]
+    step = pl.program_id(0)
+    first = 2 * BLOCKS
+    last = first + 2 * cuts * COL_TILES
+
+    def row_part(depth):
+        part = step // BLOCKS
+        place = pl.multiple_of(step % BLOCKS * PAIR, PAIR)
+        cols = pl.ds(place, PAIR)
+        count = row_hi.shape[0]
         sums = []
         for parity in (0, 1):
-            part = slice(parity * DEPTH, parity * DEPTH + depth * PAIR)
+            freq = slice(parity * DEPTH, parity * DEPTH + depth * PAIR)
             sums.append(
-                dot3((table_hi[:, part], table_lo[:, part]), (spec_hi[0, part], spec_lo[0, part]))
+                dot3((row_hi[:, freq], row_lo[:, freq]), (spec_hi[0, freq], spec_lo[0, freq]))
             )
-        outs = (out_hi, out_lo)
-        put(outs, (0, slice(0, count)), sums[0] + sums[1])
-        put(outs, (0, slice(count, 2 * count)), sums[0] - sums[1])
-
-    last = pl.program_id(0) % BLOCKS == BLOCKS - 1
-    pl.when(last)(functools.partial(blocks, BLOCKS - 1))
-    pl.when(jnp.logical_not(last))(functools.partial(blocks, BLOCKS))
-
-
-def row_inverse(spectrum, rows):
-    count = len(rows)
-    table = table_halves(paired(cos_sin(rows, np.concatenate([freqs(0), freqs(1)]))))
-    out = jax.ShapeDtypeStruct((2, 2 * count, DEPTH), jnp.bfloat16)
-    tile = pl.BlockSpec((1, 2 * count, PAIR), lambda j: (j // BLOCKS, 0, j % BLOCKS))
-    spec = pl.BlockSpec((1, 2 * DEPTH, PAIR), lambda j: (j // BLOCKS, 0, j % BLOCKS))
-    table_spec = pl.BlockSpec((count, 2 * DEPTH), lambda j: (0, 0))
+        put(rows, (part, slice(0, count), cols), sums[0] + sums[1])
+        put(rows, (part, slice(count, 2 * count), cols), sums[0] - sums[1])
+        if exports is not None:
+            for index in range(segments):
+                start = pl.multiple_of(info_ref[3 + cuts + index] * height, LANES)
+                for export, source in zip(exports, rows):
+                    export[0, index * height : (index + 1) * height] = source[
+                        part, pl.ds(start, height), cols
+                    ]
+
+    zero_blocks = step % BLOCKS == BLOCKS - 1
+    pl.when((step < first) & zero_blocks)(functools.partial(row_part, BLOCKS - 1))
+    pl.when((step < first) & jnp.logical_not(zero_blocks))(functools.partial(row_part, BLOCKS))
+
+    @pl.when((step >= first) & (step < last))
+    def _():
+        now = step - first
+        tile = now % COL_TILES
+        part = now // COL_TILES % 2
+        segment = now // (2 * COL_TILES)
+        source = pl.ds(pl.multiple_of(info_ref[3 + segment] * height, LANES), height)
+        place = pl.ds(pl.multiple_of(segment * height, LANES), height)
+        value = dot3((rows[0][part, source], rows[1][part, source]), (col_hi[0], col_lo[0]))
+        field[part, 2 * tile, place] = value[:, :LANES]
+        field[part, 2 * tile + 1, place] = value[:, LANES:]
+
+        @pl.when(tile == 0)
+        def _():
+            field[part, 2 * COL_TILES, place] = value[:, :LANES] * sign_ref[0]
+
+    @pl.when(step == last)
+    def _():
+        cut_slots(
+            layout, info_ref, slot_ref, pos_ref, re_ref, im_ref, sign_ref, field, outs
+        )
+
+
+def column_table():
+    return table_halves(both(lambda freq: paired(cos_sin(np.arange(FOLD), freq)).T))
+
+
+def inverse(layout, cuts, export, spectrum, row_list, slots, info, positions, weights, sign):
+    chip_rows, _, _, segments = layout
+    height = chip_rows + WINDOW
+    count = slots.shape[1] // 2
+    tall = len(row_list)
+    row_table = table_halves(paired(cos_sin(row_list, np.concatenate([freqs(0), freqs(1)]))))
+    first = 2 * BLOCKS
+    last = first + 2 * cuts * COL_TILES
+
+    def spec_map(i, *_):
+        i = jnp.minimum(i, first - 1)
+        return i // BLOCKS, 0, i % BLOCKS
+
+    def col_map(i, info, *_):
+        return info[2], 0, (jnp.clip(i, first, last - 1) - first) % COL_TILES
+
+    spec = pl.BlockSpec((1, 2 * DEPTH, PAIR), spec_map)
+    row_spec = pl.BlockSpec(
+        (tall, 2 * DEPTH), lambda i, *_: (0, 0), pipeline_mode=pl.Buffered(1)
+    )
+    col_spec = pl.BlockSpec((1, DEPTH, PAIR), col_map)
+    shapes = [jax.ShapeDtypeStruct((count, 2, WINDOW, WINDOW), jnp.float32)] * 2
+    specs = [
+        pl.BlockSpec(
+            (count, 2, WINDOW, WINDOW), lambda i, *_: (0, 0, 0, 0), pipeline_mode=pl.Buffered(1)
+        )
+    ] * 2
+    if export:
+        shapes += [jax.ShapeDtypeStruct((2, segments * height, DEPTH), jnp.bfloat16)] * 2
+        specs += [pl.BlockSpec((1, segments * height, PAIR), spec_map)] * 2
     return pl.pallas_call(
-        row_inverse_kernel,
-        out_shape=(out, out),
-        grid=(2 * BLOCKS,),
-        in_specs=[spec, spec, table_spec, table_spec],
-        out_specs=(tile, tile),
+        functools.partial(inverse_kernel, layout, cuts),
+        out_shape=shapes,
+        grid_spec=pltpu.PrefetchScalarGridSpec(
+            num_scalar_prefetch=6,
+            grid=(last + 1,),
+            in_specs=[spec, spec, row_spec, row_spec, col_spec, col_spec],
+            out_specs=specs,
+            scratch_shapes=[
+                pltpu.VMEM((2, 2 * tall, DEPTH), jnp.bfloat16),
+                pltpu.VMEM((2, 2 * tall, DEPTH), jnp.bfloat16),
+                pltpu.VMEM((2, 2 * COL_TILES + 1, cuts * height, WINDOW), jnp.float32),
+            ],
+        ),
         cost_estimate=pl.CostEstimate(
-            flops=24 * count * DEPTH * DEPTH,
-            bytes_accessed=16 * DEPTH * DEPTH + 16 * count * DEPTH,
+            flops=24 * tall * DEPTH * DEPTH + 12 * cuts * height * DEPTH * FOLD,
+            bytes_accessed=16 * DEPTH * DEPTH + 16 * tall * DEPTH,
             transcendentals=0,
         ),
-        name="row_inverse",
-    )(*spectrum, *table)
+        name="inverse",
+    )(
+        info, jnp.asarray(slots), positions, *weights, sign, *spectrum, *row_table,
+        *column_table(),
+    )
 
 
 def column_inverse_kernel(
     layout, info_ref, slot_ref, pos_ref, re_ref, im_ref, sign_ref,
     rows_hi, rows_lo, table_hi, table_lo, keep_ref, send_ref, field,
 ):
-    chip_rows, waves, own, segments = layout
+    chip_rows, _, _, segments = layout
     height = chip_rows + WINDOW
     step = pl.program_id(0)
     tile = step % COL_TILES
@@ -294,51 +412,22 @@
 
     @pl.when(step == 2 * segments * COL_TILES)
     def _():
-        lane = lax.broadcasted_iota(jnp.int32, (WINDOW, WINDOW), 1)
-        row_rank, wave_rank = info_ref[0], info_ref[1]
-
-        def one(index, out_ref, place):
-            target = row_rank ^ slot_ref[0, index]
-            probe = (target * waves + (wave_rank ^ slot_ref[1, index])) * own + slot_ref[2, index]
-            row = slot_ref[3, index] * height + lax.rem(pos_ref[0, probe], chip_rows)
-            start = lax.rem(pos_ref[1, probe] + (GRID - HALF), GRID)
-            col = lax.rem(start, FOLD)
-            turned = jnp.where(start >= FOLD, sign_ref[0], 1.0)
-            shift = lax.rem(col, LANES)
-            back = lax.rem(LANES - shift, LANES)
-
-            def cut(part):
-                sides = [
-                    pltpu.roll(field[part, col // LANES + side, pl.ds(row, WINDOW)], back, 1)
-                    for side in (0, 1)
-                ]
-                return jnp.where(lane < LANES - shift, sides[0], sides[1])
-
-            real_part, imag_part = cut(0), cut(1)
-            weight_re, weight_im = re_ref[probe] * turned, im_ref[probe] * turned
-            out_ref[place, 0] = weight_re * real_part - weight_im * imag_part
-            out_ref[place, 1] = weight_re * imag_part + weight_im * real_part
-
-        count = keep_ref.shape[0]
-
-        @pl.loop(0, count)
-        def _(place):
-            one(count + place, send_ref, place)
-            one(place, keep_ref, place)
+        cut_slots(
+            layout, info_ref, slot_ref, pos_ref, re_ref, im_ref, sign_ref, field,
+            (keep_ref, send_ref),
+        )
 
 
 def column_inverse(layout, rows, slots, info, positions, weights, sign):
     chip_rows, _, _, segments = layout
     count = slots.shape[1] // 2
     height = chip_rows + WINDOW
-    table = table_halves(
-        both(lambda freq: paired(cos_sin(np.arange(FOLD), freq)).T)
-    )
+    table = column_table()
     last = 2 * segments * COL_TILES - 1
 
     def rows_map(i, info, *_):
         i = jnp.minimum(i, last)
-        return i // COL_TILES % 2, info[3 + i // (2 * COL_TILES)], 0
+        return i // COL_TILES % 2, i // (2 * COL_TILES), 0
 
     rows_spec = pl.BlockSpec((1, height, DEPTH), rows_map)
     table_spec = pl.BlockSpec(
@@ -376,43 +465,48 @@
     )
 
 
-def sum_kernel(count, *refs):
-    total = refs[0][...]
+def sum_kernel(count, halve, *refs):
+    total = refs[0][0]
     for ref in refs[1:count]:
-        total += ref[...]
-    if len(refs) == count + 1:
-        refs[count][...] = total
-    else:
+        total += ref[0]
+    if halve:
         refs[count][...] = total[0]
         refs[count + 1][...] = total[1]
+    else:
+        refs[count][...] = total
 
 
 def sum_of(terms, halve):
-    count, tail = terms[0].shape[0], terms[0].shape[1:]
+    tail = terms[0][0].shape[1:]
     zeros = (0,) * len(tail)
-    if halve:
-        count //= 2
-        terms = [term.reshape((2, count) + tail) for term in terms]
-        step = max(1, count // 2)
-        in_spec = pl.BlockSpec((2, step) + tail, lambda i: (0, i) + zeros)
-    else:
-        step = max(1, count // 2)
-        in_spec = pl.BlockSpec((step,) + tail, lambda i: (i,) + zeros)
+    count = terms[0][0].shape[0] // terms[0][2] // (2 if halve else 1)
+    step = max(1, count // 2)
+    specs, arrays = [], []
+    for array, part, parts in terms:
+        if halve:
+            arrays.append(array.reshape((parts, 2, count) + tail))
+            specs.append(
+                pl.BlockSpec((1, 2, step) + tail, lambda i, part=part: (part, 0, i) + zeros)
+            )
+        else:
+            arrays.append(array.reshape((parts, count) + tail))
+            specs.append(
+                pl.BlockSpec((1, step) + tail, lambda i, part=part: (part, i) + zeros)
+            )
     out = jax.ShapeDtypeStruct((count,) + tail, jnp.float32)
     out_spec = pl.BlockSpec((step,) + tail, lambda i: (i,) + zeros)
     size = count * 4 * math.prod(tail) * (2 if halve else 1)
-    result = pl.pallas_call(
-        functools.partial(sum_kernel, len(terms)),
+    return pl.pallas_call(
+        functools.partial(sum_kernel, len(terms), halve),
         out_shape=(out, out) if halve else out,
         grid=(count // step,),
-        in_specs=[in_spec] * len(terms),
+        in_specs=specs,
         out_specs=(out_spec, out_spec) if halve else out_spec,
         cost_estimate=pl.CostEstimate(
             flops=size, bytes_accessed=(len(terms) + 1) * size, transcendentals=0
         ),
         name="sum_of",
-    )(*terms)
-    return result
+    )(*arrays)
 
 
 def power_kernel(count, scale, *refs):
@@ -483,25 +577,28 @@
     segments = far // 2
     layout = (chip_rows, wave_count, own, segments)
 
-    def slots_of(odd, half):
+    def slots_of(odd, halves):
         slots = []
         for core_bit in (0, 1):
-            for digits in range(wave_count):
-                wave = 0
-                for place, bit in enumerate(orders[half]):
-                    wave |= (digits >> (wave_bits - 1 - place) & 1) << bit
-                for index in range(segments):
-                    row = ((half * segments + index) * 2 + odd) * 2 + core_bit
-                    slots += [(row, wave, probe, index) for probe in range(own)]
+            for at, half in enumerate(halves):
+                for digits in range(wave_count):
+                    wave = 0
+                    for place, bit in enumerate(orders[half]):
+                        wave |= (digits >> (wave_bits - 1 - place) & 1) << bit
+                    for index in range(segments):
+                        row = ((half * segments + index) * 2 + odd) * 2 + core_bit
+                        where = at * segments + index
+                        slots += [(row, wave, probe, where) for probe in range(own)]
         return np.array(slots, np.int32).T
 
-    def info_of(odd, half):
+    def info_of(odd, halves):
         chip = row_rank // 2
         info = [row_rank, wave_rank, core]
-        for index in range(segments):
-            target = chip ^ ((half * segments + index) * 2 + odd)
-            away = (target - chip) % chips
-            info.append(away // far * segments + away % far // 2)
+        for half in halves:
+            for index in range(segments):
+                target = chip ^ ((half * segments + index) * 2 + odd)
+                away = (target - chip) % chips
+                info.append(away // far * segments + away % far // 2)
         return jnp.stack(info)
 
     def rows_of(odd):
@@ -512,72 +609,56 @@
             ]
         )
 
-    def cut(odd, half, rows):
-        keep, send = column_inverse(
-            layout, rows, slots_of(odd, half), info_of(odd, half), positions, weights, sign
-        )
-        return keep, flip(send, "row", 1)
-
-    def wave_stage(half, place, terms):
-        stay, send = sum_of(terms, True)
-        return stay, flip(send, "wave", 1 << orders[half][place])
-
     def later(value, *before):
         return lax.optimization_barrier((value,) + before)
 
     upper, lower = 1, 0
-    rows_odd = row_inverse(spectrum, rows_of(1))
-    odd_upper = cut(1, upper, rows_odd)
-    rows_odd, keep = later(rows_odd, odd_upper[0])
-    odd_upper = (keep, odd_upper[1])
-    odd_lower = cut(1, lower, rows_odd)
-
-    stages = {(1, upper): [odd_upper, 0], (1, lower): [odd_lower, 0]}
+    common = (positions, weights, sign)
+    stages = {}
 
     def advance(value, *keys):
         for key in keys:
             terms, place = stages[key]
-            if place == wave_bits:
-                continue
             stay, send = sum_of(terms, True)
-            value, stay, send = later(value, stay, send)
-            stages[key] = [
-                (stay, flip(send, "wave", 1 << orders[key[1]][place])), place + 1
-            ]
+            if value is not None:
+                value, stay, send = later(value, stay, send)
+            arrived = flip(send, "wave", 1 << orders[key[1]][place])
+            stages[key] = [[(stay, 0, 1), (arrived, 0, 1)], place + 1]
         return value
-
-    spectrum = later(spectrum, odd_lower[0])
-    spectrum, keep = spectrum
-    stages[1, lower] = [(keep, odd_lower[1]), 0]
-    spectrum = advance(spectrum, (1, upper))
-    rows_even = row_inverse(spectrum, rows_of(0))
-    rows_even = advance(rows_even, (1, upper), (1, lower))
-    even_upper = cut(0, upper, rows_even)
-    rows_even, keep = later(rows_even, even_upper[0])
-    stages[0, upper] = [(keep, even_upper[1]), 0]
-    rows_even = advance(rows_even, (1, lower))
-    near_upper = None
-    if stages[1, upper][1] == wave_bits:
-        total = sum_of(stages[1, upper][0], False)
-        rows_even, total = later(rows_even, total)
-        near_upper = flip(total, "row", 2)
-    stages[0, lower] = [cut(0, lower, rows_even), 0]
 
     def finish(key):
         while stages[key][1] < wave_bits:
-            terms, place = stages[key]
-            stages[key] = [wave_stage(key[1], place, terms), place + 1]
-        return list(stages[key][0])
-
-    if near_upper is None:
-        near_upper = flip(sum_of(finish((1, upper)), False), "row", 2)
+            advance(None, key)
+        return stages[key][0]
+
+    keep, send = inverse(
+        layout, 2 * segments, False, spectrum, rows_of(1), slots_of(1, (upper, lower)),
+        info_of(1, (upper, lower)), *common,
+    )
+    arrived = flip(send, "row", 1)
+    for at, half in enumerate((upper, lower)):
+        stages[1, half] = [[(keep, at, 2), (arrived, at, 2)], 0]
+    spectrum = later(spectrum, send)[0]
+    keep, send, rows_hi, rows_lo = inverse(
+        layout, segments, True, spectrum, rows_of(0), slots_of(0, (upper,)),
+        info_of(0, (upper, lower)), *common,
+    )
+    stages[0, upper] = [[(keep, 0, 1), (flip(send, "row", 1), 0, 1)], 0]
+    rows = (rows_hi, rows_lo)
+    rows = advance(rows, (1, upper), (1, lower))
+    keep, send = column_inverse(
+        layout, rows, slots_of(0, (lower,)), info_of(0, (lower,)), *common
+    )
+    stages[0, lower] = [[(keep, 0, 1), (flip(send, "row", 1), 0, 1)], 0]
+
+    near_upper = flip(sum_of(finish((1, upper)), False), "row", 2)
     near_lower = flip(sum_of(finish((1, lower)), False), "row", 2)
     bit = row_count // 2
-    send = sum_of(finish((0, upper)) + [near_upper], False)
-    terms = finish((0, lower)) + [near_lower, flip(send, "row", bit)]
+    send = sum_of(finish((0, upper)) + [(near_upper, 0, 1)], False)
+    terms = [term[0] for term in finish((0, lower))] + [near_lower, flip(send, "row", bit)]
     while bit > 4:
         bit //= 2
-        stay, send = sum_of(terms, True)
+        stay, send = sum_of([(term, 0, 1) for term in terms], True)
         terms = [stay, flip(send, "row", bit)]
     total_waves = plane_waves.shape[1] * wave_count
     power = power_of(terms, 1.0 / (WINDOW * WINDOW * total_waves))

time: 209 us -> 202 us (0.967)
  Pallas kernels: 147 us -> 138 us
  waiting for transfers between devices: 16.7 us -> 19.7 us
    pallas_call x4 -> x1, Pallas kernels: 58.9 us -> 14.8 us  [column_inverse(): pl.pallas_call(functools.partial(column_inverse_kernel, layout), out_shap...]
    pallas_call x13, Pallas kernels: 50.9 us -> 85.8 us  [the longest x2 63.1 us: inverse(): pl.pallas_call(functools.partial(inverse_kernel, layout, cuts), out_shape...]
    ppermute x16 -> x15, waiting for transfers between devices: 16.7 us -> 19.7 us  [flip(): return lax.ppermute(block, axis, [(i, i ^ bit) for i in range(count)])]
    unnamed x42 -> x34, local copies, waits for them, and re-layouts: 11.4 us -> 9.99 us
    ppermute x16 -> x15, starting transfers between devices: 16.9 us -> 17.3 us  [flip(): return lax.ppermute(block, axis, [(i, i ^ bit) for i in range(count)])]
  transfers between devices with their start and end apart: 16 -> 15, of which waited for: 5 -> 6; matrix products, arithmetic and copies ran while one was open for 2% -> 3% of each run, Pallas kernels for 41% -> 35%
where the time goes in v3:
time: 202 us; the launch traced here: 201 us
  Pallas kernels  138 us (68%)
  waiting for transfers between devices  19.7 us (10%)
  starting transfers between devices  17.3 us (9%)
  local copies, waits for them, and re-layouts  13.7 us (7%)
  blocking collectives  7.72 us (4%)
  other arithmetic  3.11 us (2%)
    pallas_call x2, Pallas kernels, inverse(): pl.pallas_call(functools.partial(inverse_kernel, layout, cuts), out_shape...  63.1 us
    pallas_call x11, Pallas kernels, sum_of(): pl.pallas_call(functools.partial(sum_kernel, len(terms), halve), out_shap...  22.7 us
    ppermute x15, waiting for transfers between devices, flip(): return lax.ppermute(block, axis, [(i, i ^ bit) for i in range(count)])  19.7 us
    ppermute x15, starting transfers between devices, flip(): return lax.ppermute(block, axis, [(i, i ^ bit) for i in range(count)])  17.3 us
    pallas_call x1, Pallas kernels, column_inverse(): pl.pallas_call(functools.partial(column_inverse_kernel, layout), out_shap...  14.8 us
    pallas_call x1, Pallas kernels, row_forward(): pl.pallas_call(row_forward_kernel, out_shape=(out, out), grid_spec=pltpu....  13.7 us
    pallas_call x2, Pallas kernels, column_forward(): pl.pallas_call(column_forward_kernel, out_shape=jax.ShapeDtypeStruct((2,...  12.8 us
    unnamed x34, local copies, waits for them, and re-layouts  9.99 us
  transfers between devices with their start and end apart: 15, of which 6 were waited for; matrix products, arithmetic and copies ran while one was open for 3% of the time, Pallas kernels for 35%

profile of v3, /device:TPU:0, one launch (start us, length us, event | category | flops | bytes accessed | tf_op | source)
XLA Modules:
  0.0 200.7 jit_solution(7556286954653201703)
XLA Ops:
  0.0 7.9 %split_columns.1 = (f32[2,256,1024]{2,1,0:T(8,128)}, f32[2,256,1024]{2,1,0:T(8,128)}) custom-call(f32[1]{0:T(128)} %bitcast.9.sign_ref, f32[2,1,256,2048]{3,2,1,0:T(8,128)} %wave_ref.1, f32[1,2,256,2048]{3,2,1,0:T(8,128)} %trans_ref.1), custom_call_target="tpu_custom_call" | custom-call | flops 10485760 | bytes 12582912 | tf_op jit(solution)/shard_map/split_columns/pallas_call | solution.py:91
  11.0 2.0 sine_multiply_fusion
  13.5 6.4 %column_forward.2.mine_ref = f32[2,256,768]{2,1,0:T(8,128)} custom-call(s32[1]{0:T(128)} %bitcast.2.parity_ref, f32[2,256,1024]{2,1,0:T(8,128)} %get-tuple-element.45.field_ref, bf16[2,1024,768]{2,1,0:T(8,128)(2,1)} %constant.242.clone.table_hi, bf16[2,1024,768]{2,1,0:T(8,128)(2,1)} %constant.243.clone.table_lo), custom_call_target="tpu_custom_call" | custom-call | flops 2415919104 | bytes 3670016 | tf_op jit(solution)/shard_map/column_forward/pallas_call | solution.py:127
  21.3 6.4 %column_forward.3.theirs_ref = f32[2,256,768]{2,1,0:T(8,128)} custom-call(s32[1]{0:T(128)} %bitcast.2.parity_ref, f32[2,256,1024]{2,1,0:T(8,128)} %copy-done.1, bf16[2,1024,768]{2,1,0:T(8,128)(2,1)} %constant.242.clone.table_hi, bf16[2,1024,768]{2,1,0:T(8,128)(2,1)} %constant.243.clone.table_lo), custom_call_target="tpu_custom_call" | custom-call | flops 2415919104 | bytes 3670016 | tf_op jit(solution)/shard_map/column_forward/pallas_call | solution.py:127
  27.7 13.7 %row_forward.1 = (bf16[2,1536,768]{2,1,0:T(8,128)(2,1)}, bf16[2,1536,768]{2,1,0:T(8,128)(2,1)}) custom-call(s32[1]{0:T(128)} %bitcast.2.parity_ref, f32[2,256,768]{2,1,0:T(8,128)} %column_forward.2.mine_ref, f32[2,256,768]{2,1,0:T(8,128)} %column_forward.3.theirs_ref, bf16[1536,512]{1,0:T(8,128)(2,1)} %constant.244.clone.table_hi, ...), custom_call_target="tpu_custom_call" | custom-call | flops 7247757312 | bytes 12582912 | tf_op jit(solution)/shard_map/row_forward/pallas_call | solution.py:206
  41.4 36.7 %inverse.2 = (f32[16,2,128,128]{3,2,1,0:T(8,128)}, f32[16,2,128,128]{3,2,1,0:T(8,128)}) custom-call(s32[5]{0:T(128)} %stack.43.info_ref, s32[4,32]{1,0:T(4,128)} %constant.250.clone.slot_ref, s32[2,64]{1,0:T(2,128)} %bitcast.66, f32[64]{0:T(128)} %cosine_multiply_fusion.re_ref, f32[64]{0:T(128)} %get-tuple-element.85.im_ref, f32[1]{0:T(128)} %bitcast.9.sign_ref, ...), custom_call_target="tpu_custom_call" | custom-call | flops 21139292160 | bytes 17301504 | tf_op jit(solution)/shard_map/inverse/pallas_call | solution.py:365
  79.4 26.4 %inverse.3 = (f32[8,2,128,128]{3,2,1,0:T(8,128)}, f32[8,2,128,128]{3,2,1,0:T(8,128)}, bf16[2,640,768]{2,1,0:T(8,128)(2,1)}, bf16[2,640,768]{2,1,0:T(8,128)(2,1)}) custom-call(s32[5]{0:T(128)} %stack.40.info_ref, s32[4,16]{1,0:T(4,128)} %constant.255.clone.slot_ref, s32[2,64]{1,0:T(2,128)} %bitcast.67, f32[64]{0:T(128)} %cosine_multiply_fusion.re_ref, ...), custom_call_target="tpu_custom_call" | custom-call | flops 15099494400 | bytes 17301504 | tf_op jit(solution)/shard_map/inverse/pallas_call | solution.py:365
  107.7 2.4 %sum_of.12 = (f32[4,2,128,128]{3,2,1,0:T(8,128)}, f32[4,2,128,128]{3,2,1,0:T(8,128)}) custom-call(f32[2,2,4,2,128,128]{5,4,3,2,1,0:T(8,128)} %bitcast.43, f32[2,2,4,2,128,128]{5,4,3,2,1,0:T(8,128)} %bitcast.45), custom_call_target="tpu_custom_call" | custom-call | flops 1048576 | bytes 3145728 | tf_op jit(solution)/shard_map/sum_of/pallas_call | solution.py:499
  110.1 2.4 %sum_of.11 = (f32[4,2,128,128]{3,2,1,0:T(8,128)}, f32[4,2,128,128]{3,2,1,0:T(8,128)}) custom-call(f32[2,2,4,2,128,128]{5,4,3,2,1,0:T(8,128)} %bitcast.44, f32[2,2,4,2,128,128]{5,4,3,2,1,0:T(8,128)} %bitcast.46), custom_call_target="tpu_custom_call" | custom-call | flops 1048576 | bytes 3145728 | tf_op jit(solution)/shard_map/sum_of/pallas_call | solution.py:499
  112.5 14.8 %column_inverse.1 = (f32[8,2,128,128]{3,2,1,0:T(8,128)}, f32[8,2,128,128]{3,2,1,0:T(8,128)}) custom-call(s32[4]{0:T(128)} %pad_add_fusion.info_ref, s32[4,16]{1,0:T(4,128)} %constant.256.clone.slot_ref, s32[2,64]{1,0:T(2,128)} %bitcast.68, f32[64]{0:T(128)} %cosine_multiply_fusion.re_ref, f32[64]{0:T(128)} %get-tuple-element.85.im_ref, f32[1]{0:T(128)} %bitcast.9.sign_ref, ...), custom_call_target="tpu_custom_call" | custom-call | flops 6039797760 | bytes 6029312 | tf_op jit(solution)/shard_map/column_inverse/pallas_call | solution.py:440
  127.3 2.9 %collective-permute-start.11 = (f32[4,2,128,128]{3,2,1,0:T(8,128)S(1)}, f32[4,2,128,128]{3,2,1,0:T(8,128)}, u32[]{:S(2)}, u32[]{:S(2)}) collective-permute-start(f32[4,2,128,128]{3,2,1,0:T(8,128)S(1)} %copy-done.16), channel_id=1, source_target_pairs={{0,8},{8,0},{16,24},{24,16},{1,9},{9,1},{17,25},{25,17},{2,10},{10... | collective-permute-start | bytes 1572872 | tf_op jit(solution)/shard_map/ppermute | solution.py:550
  131.2 2.4 %sum_of.17 = (f32[4,2,128,128]{3,2,1,0:T(8,128)}, f32[4,2,128,128]{3,2,1,0:T(8,128)}) custom-call(f32[1,2,4,2,128,128]{5,4,3,2,1,0:T(8,128)} %bitcast.48, f32[1,2,4,2,128,128]{5,4,3,2,1,0:T(8,128)} %bitcast.49), custom_call_target="tpu_custom_call" | custom-call | flops 1048576 | bytes 3145728 | tf_op jit(solution)/shard_map/sum_of/pallas_call | solution.py:499
  133.6 2.0 %collective-permute-start.5 = (f32[4,2,128,128]{3,2,1,0:T(8,128)}, f32[4,2,128,128]{3,2,1,0:T(8,128)S(1)}, u32[]{:S(2)}, u32[]{:S(2)}) collective-permute-start(f32[4,2,128,128]{3,2,1,0:T(8,128)} %get-tuple-element.72), channel_id=1, source_target_pairs={{0,16},{8,24},{16,0},{24,8},{1,17},{9,25},{17,1},{25,9},{2,18},{10... | collective-permute-start | bytes 1572872 | tf_op jit(solution)/shard_map/ppermute | solution.py:550
  135.6 7.5 %collective-permute-done.11 = f32[4,2,128,128]{3,2,1,0:T(8,128)} collective-permute-done((f32[4,2,128,128]{3,2,1,0:T(8,128)S(1)}, f32[4,2,128,128]{3,2,1,0:T(8,128)}, u32[]{:S(2)}, u32[]{:S(2)}) %collective-permute-start.11) | collective-permute-done | bytes 524320 | tf_op jit(solution)/shard_map/ppermute | solution.py:550
  143.1 1.9 sum_of.19
  145.0 2.1 %collective-permute-start.12 = (f32[2,2,128,128]{3,2,1,0:T(8,128)}, f32[2,2,128,128]{3,2,1,0:T(8,128)S(1)}, u32[]{:S(2)}, u32[]{:S(2)}) collective-permute-start(f32[2,2,128,128]{3,2,1,0:T(8,128)} %get-tuple-element.84), channel_id=1, source_target_pairs={{0,16},{8,24},{16,0},{24,8},{1,17},{9,25},{17,1},{25,9},{2,18},{10... | collective-permute-start | bytes 786440 | tf_op jit(solution)/shard_map/ppermute | solution.py:550
  148.1 2.4 %sum_of.13 = (f32[4,2,128,128]{3,2,1,0:T(8,128)}, f32[4,2,128,128]{3,2,1,0:T(8,128)}) custom-call(f32[1,2,4,2,128,128]{5,4,3,2,1,0:T(8,128)} %bitcast.47, f32[1,2,4,2,128,128]{5,4,3,2,1,0:T(8,128)} %bitcast.50), custom_call_target="tpu_custom_call" | custom-call | flops 1048576 | bytes 3145728 | tf_op jit(solution)/shard_map/sum_of/pallas_call | solution.py:499
  150.5 3.2 %collective-permute-done.9 = f32[4,2,128,128]{3,2,1,0:T(8,128)S(1)} collective-permute-done((f32[4,2,128,128]{3,2,1,0:T(8,128)}, f32[4,2,128,128]{3,2,1,0:T(8,128)S(1)}, u32[]{:S(2)}, u32[]{:S(2)}) %collective-permute-start.9) | collective-permute-done | bytes 524320 | tf_op jit(solution)/shard_map/ppermute | solution.py:550
  154.5 1.9 sum_of.18
  157.2 2.0 sum_of.15
  159.2 1.7 collective-permute-start.6
  163.2 1.8 sum_of.20
  164.9 1.6 collective-permute-start.13
  167.8 1.8 sum_of.16
  169.6 1.5 collective-permute-start.7
  171.2 1.8 collective-permute-done.13
  173.7 1.9 sum_of.21
  175.6 2.9 %collective-permute-start.14 = (f32[2,2,128,128]{3,2,1,0:T(8,128)}, f32[2,2,128,128]{3,2,1,0:T(8,128)S(1)}, u32[]{:S(2)}, u32[]{:S(2)}) collective-permute-start(f32[2,2,128,128]{3,2,1,0:T(8,128)} %sum_of.21), channel_id=1, source_target_pairs={{0,4},{1,5},{2,6},{3,7},{4,0},{5,1},{6,2},{7,3},{8,12},{9,13},{10,... | collective-permute-start | bytes 786440 | tf_op jit(solution)/shard_map/ppermute | solution.py:550
  179.3 1.9 sum_of.14
  181.2 6.5 %collective-permute-done.14.refs_3_ = f32[2,2,128,128]{3,2,1,0:T(8,128)S(1)} collective-permute-done((f32[2,2,128,128]{3,2,1,0:T(8,128)}, f32[2,2,128,128]{3,2,1,0:T(8,128)S(1)}, u32[]{:S(2)}, u32[]{:S(2)}) %collective-permute-start.14) | collective-permute-done | bytes 262176 | tf_op jit(solution)/shard_map/ppermute | solution.py:550
  188.5 2.8 %power_of.1 = f32[2,128,128]{2,1,0:T(8,128)} custom-call(f32[2,2,128,128]{3,2,1,0:T(8,128)} %get-tuple-element.69.refs_0_, f32[2,2,128,128]{3,2,1,0:T(8,128)} %copy-done.13, f32[2,2,128,128]{3,2,1,0:T(8,128)} %copy-done.9, f32[2,2,128,128]{3,2,1,0:T(8,128)} %copy-done.11, f32[256,128]{1,0:T(8,128)} %constant.257.clone.refs_4_, ...), custom_call_target="tpu_custom_call" | custom-call | tf_op jit(solution)/shard_map/power_of/pallas_call | solution.py:532
  192.3 7.7 %all_to_all.18 = f32[2,128,128]{2,0,1:T(2,128)S(1)} all-to-all(f32[2,128,128]{2,0,1:T(2,128)S(1)} %copy.31), channel_id=1, replica_groups=mesh['wave'=4,'row'=8] {'wave'}, dimensions={1} | all-to-all | bytes 262144 | tf_op jit(solution)/shard_map/all_to_all | solution.py:665
  (60 shorter events, 18.1 us)
Async XLA Ops:
  0.0 10.4 %copy-start.14 = (s32[1,2]{1,0:T(1,128)S(1)}, s32[1,2]{1,0:T(1,128)}, u32[]{:S(2)}) copy-start(s32[1,2]{1,0:T(1,128)} %param.31) | copy-start | bytes 28
  0.0 11.0 %copy-start.15 = (s32[64,2]{0,1:T(2,128)S(1)}, s32[64,2]{0,1:T(2,128)}, u32[]{:S(2)}) copy-start(s32[64,2]{0,1:T(2,128)} %param.34) | copy-start | bytes 1540
  7.9 12.1 %collective-permute-start = (f32[2,256,1024]{2,1,0:T(8,128)}, f32[2,256,1024]{2,1,0:T(8,128)S(1)}, u32[]{:S(2)}, u32[]{:S(2)}) collective-permute-start(f32[2,256,1024]{2,1,0:T(8,128)} %get-tuple-element.46), channel_id=1, source_target_pairs={{0,1},{1,0},{2,3},{3,2},{4,5},{5,4},{6,7},{7,6},{8,9},{9,8},{10,11... | collective-permute-start | bytes 6291464 | tf_op jit(solution)/shard_map/ppermute | solution.py:550
  20.0 1.3 copy-start.1
  78.1 28.2 %collective-permute-start.1 = (f32[16,2,128,128]{3,2,1,0:T(8,128)}, f32[16,2,128,128]{3,2,1,0:T(8,128)S(1)}, u32[]{:S(2)}, u32[]{:S(2)}) collective-permute-start(f32[16,2,128,128]{3,2,1,0:T(8,128)} %get-tuple-element.51), channel_id=1, source_target_pairs={{0,1},{1,0},{2,3},{3,2},{4,5},{5,4},{6,7},{7,6},{8,9},{9,8},{10,11... | collective-permute-start | bytes 6291464 | tf_op jit(solution)/shard_map/ppermute | solution.py:550
  105.8 24.4 %collective-permute-start.8 = (f32[8,2,128,128]{3,2,1,0:T(8,128)}, f32[8,2,128,128]{3,2,1,0:T(8,128)S(1)}, u32[]{:S(2)}, u32[]{:S(2)}) collective-permute-start(f32[8,2,128,128]{3,2,1,0:T(8,128)} %get-tuple-element.76), channel_id=1, source_target_pairs={{0,1},{1,0},{2,3},{3,2},{4,5},{5,4},{6,7},{7,6},{8,9},{9,8},{10,11... | collective-permute-start | bytes 3145736 | tf_op jit(solution)/shard_map/ppermute | solution.py:550
  106.3 1.3 copy-start
  112.5 14.8 %copy-start.16 = (f32[4,2,128,128]{3,2,1,0:T(8,128)S(1)}, f32[4,2,128,128]{3,2,1,0:T(8,128)}, u32[]{:S(2)}) copy-start(f32[4,2,128,128]{3,2,1,0:T(8,128)} %get-tuple-element.82) | copy-start | bytes 1572868
  127.3 19.8 %collective-permute-start.2 = (f32[8,2,128,128]{3,2,1,0:T(8,128)}, f32[8,2,128,128]{3,2,1,0:T(8,128)S(1)}, u32[]{:S(2)}, u32[]{:S(2)}) collective-permute-start(f32[8,2,128,128]{3,2,1,0:T(8,128)} %get-tuple-element.66), channel_id=1, source_target_pairs={{0,1},{1,0},{2,3},{3,2},{4,5},{5,4},{6,7},{7,6},{8,9},{9,8},{10,11... | collective-permute-start | bytes 3145736 | tf_op jit(solution)/shard_map/ppermute | solution.py:550
  127.3 15.8 %collective-permute-start.11 = (f32[4,2,128,128]{3,2,1,0:T(8,128)S(1)}, f32[4,2,128,128]{3,2,1,0:T(8,128)}, u32[]{:S(2)}, u32[]{:S(2)}) collective-permute-start(f32[4,2,128,128]{3,2,1,0:T(8,128)S(1)} %copy-done.16), channel_id=1, source_target_pairs={{0,8},{8,0},{16,24},{24,16},{1,9},{9,1},{17,25},{25,17},{2,10},{10... | collective-permute-start | bytes 1572872 | tf_op jit(solution)/shard_map/ppermute | solution.py:550
  130.2 1.0 copy-start.2
  133.6 20.1 %collective-permute-start.9 = (f32[4,2,128,128]{3,2,1,0:T(8,128)}, f32[4,2,128,128]{3,2,1,0:T(8,128)S(1)}, u32[]{:S(2)}, u32[]{:S(2)}) collective-permute-start(f32[4,2,128,128]{3,2,1,0:T(8,128)} %get-tuple-element.78), channel_id=1, source_target_pairs={{0,8},{8,0},{16,24},{24,16},{1,9},{9,1},{17,25},{25,17},{2,10},{10... | collective-permute-start | bytes 1572872 | tf_op jit(solution)/shard_map/ppermute | solution.py:550
  133.6 22.8 %collective-permute-start.5 = (f32[4,2,128,128]{3,2,1,0:T(8,128)}, f32[4,2,128,128]{3,2,1,0:T(8,128)S(1)}, u32[]{:S(2)}, u32[]{:S(2)}) collective-permute-start(f32[4,2,128,128]{3,2,1,0:T(8,128)} %get-tuple-element.72), channel_id=1, source_target_pairs={{0,16},{8,24},{16,0},{24,8},{1,17},{9,25},{17,1},{25,9},{2,18},{10... | collective-permute-start | bytes 1572872 | tf_op jit(solution)/shard_map/ppermute | solution.py:550
  145.0 17.4 %collective-permute-start.12 = (f32[2,2,128,128]{3,2,1,0:T(8,128)}, f32[2,2,128,128]{3,2,1,0:T(8,128)S(1)}, u32[]{:S(2)}, u32[]{:S(2)}) collective-permute-start(f32[2,2,128,128]{3,2,1,0:T(8,128)} %get-tuple-element.84), channel_id=1, source_target_pairs={{0,16},{8,24},{16,0},{24,8},{1,17},{9,25},{17,1},{25,9},{2,18},{10... | collective-permute-start | bytes 786440 | tf_op jit(solution)/shard_map/ppermute | solution.py:550
  147.1 1.0 copy-start.3
  150.4 28.0 %collective-permute-start.3 = (f32[4,2,128,128]{3,2,1,0:T(8,128)}, f32[4,2,128,128]{3,2,1,0:T(8,128)S(1)}, u32[]{:S(2)}, u32[]{:S(2)}) collective-permute-start(f32[4,2,128,128]{3,2,1,0:T(8,128)} %get-tuple-element.68), channel_id=1, source_target_pairs={{0,16},{8,24},{16,0},{24,8},{1,17},{9,25},{17,1},{25,9},{2,18},{10... | collective-permute-start | bytes 1572872 | tf_op jit(solution)/shard_map/ppermute | solution.py:550
  153.6 0.8 copy-start.6
  156.4 0.8 copy-start.5
  159.2 7.9 %collective-permute-start.6 = (f32[2,2,128,128]{3,2,1,0:T(8,128)}, f32[2,2,128,128]{3,2,1,0:T(8,128)S(1)}, u32[]{:S(2)}, u32[]{:S(2)}) collective-permute-start(f32[2,2,128,128]{3,2,1,0:T(8,128)} %get-tuple-element.74), channel_id=1, source_target_pairs={{0,8},{8,0},{16,24},{24,16},{1,9},{9,1},{17,25},{25,17},{2,10},{10... | collective-permute-start | bytes 786440 | tf_op jit(solution)/shard_map/ppermute | solution.py:550
  160.9 10.2 %collective-permute-start.10 = (f32[2,2,128,128]{3,2,1,0:T(8,128)}, f32[2,2,128,128]{3,2,1,0:T(8,128)S(1)}, u32[]{:S(2)}, u32[]{:S(2)}) collective-permute-start(f32[2,2,128,128]{3,2,1,0:T(8,128)} %get-tuple-element.80), channel_id=1, source_target_pairs={{0,16},{8,24},{16,0},{24,8},{1,17},{9,25},{17,1},{25,9},{2,18},{10... | collective-permute-start | bytes 786440 | tf_op jit(solution)/shard_map/ppermute | solution.py:550
  162.4 0.7 copy-start.7
  164.9 8.0 %collective-permute-start.13 = (f32[2,2,128,128]{3,2,1,0:T(8,128)}, f32[2,2,128,128]{3,2,1,0:T(8,128)S(1)}, u32[]{:S(2)}, u32[]{:S(2)}) collective-permute-start(f32[2,2,128,128]{3,2,1,0:T(8,128)} %sum_of.20), channel_id=1, source_target_pairs={{0,2},{1,3},{2,0},{3,1},{4,6},{5,7},{6,4},{7,5},{8,10},{9,11},{10,... | collective-permute-start | bytes 786440 | tf_op jit(solution)/shard_map/ppermute | solution.py:550
  167.1 0.7 copy-start.8
  169.6 11.6 %collective-permute-start.7 = (f32[2,2,128,128]{3,2,1,0:T(8,128)}, f32[2,2,128,128]{3,2,1,0:T(8,128)S(1)}, u32[]{:S(2)}, u32[]{:S(2)}) collective-permute-start(f32[2,2,128,128]{3,2,1,0:T(8,128)} %sum_of.16), channel_id=1, source_target_pairs={{0,2},{1,3},{2,0},{3,1},{4,6},{5,7},{6,4},{7,5},{8,10},{9,11},{10,... | collective-permute-start | bytes 786440 | tf_op jit(solution)/shard_map/ppermute | solution.py:550
  171.2 1.8 copy-start.10
  173.0 0.7 copy-start.12
  175.6 12.2 %collective-permute-start.14 = (f32[2,2,128,128]{3,2,1,0:T(8,128)}, f32[2,2,128,128]{3,2,1,0:T(8,128)S(1)}, u32[]{:S(2)}, u32[]{:S(2)}) collective-permute-start(f32[2,2,128,128]{3,2,1,0:T(8,128)} %sum_of.21), channel_id=1, source_target_pairs={{0,4},{1,5},{2,6},{3,7},{4,0},{5,1},{6,2},{7,3},{8,12},{9,13},{10,... | collective-permute-start | bytes 786440 | tf_op jit(solution)/shard_map/ppermute | solution.py:550
  178.5 0.8 copy-start.4
  181.2 6.6 %collective-permute-start.4 = (f32[2,2,128,128]{3,2,1,0:T(8,128)}, f32[2,2,128,128]{3,2,1,0:T(8,128)S(1)}, u32[]{:S(2)}, u32[]{:S(2)}) collective-permute-start(f32[2,2,128,128]{3,2,1,0:T(8,128)} %get-tuple-element.70), channel_id=1, source_target_pairs={{0,8},{8,0},{16,24},{24,16},{1,9},{9,1},{17,25},{25,17},{2,10},{10... | collective-permute-start | bytes 786440 | tf_op jit(solution)/shard_map/ppermute | solution.py:550
  181.2 6.6 %copy-start.9 = (f32[2,2,128,128]{3,2,1,0:T(8,128)}, f32[2,2,128,128]{3,2,1,0:T(8,128)S(1)}, u32[]{:S(2)}) copy-start(f32[2,2,128,128]{3,2,1,0:T(8,128)S(1)} %collective-permute-done.7.refs_2_) | copy-start | bytes 786436
  187.7 0.7 copy-start.11
  187.8 0.8 copy-start.13

commit v4 on v3

--- a/solution.py
+++ b/solution.py
@@ -23,6 +23,7 @@
 DEPTH = BLOCKS * PAIR
 FREQS = BLOCKS * LANES
 COL_TILES = FOLD // PAIR
+CUT_STEPS = 4
 
 
 def angles_of(first, second):
@@ -71,10 +72,14 @@
     refs[1][place] = low
 
 
-def split_kernel(sign_ref, wave_ref, trans_ref, mine_ref, theirs_ref):
+def sign_of(info_ref):
+    return 1.0 - 2.0 * info_ref[2].astype(jnp.float32)
+
+
+def split_kernel(info_ref, wave_ref, trans_ref, mine_ref, theirs_ref):
     wave_re, wave_im = wave_ref[0, 0], wave_ref[1, 0]
     trans_re, trans_im = trans_ref[0, 0], trans_ref[0, 1]
-    sign = sign_ref[0]
+    sign = sign_of(info_ref)
     for part, value in enumerate(
         (wave_re * trans_re - wave_im * trans_im, wave_re * trans_im + wave_im * trans_re)
     ):
@@ -83,7 +88,7 @@
         theirs_ref[part] = low - high
 
 
-def split_columns(sign, plane_waves, transmission):
+def split_columns(info, plane_waves, transmission):
     rows = plane_waves.shape[2]
     step = 32
     out = jax.ShapeDtypeStruct((2, rows, FOLD), jnp.float32)
@@ -104,10 +109,14 @@
             flops=20 * rows * GRID, bytes_accessed=24 * rows * GRID, transcendentals=0
         ),
         name="split_columns",
-    )(sign, plane_waves, transmission)
-
-
-def column_forward_kernel(parity_ref, field_ref, table_hi, table_lo, out_ref, *field):
+    )(info, plane_waves, transmission)
+
+
+def column_forward_table():
+    return table_halves(both(lambda freq: paired(cos_sin(np.arange(FOLD), freq))))
+
+
+def column_forward_kernel(info_ref, field_ref, table_hi, table_lo, out_ref, *field):
     rows = field_ref.shape[1]
 
     @pl.when(pl.program_id(0) == 0)
@@ -120,10 +129,10 @@
         out_ref[part] = result[part * rows : (part + 1) * rows]
 
 
-def column_forward(parity, field):
+def column_forward(info, field):
     rows = field.shape[1]
-    table = table_halves(both(lambda freq: paired(cos_sin(np.arange(FOLD), freq))))
-    table_spec = pl.BlockSpec((1, FOLD, PAIR), lambda j, c: (c[0], 0, j))
+    table = column_forward_table()
+    table_spec = pl.BlockSpec((1, FOLD, PAIR), lambda j, info: (info[2], 0, j))
     return pl.pallas_call(
         column_forward_kernel,
         out_shape=jax.ShapeDtypeStruct((2, rows, DEPTH), jnp.float32),
@@ -144,20 +153,29 @@
             transcendentals=0,
         ),
         name="column_forward",
-    )(parity, field, *table)
+    )(info, field, *table)
 
 
 def row_forward_kernel(
-    parity_ref, mine_ref, theirs_ref, table_hi, table_lo, down_ref, along_ref,
-    out_hi, out_lo, field_hi, field_lo,
+    info_ref, mine_ref, theirs_ref, col_hi, col_lo, table_hi, table_lo, down_ref, along_ref,
+    out_hi, out_lo, field_hi, field_lo, theirs_hi, theirs_lo,
 ):
     rows = mine_ref.shape[1]
     field = (field_hi, field_lo)
-    core = parity_ref[0]
-    for place, ref in ((core, mine_ref), (1 - core, theirs_ref)):
-        start = pl.ds(pl.multiple_of(place * rows, LANES), rows)
+    core = info_ref[2]
+
+    @pl.when(pl.program_id(0) == 0)
+    def _():
         for part in (0, 1):
-            put(field, (start, slice(part * PAIR, (part + 1) * PAIR)), ref[part])
+            put((theirs_hi, theirs_lo), slice(part * rows, (part + 1) * rows), theirs_ref[part])
+
+    theirs = dot3((theirs_hi[...], theirs_lo[...]), (col_hi[0], col_lo[0]))
+    here = pl.ds(pl.multiple_of(core * rows, LANES), rows)
+    there = pl.ds(pl.multiple_of((1 - core) * rows, LANES), rows)
+    for part in (0, 1):
+        cols = slice(part * PAIR, (part + 1) * PAIR)
+        put(field, (here, cols), mine_ref[part])
+        put(field, (there, cols), theirs[part * rows : (part + 1) * rows])
     cos_x, sin_x, square_x = (along_ref[0, i : i + 1] for i in range(3))
     outs = (out_hi, out_lo)
 
@@ -193,7 +211,7 @@
     return [np.cos(angle) * weight, np.sin(angle) * weight, freq.astype(np.float64) ** 2]
 
 
-def row_forward(parity, mine, theirs):
+def row_forward(info, mine, theirs):
     rows = mine.shape[1]
     all_freqs = np.concatenate([freqs(0), freqs(1)])
     table = table_halves(paired(cos_sin(np.arange(2 * rows), all_freqs)).T)
@@ -202,7 +220,10 @@
     tile = pl.BlockSpec((2, rows, PAIR), lambda j, *_: (0, 0, j))
     out = jax.ShapeDtypeStruct((2, 2 * DEPTH, DEPTH), jnp.bfloat16)
     out_spec = pl.BlockSpec((2, 2 * DEPTH, PAIR), lambda j, *_: (0, 0, j))
-    table_spec = pl.BlockSpec((2 * DEPTH, 2 * rows), lambda j, *_: (0, 0))
+    table_spec = pl.BlockSpec(
+        (2 * DEPTH, 2 * rows), lambda j, *_: (0, 0), pipeline_mode=pl.Buffered(1)
+    )
+    col_spec = pl.BlockSpec((1, FOLD, PAIR), lambda j, info: (info[2], 0, j))
     return pl.pallas_call(
         row_forward_kernel,
         out_shape=(out, out),
@@ -211,14 +232,19 @@
             grid=(BLOCKS,),
             in_specs=[
                 tile,
-                tile,
+                pl.BlockSpec(
+                    (2, rows, FOLD), lambda j, *_: (0, 0, 0), pipeline_mode=pl.Buffered(1)
+                ),
+                col_spec,
+                col_spec,
                 table_spec,
                 table_spec,
                 pl.BlockSpec(down.shape, lambda j, *_: (0, 0)),
-                pl.BlockSpec((1, 3, LANES), lambda j, c: (c[0], 0, j)),
+                pl.BlockSpec((1, 3, LANES), lambda j, info: (info[2], 0, j)),
             ],
             out_specs=(out_spec, out_spec),
-            scratch_shapes=[pltpu.VMEM((2 * rows, 2 * PAIR), jnp.bfloat16)] * 2,
+            scratch_shapes=[pltpu.VMEM((2 * rows, 2 * PAIR), jnp.bfloat16)] * 2
+            + [pltpu.VMEM((2 * rows, FOLD), jnp.bfloat16)] * 2,
         ),
         cost_estimate=pl.CostEstimate(
             flops=48 * rows * DEPTH * DEPTH,
@@ -226,10 +252,13 @@
             transcendentals=0,
         ),
         name="row_forward",
-    )(parity, mine, theirs, *table, jnp.asarray(down), jnp.asarray(along))
-
-
-def cut_slots(layout, info_ref, slot_ref, pos_ref, re_ref, im_ref, sign_ref, field, outs):
+    )(
+        info, mine, theirs, *column_forward_table(), *table, jnp.asarray(down),
+        jnp.asarray(along),
+    )
+
+
+def cut_slots(layout, first, info_ref, slot_ref, pos_ref, weight_ref, field, outs):
     chip_rows, waves, own, _ = layout
     height = chip_rows + WINDOW
     lane = lax.broadcasted_iota(jnp.int32, (WINDOW, WINDOW), 1)
@@ -238,10 +267,10 @@
     def one(index, out_ref, place):
         target = row_rank ^ slot_ref[0, index]
         probe = (target * waves + (wave_rank ^ slot_ref[1, index])) * own + slot_ref[2, index]
-        row = slot_ref[3, index] * height + lax.rem(pos_ref[0, probe], chip_rows)
-        start = lax.rem(pos_ref[1, probe] + (GRID - HALF), GRID)
+        row = slot_ref[3, index] * height + lax.rem(pos_ref[probe, 0], chip_rows)
+        start = lax.rem(pos_ref[probe, 1] + (GRID - HALF), GRID)
         col = lax.rem(start, FOLD)
-        turned = jnp.where(start >= FOLD, sign_ref[0], 1.0)
+        turned = jnp.where(start >= FOLD, sign_of(info_ref), 1.0)
         shift = lax.rem(col, LANES)
         back = lax.rem(LANES - shift, LANES)
 
@@ -253,21 +282,21 @@
             return jnp.where(lane < LANES - shift, sides[0], sides[1])
 
         real_part, imag_part = cut(0), cut(1)
-        weight_re, weight_im = re_ref[probe] * turned, im_ref[probe] * turned
+        weight_re, weight_im = weight_ref[0, probe] * turned, weight_ref[1, probe] * turned
         out_ref[place, 0] = weight_re * real_part - weight_im * imag_part
         out_ref[place, 1] = weight_re * imag_part + weight_im * real_part
 
     keep_ref, send_ref = outs
-    count = keep_ref.shape[0]
-
-    @pl.loop(0, count)
+    total = slot_ref.shape[1] // 2
+
+    @pl.loop(0, keep_ref.shape[0])
     def _(place):
-        one(count + place, send_ref, place)
-        one(place, keep_ref, place)
+        one(total + first + place, send_ref, place)
+        one(first + place, keep_ref, place)
 
 
 def inverse_kernel(
-    layout, cuts, info_ref, slot_ref, pos_ref, re_ref, im_ref, sign_ref,
+    layout, cuts, base, info_ref, slot_ref, pos_ref, weight_ref,
     spec_hi, spec_lo, row_hi, row_lo, col_hi, col_lo, *refs,
 ):
     chip_rows, _, _, segments = layout
@@ -295,7 +324,7 @@
         put(rows, (part, slice(count, 2 * count), cols), sums[0] - sums[1])
         if exports is not None:
             for index in range(segments):
-                start = pl.multiple_of(info_ref[3 + cuts + index] * height, LANES)
+                start = pl.multiple_of(info_ref[base + cuts + index] * height, LANES)
                 for export, source in zip(exports, rows):
                     export[0, index * height : (index + 1) * height] = source[
                         part, pl.ds(start, height), cols
@@ -311,7 +340,7 @@
         tile = now % COL_TILES
         part = now // COL_TILES % 2
         segment = now // (2 * COL_TILES)
-        source = pl.ds(pl.multiple_of(info_ref[3 + segment] * height, LANES), height)
+        source = pl.ds(pl.multiple_of(info_ref[base + segment] * height, LANES), height)
         place = pl.ds(pl.multiple_of(segment * height, LANES), height)
         value = dot3((rows[0][part, source], rows[1][part, source]), (col_hi[0], col_lo[0]))
         field[part, 2 * tile, place] = value[:, :LANES]
@@ -319,20 +348,26 @@
 
         @pl.when(tile == 0)
         def _():
-            field[part, 2 * COL_TILES, place] = value[:, :LANES] * sign_ref[0]
-
-    @pl.when(step == last)
+            field[part, 2 * COL_TILES, place] = value[:, :LANES] * sign_of(info_ref)
+
+    @pl.when(step >= last)
     def _():
-        cut_slots(
-            layout, info_ref, slot_ref, pos_ref, re_ref, im_ref, sign_ref, field, outs
-        )
+        begin = (step - last) * outs[0].shape[0]
+        cut_slots(layout, begin, info_ref, slot_ref, pos_ref, weight_ref, field, outs)
+
+
+def window_spec(count, last):
+    return pl.BlockSpec(
+        (count // CUT_STEPS, 2, WINDOW, WINDOW),
+        lambda i, *_: (jnp.maximum(i - last, 0), 0, 0, 0),
+    )
 
 
 def column_table():
     return table_halves(both(lambda freq: paired(cos_sin(np.arange(FOLD), freq)).T))
 
 
-def inverse(layout, cuts, export, spectrum, row_list, slots, info, positions, weights, sign):
+def inverse(layout, cuts, export, base, spectrum, row_list, slots, info, positions, weights):
     chip_rows, _, _, segments = layout
     height = chip_rows + WINDOW
     count = slots.shape[1] // 2
@@ -354,20 +389,16 @@
     )
     col_spec = pl.BlockSpec((1, DEPTH, PAIR), col_map)
     shapes = [jax.ShapeDtypeStruct((count, 2, WINDOW, WINDOW), jnp.float32)] * 2
-    specs = [
-        pl.BlockSpec(
-            (count, 2, WINDOW, WINDOW), lambda i, *_: (0, 0, 0, 0), pipeline_mode=pl.Buffered(1)
-        )
-    ] * 2
+    specs = [window_spec(count, last)] * 2
     if export:
         shapes += [jax.ShapeDtypeStruct((2, segments * height, DEPTH), jnp.bfloat16)] * 2
         specs += [pl.BlockSpec((1, segments * height, PAIR), spec_map)] * 2
     return pl.pallas_call(
-        functools.partial(inverse_kernel, layout, cuts),
+        functools.partial(inverse_kernel, layout, cuts, base),
         out_shape=shapes,
         grid_spec=pltpu.PrefetchScalarGridSpec(
-            num_scalar_prefetch=6,
-            grid=(last + 1,),
+            num_scalar_prefetch=4,
+            grid=(last + CUT_STEPS,),
             in_specs=[spec, spec, row_spec, row_spec, col_spec, col_spec],
             out_specs=specs,
             scratch_shapes=[
@@ -383,13 +414,12 @@
         ),
         name="inverse",
     )(
-        info, jnp.asarray(slots), positions, *weights, sign, *spectrum, *row_table,
-        *column_table(),
+        info, jnp.asarray(slots), positions, weights, *spectrum, *row_table, *column_table(),
     )
 
 
 def column_inverse_kernel(
-    layout, info_ref, slot_ref, pos_ref, re_ref, im_ref, sign_ref,
+    layout, info_ref, slot_ref, pos_ref, weight_ref,
     rows_hi, rows_lo, table_hi, table_lo, keep_ref, send_ref, field,
 ):
     chip_rows, _, _, segments = layout
@@ -408,17 +438,16 @@
 
         @pl.when(tile == 0)
         def _():
-            field[part, 2 * COL_TILES, rows] = value[:, :LANES] * sign_ref[0]
-
-    @pl.when(step == 2 * segments * COL_TILES)
+            field[part, 2 * COL_TILES, rows] = value[:, :LANES] * sign_of(info_ref)
+
+    @pl.when(step >= 2 * segments * COL_TILES)
     def _():
-        cut_slots(
-            layout, info_ref, slot_ref, pos_ref, re_ref, im_ref, sign_ref, field,
-            (keep_ref, send_ref),
-        )
-
-
-def column_inverse(layout, rows, slots, info, positions, weights, sign):
+        begin = (step - 2 * segments * COL_TILES) * keep_ref.shape[0]
+        outs = (keep_ref, send_ref)
+        cut_slots(layout, begin, info_ref, slot_ref, pos_ref, weight_ref, field, outs)
+
+
+def column_inverse(layout, rows, slots, info, positions, weights):
     chip_rows, _, _, segments = layout
     count = slots.shape[1] // 2
     height = chip_rows + WINDOW
@@ -434,15 +463,13 @@
         (1, DEPTH, PAIR), lambda i, info, *_: (info[2], 0, jnp.minimum(i, last) % COL_TILES)
     )
     out = jax.ShapeDtypeStruct((count, 2, WINDOW, WINDOW), jnp.float32)
-    out_spec = pl.BlockSpec(
-        (count, 2, WINDOW, WINDOW), lambda i, *_: (0, 0, 0, 0), pipeline_mode=pl.Buffered(1)
-    )
+    out_spec = window_spec(count, last + 1)
     return pl.pallas_call(
         functools.partial(column_inverse_kernel, layout),
         out_shape=(out, out),
         grid_spec=pltpu.PrefetchScalarGridSpec(
-            num_scalar_prefetch=6,
-            grid=(last + 2,),
+            num_scalar_prefetch=4,
+            grid=(last + 1 + CUT_STEPS,),
             in_specs=[
                 rows_spec,
                 rows_spec,
@@ -461,7 +488,7 @@
         ),
         name="column_inverse",
     )(
-        info, jnp.asarray(slots), positions, *weights, sign, *rows, *table,
+        info, jnp.asarray(slots), positions, weights, *rows, *table,
     )
 
 
@@ -509,40 +536,78 @@
     )(*arrays)
 
 
+def spread_kernel(first_ref, second_ref, *outs):
+    for index, out_ref in enumerate(outs):
+        out_ref[...] = first_ref[index] + second_ref[index]
+
+
+def spread_sum(first, second, count):
+    tail = first.shape[1:]
+    zeros = (0,) * len(tail)
+    size = first.shape[0] // count
+    step = max(1, size // 2)
+    out = jax.ShapeDtypeStruct((size,) + tail, jnp.float32)
+    spec = pl.BlockSpec((count, step) + tail, lambda i: (0, i) + zeros)
+    return pl.pallas_call(
+        spread_kernel,
+        out_shape=[out] * count,
+        grid=(size // step,),
+        in_specs=[spec, spec],
+        out_specs=[pl.BlockSpec((step,) + tail, lambda i: (i,) + zeros)] * count,
+        cost_estimate=pl.CostEstimate(
+            flops=first.size, bytes_accessed=12 * first.size, transcendentals=0
+        ),
+        name="spread_sum",
+    )(*(value.reshape((count, size) + tail) for value in (first, second)))
+
+
 def power_kernel(count, scale, *refs):
     terms, (down_ref, along_ref, out_ref) = refs[:count], refs[count:]
     down, along = halves_of(down_ref[...]), halves_of(along_ref[...])
-    for probe in range(out_ref.shape[0]):
-        total = terms[0][probe]
-        for term in terms[1:]:
-            total += term[probe]
-        value = dot3(down, halves_of(jnp.concatenate([total[0], total[1]], axis=1)))
-        cos_part, sin_part = value[:WINDOW], value[WINDOW:]
-        real_part = cos_part[:, :WINDOW] + sin_part[:, WINDOW:]
-        imag_part = cos_part[:, WINDOW:] - sin_part[:, :WINDOW]
-        value = dot3(halves_of(jnp.concatenate([real_part, imag_part])), along)
-        real_part = value[:WINDOW, :WINDOW] + value[WINDOW:, WINDOW:]
-        imag_part = value[WINDOW:, :WINDOW] - value[:WINDOW, WINDOW:]
-        out_ref[probe] = (real_part * real_part + imag_part * imag_part) * scale
+    total = terms[0][0, 0]
+    for term in terms[1:]:
+        total += term[0, 0]
+    value = dot3(down, halves_of(jnp.concatenate([total[0], total[1]], axis=1)))
+    cos_part, sin_part = value[:WINDOW], value[WINDOW:]
+    real_part = cos_part[:, :WINDOW] + sin_part[:, WINDOW:]
+    imag_part = cos_part[:, WINDOW:] - sin_part[:, :WINDOW]
+    value = dot3(halves_of(jnp.concatenate([real_part, imag_part])), along)
+    real_part = value[:WINDOW, :WINDOW] + value[WINDOW:, WINDOW:]
+    imag_part = value[WINDOW:, :WINDOW] - value[:WINDOW, WINDOW:]
+    out_ref[0] = (real_part * real_part + imag_part * imag_part) * scale
 
 
 def power_of(terms, scale):
-    count = terms[0].shape[0]
-    table = cos_sin(np.arange(WINDOW), FACTOR * np.arange(WINDOW))
+    tail = terms[0][0].shape[1:]
+    count = terms[0][0].shape[0] // terms[0][2]
+    table = cos_sin(np.arange(WINDOW), FACTOR * np.arange(WINDOW)).astype(np.float32)
+    down, along = np.concatenate(list(table)), np.concatenate(list(table), axis=1)
     return pl.pallas_call(
         functools.partial(power_kernel, len(terms), scale),
         out_shape=jax.ShapeDtypeStruct((count, WINDOW, WINDOW), jnp.float32),
+        grid=(count,),
+        in_specs=[
+            pl.BlockSpec((1, 1) + tail, lambda i, part=part: (part, i, 0, 0, 0))
+            for _, part, _ in terms
+        ]
+        + [
+            pl.BlockSpec(down.shape, lambda i: (0, 0)),
+            pl.BlockSpec(along.shape, lambda i: (0, 0)),
+        ],
+        out_specs=pl.BlockSpec((1, WINDOW, WINDOW), lambda i: (i, 0, 0)),
         name="power_of",
     )(
-        *terms, jnp.asarray(np.concatenate(list(table)).astype(np.float32)),
-        jnp.asarray(np.concatenate(list(table), axis=1).astype(np.float32)),
+        *(array.reshape((parts, count) + tail) for array, _, parts in terms),
+        jnp.asarray(down), jnp.asarray(along),
     )
 
 
 def coefficients(positions, wave_index, wave_weight, wave_phase):
-    turns = (FACTOR * (positions[0] * wave_index[0, 0] + positions[1] * wave_index[0, 1])) % GRID
+    turns = (
+        FACTOR * (positions[:, 0] * wave_index[0, 0] + positions[:, 1] * wave_index[0, 1])
+    ) % GRID
     angles = wave_phase[0] - turns.astype(jnp.float32) * (2.0 * math.pi / GRID)
-    return wave_weight[0] * jnp.cos(angles), wave_weight[0] * jnp.sin(angles)
+    return wave_weight[0] * jnp.stack([jnp.cos(angles), jnp.sin(angles)])
 
 
 def flip(block, axis, bit):
@@ -557,49 +622,42 @@
     row_rank = lax.axis_index("row")
     wave_rank = lax.axis_index("wave")
     core = row_rank % 2
-    sign = (1.0 - 2.0 * core.astype(jnp.float32))[None]
-    parity = core[None]
     chip_rows = 2 * rows_here
     chips = row_count // 2
     far = chips // 2
     own = probe_pos.shape[0] // (row_count * wave_count)
 
-    mine, theirs = split_columns(sign, plane_waves, transmission)
-    theirs = flip(theirs, "row", 1)
-    positions = probe_pos.T
-    weights = coefficients(positions, wave_index, wave_weight, wave_phase)
-    mine = column_forward(parity, mine)
-    mine, theirs = lax.optimization_barrier((mine, theirs))
-    spectrum = row_forward(parity, mine, column_forward(parity, theirs))
-
-    wave_bits = wave_count.bit_length() - 1
-    orders = (list(range(wave_bits - 1, -1, -1)), list(range(wave_bits)))
     segments = far // 2
     layout = (chip_rows, wave_count, own, segments)
 
     def slots_of(odd, halves):
         slots = []
         for core_bit in (0, 1):
-            for at, half in enumerate(halves):
-                for digits in range(wave_count):
-                    wave = 0
-                    for place, bit in enumerate(orders[half]):
-                        wave |= (digits >> (wave_bits - 1 - place) & 1) << bit
+            for wave in range(wave_count):
+                for at, half in enumerate(halves):
                     for index in range(segments):
                         row = ((half * segments + index) * 2 + odd) * 2 + core_bit
                         where = at * segments + index
                         slots += [(row, wave, probe, where) for probe in range(own)]
         return np.array(slots, np.int32).T
 
-    def info_of(odd, halves):
-        chip = row_rank // 2
-        info = [row_rank, wave_rank, core]
-        for half in halves:
+    upper, lower = 1, 0
+    chip = row_rank // 2
+    info = [row_rank, wave_rank, core]
+    for odd in (1, 0):
+        for half in (upper, lower):
             for index in range(segments):
                 target = chip ^ ((half * segments + index) * 2 + odd)
                 away = (target - chip) % chips
                 info.append(away // far * segments + away % far // 2)
-        return jnp.stack(info)
+    info = jnp.stack(info)
+
+    mine, theirs = split_columns(info, plane_waves, transmission)
+    theirs = flip(theirs, "row", 1)
+    weights = coefficients(probe_pos, wave_index, wave_weight, wave_phase)
+    mine = column_forward(info, mine)
+    mine, theirs = lax.optimization_barrier((mine, theirs))
+    spectrum = row_forward(info, mine, theirs)
 
     def rows_of(odd):
         return np.concatenate(
@@ -612,54 +670,42 @@
     def later(value, *before):
         return lax.optimization_barrier((value,) + before)
 
-    upper, lower = 1, 0
-    common = (positions, weights, sign)
-    stages = {}
-
-    def advance(value, *keys):
-        for key in keys:
-            terms, place = stages[key]
-            stay, send = sum_of(terms, True)
-            if value is not None:
-                value, stay, send = later(value, stay, send)
-            arrived = flip(send, "wave", 1 << orders[key[1]][place])
-            stages[key] = [[(stay, 0, 1), (arrived, 0, 1)], place + 1]
-        return value
-
-    def finish(key):
-        while stages[key][1] < wave_bits:
-            advance(None, key)
-        return stages[key][0]
-
+    def over_waves(pieces):
+        return [(pieces[0], 0, 1)] + [
+            (flip(piece, "wave", bits), 0, 1) for bits, piece in enumerate(pieces) if bits
+        ]
+
+    common = (info, probe_pos, weights)
     keep, send = inverse(
-        layout, 2 * segments, False, spectrum, rows_of(1), slots_of(1, (upper, lower)),
-        info_of(1, (upper, lower)), *common,
+        layout, 2 * segments, False, 3, spectrum, rows_of(1), slots_of(1, (upper, lower)), *common
     )
     arrived = flip(send, "row", 1)
-    for at, half in enumerate((upper, lower)):
-        stages[1, half] = [[(keep, at, 2), (arrived, at, 2)], 0]
-    spectrum = later(spectrum, send)[0]
-    keep, send, rows_hi, rows_lo = inverse(
-        layout, segments, True, spectrum, rows_of(0), slots_of(0, (upper,)),
-        info_of(0, (upper, lower)), *common,
-    )
-    stages[0, upper] = [[(keep, 0, 1), (flip(send, "row", 1), 0, 1)], 0]
-    rows = (rows_hi, rows_lo)
-    rows = advance(rows, (1, upper), (1, lower))
-    keep, send = column_inverse(
-        layout, rows, slots_of(0, (lower,)), info_of(0, (lower,)), *common
-    )
-    stages[0, lower] = [[(keep, 0, 1), (flip(send, "row", 1), 0, 1)], 0]
-
-    near_upper = flip(sum_of(finish((1, upper)), False), "row", 2)
-    near_lower = flip(sum_of(finish((1, lower)), False), "row", 2)
+    spectrum, keep = later(spectrum, keep)
+    keep_upper, send, rows_hi, rows_lo = inverse(
+        layout, segments, True, 3 + far, spectrum, rows_of(0), slots_of(0, (upper,)), *common
+    )
+    arrived_upper = flip(send, "row", 1)
+    pieces = spread_sum(keep, arrived, wave_count)
+    (rows_hi, rows_lo), pieces = later((rows_hi, rows_lo), pieces)
+    odd_terms = over_waves(pieces)
+    keep_lower, send = column_inverse(
+        layout, (rows_hi, rows_lo), slots_of(0, (lower,)), *common
+    )
+    arrived_lower = flip(send, "row", 1)
+    pieces = spread_sum(keep_upper, arrived_upper, wave_count)
+    odd_arrays, pieces = later([term[0] for term in odd_terms], pieces)
+    odd_terms = [(array, 0, 1) for array in odd_arrays]
+    upper_terms = over_waves(pieces)
+    near = flip(sum_of(odd_terms, False), "row", 2)
+    lower_terms = over_waves(spread_sum(keep_lower, arrived_lower, wave_count))
+
     bit = row_count // 2
-    send = sum_of(finish((0, upper)) + [(near_upper, 0, 1)], False)
-    terms = [term[0] for term in finish((0, lower))] + [near_lower, flip(send, "row", bit)]
+    send = sum_of(upper_terms + [(near, 0, 2)], False)
+    terms = lower_terms + [(near, 1, 2), (flip(send, "row", bit), 0, 1)]
     while bit > 4:
         bit //= 2
-        stay, send = sum_of([(term, 0, 1) for term in terms], True)
-        terms = [stay, flip(send, "row", bit)]
+        stay, send = sum_of(terms, True)
+        terms = [(stay, 0, 1), (flip(send, "row", bit), 0, 1)]
     total_waves = plane_waves.shape[1] * wave_count
     power = power_of(terms, 1.0 / (WINDOW * WINDOW * total_waves))
     return lax.all_to_all(power, "wave", split_axis=1, concat_axis=0, tiled=True)

time: 202 us -> 193 us (0.955)
  Pallas kernels: 138 us -> 129 us
  waiting for transfers between devices: 19.7 us -> 24.3 us
  local copies, waits for them, and re-layouts: 13.7 us -> 10.8 us
    pallas_call x11 -> x2, Pallas kernels: 22.7 us -> 4.32 us  [sum_of(): pl.pallas_call(functools.partial(sum_kernel, len(terms), halve), out_shap...]
    pallas_call x2 -> x5, Pallas kernels: 63.1 us -> 72.2 us  [the longest x2 64.1 us: inverse(): pl.pallas_call(functools.partial(inverse_kernel, layout, cuts, base), out...]
    pallas_call x2 -> x1, Pallas kernels: 12.8 us -> 7.12 us  [column_forward(): pl.pallas_call(column_forward_kernel, out_shape=jax.ShapeDtypeStruct((2,...]
    ppermute x15, waiting for transfers between devices: 19.7 us -> 24.3 us  [flip(): return lax.ppermute(block, axis, [(i, i ^ bit) for i in range(count)])]
    pallas_call x1, Pallas kernels: 13.7 us -> 17.9 us  [row_forward(): pl.pallas_call(row_forward_kernel, out_shape=(out, out), grid_spec=pltpu....]
    unnamed x34 -> x39, local copies, waits for them, and re-layouts: 9.99 us -> 7.86 us
  transfers between devices with their start and end apart: 15 -> 15, of which waited for: 6 -> 7; matrix products, arithmetic and copies ran while one was open for 3% -> 2% of each run, Pallas kernels for 35% -> 32%
where the time goes in v4:
time: 193 us; the launch traced here: 191 us
  Pallas kernels  129 us (67%)
  waiting for transfers between devices  24.3 us (13%)
  starting transfers between devices  16.2 us (8%)
  local copies, waits for them, and re-layouts  10.8 us (6%)
  blocking collectives  7.96 us (4%)
    pallas_call x2, Pallas kernels, inverse(): pl.pallas_call(functools.partial(inverse_kernel, layout, cuts, base), out...  64.1 us
    ppermute x15, waiting for transfers between devices, flip(): return lax.ppermute(block, axis, [(i, i ^ bit) for i in range(count)])  24.3 us
    pallas_call x1, Pallas kernels, row_forward(): pl.pallas_call(row_forward_kernel, out_shape=(out, out), grid_spec=pltpu....  17.9 us
    ppermute x15, starting transfers between devices, flip(): return lax.ppermute(block, axis, [(i, i ^ bit) for i in range(count)])  16.2 us
    pallas_call x1, Pallas kernels, column_inverse(): pl.pallas_call(functools.partial(column_inverse_kernel, layout), out_shap...  15.2 us
    pallas_call x1, Pallas kernels, split_columns(): pl.pallas_call(split_kernel, out_shape=(out, out), grid_spec=pltpu.Prefet...  8.56 us
    pallas_call x3, Pallas kernels, spread_sum(): pl.pallas_call(spread_kernel, out_shape=[out] * count, grid=(size // step...  8.09 us
    all_to_all x1, blocking collectives, shards(): lax.all_to_all(power, 'wave', split_axis=1, concat_axis=0, tiled=True)  7.96 us
  transfers between devices with their start and end apart: 15, of which 7 were waited for; matrix products, arithmetic and copies ran while one was open for 2% of the time, Pallas kernels for 32%

profile of v4, /device:TPU:0, one launch (start us, length us, event | category | flops | bytes accessed | tf_op | source)
XLA Modules:
  0.0 191.2 jit_solution(5353619188393835945)
XLA Ops:
  0.6 8.6 %split_columns.1 = (f32[2,256,1024]{2,1,0:T(8,128)}, f32[2,256,1024]{2,1,0:T(8,128)}) custom-call(s32[7]{0:T(128)} %stack.33.info_ref, f32[2,1,256,2048]{3,2,1,0:T(8,128)} %wave_ref.1, f32[1,2,256,2048]{3,2,1,0:T(8,128)} %trans_ref.1), custom_call_target="tpu_custom_call" | custom-call | flops 10485760 | bytes 12582912 | tf_op jit(solution)/shard_map/split_columns/pallas_call | solution.py:96
  12.3 1.3 fusion.4
  14.3 7.1 %column_forward.1.mine_ref = f32[2,256,768]{2,1,0:T(8,128)} custom-call(s32[7]{0:T(128)} %stack.33.info_ref, f32[2,256,1024]{2,1,0:T(8,128)} %get-tuple-element.48.field_ref, bf16[2,1024,768]{2,1,0:T(8,128)(2,1)} %constant.228.clone.table_hi.col_hi, bf16[2,1024,768]{2,1,0:T(8,128)(2,1)} %constant.229.clone.table_lo.col_lo), custom_call_target="tpu_custom_call" | custom-call | flops 2415919104 | bytes 3670016 | tf_op jit(solution)/shard_map/column_forward/pallas_call | solution.py:136
  21.4 1.3 copy-done.15
  22.7 17.9 %row_forward.1 = (bf16[2,1536,768]{2,1,0:T(8,128)(2,1)}, bf16[2,1536,768]{2,1,0:T(8,128)(2,1)}) custom-call(s32[7]{0:T(128)} %stack.33.info_ref, f32[2,256,768]{2,1,0:T(8,128)} %column_forward.1.mine_ref, f32[2,256,1024]{2,1,0:T(8,128)} %copy-done.15, bf16[2,1024,768]{2,1,0:T(8,128)(2,1)} %constant.228.clone.table_hi.col_hi, ...), custom_call_target="tpu_custom_call" | custom-call | flops 7247757312 | bytes 12582912 | tf_op jit(solution)/shard_map/row_forward/pallas_call | solution.py:227
  40.6 36.8 %inverse.2 = (f32[16,2,128,128]{3,2,1,0:T(8,128)}, f32[16,2,128,128]{3,2,1,0:T(8,128)}) custom-call(s32[7]{0:T(128)} %stack.33.info_ref, s32[4,32]{1,0:T(4,128)} %constant.236.clone.slot_ref, s32[64,2]{1,0:T(8,128)} %copy.36.pos_ref, f32[2,64]{1,0:T(2,128)} %maximum_multiply_fusion.weight_ref, bf16[2,1536,768]{2,1,0:T(8,128)(2,1)} %get-tuple-element.55.spec_hi, ...), custom_call_target="tpu_custom_call" | custom-call | flops 21139292160 | bytes 17301504 | tf_op jit(solution)/shard_map/inverse/pallas_call | solution.py:396
  77.4 27.4 %inverse.3 = (f32[8,2,128,128]{3,2,1,0:T(8,128)}, f32[8,2,128,128]{3,2,1,0:T(8,128)}, bf16[2,640,768]{2,1,0:T(8,128)(2,1)}, bf16[2,640,768]{2,1,0:T(8,128)(2,1)}) custom-call(s32[7]{0:T(128)} %stack.33.info_ref, s32[4,16]{1,0:T(4,128)} %constant.241.clone.slot_ref, s32[64,2]{1,0:T(8,128)} %copy.36.pos_ref, f32[2,64]{1,0:T(2,128)} %maximum_multiply_fusion.weight_ref, ...), custom_call_target="tpu_custom_call" | custom-call | flops 15099494400 | bytes 17301504 | tf_op jit(solution)/shard_map/inverse/pallas_call | solution.py:396
  105.3 1.4 copy-done.1
  106.7 3.3 %spread_sum.3 = (f32[4,2,128,128]{3,2,1,0:T(8,128)}, f32[4,2,128,128]{3,2,1,0:T(8,128)}, f32[4,2,128,128]{3,2,1,0:T(8,128)}, f32[4,2,128,128]{3,2,1,0:T(8,128)}) custom-call(f32[4,4,2,128,128]{4,3,2,1,0:T(8,128)} %bitcast.41, f32[4,4,2,128,128]{4,3,2,1,0:T(8,128)} %bitcast.42), custom_call_target="tpu_custom_call" | custom-call | flops 524288 | bytes 6291456 | tf_op jit(solution)/shard_map/spread_sum/pallas_call | solution.py:551
  110.0 2.5 %collective-permute-start.6 = (f32[4,2,128,128]{3,2,1,0:T(8,128)}, f32[4,2,128,128]{3,2,1,0:T(8,128)S(1)}, u32[]{:S(2)}, u32[]{:S(2)}) collective-permute-start(f32[4,2,128,128]{3,2,1,0:T(8,128)} %get-tuple-element.74), channel_id=1, source_target_pairs={{0,8},{8,0},{16,24},{24,16},{1,9},{9,1},{17,25},{25,17},{2,10},{10... | collective-permute-start | bytes 1572872 | tf_op jit(solution)/shard_map/ppermute | solution.py:615
  112.5 1.5 collective-permute-start.7
  114.0 15.2 %column_inverse.1 = (f32[8,2,128,128]{3,2,1,0:T(8,128)}, f32[8,2,128,128]{3,2,1,0:T(8,128)}) custom-call(s32[7]{0:T(128)} %stack.33.info_ref, s32[4,16]{1,0:T(4,128)} %constant.242.clone.slot_ref, s32[64,2]{1,0:T(8,128)} %copy.36.pos_ref, f32[2,64]{1,0:T(2,128)} %maximum_multiply_fusion.weight_ref, bf16[2,640,768]{2,1,0:T(8,128)(2,1)} %get-tuple-element.65.rows_hi, ...), custom_call_target="tpu_custom_call" | custom-call | flops 6039797760 | bytes 6029312 | tf_op jit(solution)/shard_map/column_inverse/pallas_call | solution.py:467
  130.2 2.4 %spread_sum.5 = (f32[2,2,128,128]{3,2,1,0:T(8,128)}, f32[2,2,128,128]{3,2,1,0:T(8,128)}, f32[2,2,128,128]{3,2,1,0:T(8,128)}, f32[2,2,128,128]{3,2,1,0:T(8,128)}) custom-call(f32[4,2,2,128,128]{4,3,2,1,0:T(8,128)} %bitcast.45, f32[4,2,2,128,128]{4,3,2,1,0:T(8,128)} %bitcast.46), custom_call_target="tpu_custom_call" | custom-call | flops 262144 | bytes 3145728 | tf_op jit(solution)/shard_map/spread_sum/pallas_call | solution.py:551
  132.6 5.4 %collective-permute-done.7 = f32[4,2,128,128]{3,2,1,0:T(8,128)S(1)} collective-permute-done((f32[4,2,128,128]{3,2,1,0:T(8,128)}, f32[4,2,128,128]{3,2,1,0:T(8,128)S(1)}, u32[]{:S(2)}, u32[]{:S(2)}) %collective-permute-start.7) | collective-permute-done | bytes 524320 | tf_op jit(solution)/shard_map/ppermute | solution.py:615
  138.8 2.3 %sum_of.2 = f32[4,2,128,128]{3,2,1,0:T(8,128)} custom-call(f32[1,4,2,128,128]{4,3,2,1,0:T(8,128)} %bitcast.47, f32[1,4,2,128,128]{4,3,2,1,0:T(8,128)} %bitcast.48, f32[1,4,2,128,128]{4,3,2,1,0:T(8,128)} %bitcast.49, f32[1,4,2,128,128]{4,3,2,1,0:T(8,128)} %bitcast.24.refs_3_), custom_call_target="tpu_custom_call" | custom-call | flops 524288 | bytes 2621440 | tf_op jit(solution)/shard_map/sum_of/pallas_call | solution.py:526
  141.0 1.6 collective-permute-start.10
  143.2 1.5 collective-permute-start.12
  144.7 1.4 collective-permute-start.13
  146.1 5.7 %collective-permute-done.11 = f32[2,2,128,128]{3,2,1,0:T(8,128)S(1)} collective-permute-done((f32[2,2,128,128]{3,2,1,0:T(8,128)S(1)}, f32[2,2,128,128]{3,2,1,0:T(8,128)S(1)}, u32[]{:S(2)}, u32[]{:S(2)}) %collective-permute-start.11) | collective-permute-done | bytes 262176 | tf_op jit(solution)/shard_map/ppermute | solution.py:615
  151.8 2.8 %collective-permute-done.12 = f32[2,2,128,128]{3,2,1,0:T(8,128)S(1)} collective-permute-done((f32[2,2,128,128]{3,2,1,0:T(8,128)S(1)}, f32[2,2,128,128]{3,2,1,0:T(8,128)S(1)}, u32[]{:S(2)}, u32[]{:S(2)}) %collective-permute-start.12) | collective-permute-done | bytes 262176 | tf_op jit(solution)/shard_map/ppermute | solution.py:615
  154.6 1.8 collective-permute-done.13
  157.4 2.0 %sum_of.3 = f32[2,2,128,128]{3,2,1,0:T(8,128)} custom-call(f32[1,2,2,128,128]{4,3,2,1,0:T(8,128)} %bitcast.51, f32[1,2,2,128,128]{4,3,2,1,0:T(8,128)} %bitcast.56, f32[1,2,2,128,128]{4,3,2,1,0:T(8,128)} %bitcast.58, f32[1,2,2,128,128]{4,3,2,1,0:T(8,128)} %bitcast.59, f32[2,2,2,128,128]{4,3,2,1,0:T(8,128)} %bitcast.39), custom_call_target="tpu_custom_call" | custom-call | flops 262144 | bytes 1572864 | tf_op jit(solution)/shard_map/sum_of/pallas_call | solution.py:526
  159.4 2.6 %collective-permute-start.14 = (f32[2,2,128,128]{3,2,1,0:T(8,128)}, f32[2,2,128,128]{3,2,1,0:T(8,128)S(1)}, u32[]{:S(2)}, u32[]{:S(2)}) collective-permute-start(f32[2,2,128,128]{3,2,1,0:T(8,128)} %sum_of.3), channel_id=1, source_target_pairs={{0,4},{1,5},{2,6},{3,7},{4,0},{5,1},{6,2},{7,3},{8,12},{9,13},{10,... | collective-permute-start | bytes 786440 | tf_op jit(solution)/shard_map/ppermute | solution.py:615
  163.0 2.4 %spread_sum.4 = (f32[2,2,128,128]{3,2,1,0:T(8,128)}, f32[2,2,128,128]{3,2,1,0:T(8,128)}, f32[2,2,128,128]{3,2,1,0:T(8,128)}, f32[2,2,128,128]{3,2,1,0:T(8,128)}) custom-call(f32[4,2,2,128,128]{4,3,2,1,0:T(8,128)} %bitcast.43, f32[4,2,2,128,128]{4,3,2,1,0:T(8,128)} %bitcast.44), custom_call_target="tpu_custom_call" | custom-call | flops 262144 | bytes 3145728 | tf_op jit(solution)/shard_map/spread_sum/pallas_call | solution.py:551
  166.0 1.7 collective-permute-start.4
  167.8 1.1 collective-permute-start.5
  168.9 3.6 %collective-permute-done.14 = f32[2,2,128,128]{3,2,1,0:T(8,128)S(1)} collective-permute-done((f32[2,2,128,128]{3,2,1,0:T(8,128)}, f32[2,2,128,128]{3,2,1,0:T(8,128)S(1)}, u32[]{:S(2)}, u32[]{:S(2)}) %collective-permute-start.14) | collective-permute-done | bytes 262176 | tf_op jit(solution)/shard_map/ppermute | solution.py:615
  172.5 2.1 %collective-permute-done.3 = f32[2,2,128,128]{3,2,1,0:T(8,128)S(1)} collective-permute-done((f32[2,2,128,128]{3,2,1,0:T(8,128)}, f32[2,2,128,128]{3,2,1,0:T(8,128)S(1)}, u32[]{:S(2)}, u32[]{:S(2)}) %collective-permute-start.3) | collective-permute-done | bytes 262176 | tf_op jit(solution)/shard_map/ppermute | solution.py:615
  174.5 2.9 %collective-permute-done.4 = f32[2,2,128,128]{3,2,1,0:T(8,128)S(1)} collective-permute-done((f32[2,2,128,128]{3,2,1,0:T(8,128)}, f32[2,2,128,128]{3,2,1,0:T(8,128)S(1)}, u32[]{:S(2)}, u32[]{:S(2)}) %collective-permute-start.4) | collective-permute-done | bytes 262176 | tf_op jit(solution)/shard_map/ppermute | solution.py:615
  178.2 3.3 %power_of.1 = f32[2,128,128]{2,1,0:T(8,128)} custom-call(f32[1,2,2,128,128]{4,3,2,1,0:T(8,128)} %bitcast.53, f32[1,2,2,128,128]{4,3,2,1,0:T(8,128)} %bitcast.54, f32[1,2,2,128,128]{4,3,2,1,0:T(8,128)} %bitcast.55, f32[1,2,2,128,128]{4,3,2,1,0:T(8,128)} %bitcast.57, f32[2,2,2,128,128]{4,3,2,1,0:T(8,128)} %bitcast.40, f32[1,2,2,128,128]{4,3,2,1,0:T(8,128)} %bitcast.52, ...), custom_call_target="tpu_custom_call" | custom-call | tf_op jit(solution)/shard_map/power_of/pallas_call | solution.py:585
  181.6 1.0 copy.37
  182.6 8.0 %all_to_all.18 = f32[2,128,128]{2,0,1:T(2,128)S(1)} all-to-all(f32[2,128,128]{2,0,1:T(2,128)S(1)} %copy.37), channel_id=1, replica_groups=mesh['wave'=4,'row'=8] {'wave'}, dimensions={1} | all-to-all | bytes 262144 | tf_op jit(solution)/shard_map/all_to_all | solution.py:711
  (57 shorter events, 10.0 us)
Async XLA Ops:
  0.6 10.4 %copy-start.13 = (s32[64,2]{0,1:T(2,128)S(1)}, s32[64,2]{0,1:T(2,128)}, u32[]{:S(2)}) copy-start(s32[64,2]{0,1:T(2,128)} %param.34) | copy-start | bytes 1540
  0.6 11.1 %copy-start.14 = (s32[1,2]{1,0:T(1,128)S(1)}, s32[1,2]{1,0:T(1,128)}, u32[]{:S(2)}) copy-start(s32[1,2]{1,0:T(1,128)} %param.31) | copy-start | bytes 28
  9.2 12.2 %collective-permute-start = (f32[2,256,1024]{2,1,0:T(8,128)}, f32[2,256,1024]{2,1,0:T(8,128)S(1)}, u32[]{:S(2)}, u32[]{:S(2)}) collective-permute-start(f32[2,256,1024]{2,1,0:T(8,128)} %get-tuple-element.49), channel_id=1, source_target_pairs={{0,1},{1,0},{2,3},{3,2},{4,5},{5,4},{6,7},{7,6},{8,9},{9,8},{10,11... | collective-permute-start | bytes 6291464 | tf_op jit(solution)/shard_map/ppermute | solution.py:615
  21.4 1.3 copy-start.15
  77.4 27.9 %collective-permute-start.1 = (f32[16,2,128,128]{3,2,1,0:T(8,128)}, f32[16,2,128,128]{3,2,1,0:T(8,128)S(1)}, u32[]{:S(2)}, u32[]{:S(2)}) collective-permute-start(f32[16,2,128,128]{3,2,1,0:T(8,128)} %get-tuple-element.60), channel_id=1, source_target_pairs={{0,1},{1,0},{2,3},{3,2},{4,5},{5,4},{6,7},{7,6},{8,9},{9,8},{10,11... | collective-permute-start | bytes 6291464 | tf_op jit(solution)/shard_map/ppermute | solution.py:615
  104.8 24.4 %collective-permute-start.9 = (f32[8,2,128,128]{3,2,1,0:T(8,128)}, f32[8,2,128,128]{3,2,1,0:T(8,128)S(1)}, u32[]{:S(2)}, u32[]{:S(2)}) collective-permute-start(f32[8,2,128,128]{3,2,1,0:T(8,128)} %get-tuple-element.78), channel_id=1, source_target_pairs={{0,1},{1,0},{2,3},{3,2},{4,5},{5,4},{6,7},{7,6},{8,9},{9,8},{10,11... | collective-permute-start | bytes 3145736 | tf_op jit(solution)/shard_map/ppermute | solution.py:615
  105.3 1.4 copy-start.1
  110.0 22.6 %collective-permute-start.6 = (f32[4,2,128,128]{3,2,1,0:T(8,128)}, f32[4,2,128,128]{3,2,1,0:T(8,128)S(1)}, u32[]{:S(2)}, u32[]{:S(2)}) collective-permute-start(f32[4,2,128,128]{3,2,1,0:T(8,128)} %get-tuple-element.74), channel_id=1, source_target_pairs={{0,8},{8,0},{16,24},{24,16},{1,9},{9,1},{17,25},{25,17},{2,10},{10... | collective-permute-start | bytes 1572872 | tf_op jit(solution)/shard_map/ppermute | solution.py:615
  112.5 25.5 %collective-permute-start.7 = (f32[4,2,128,128]{3,2,1,0:T(8,128)}, f32[4,2,128,128]{3,2,1,0:T(8,128)S(1)}, u32[]{:S(2)}, u32[]{:S(2)}) collective-permute-start(f32[4,2,128,128]{3,2,1,0:T(8,128)} %get-tuple-element.75), channel_id=1, source_target_pairs={{0,16},{8,24},{16,0},{24,8},{1,17},{9,25},{17,1},{25,9},{2,18},{10... | collective-permute-start | bytes 1572872 | tf_op jit(solution)/shard_map/ppermute | solution.py:615
  114.0 24.0 %collective-permute-start.8 = (f32[4,2,128,128]{3,2,1,0:T(8,128)}, f32[4,2,128,128]{3,2,1,0:T(8,128)}, u32[]{:S(2)}, u32[]{:S(2)}) collective-permute-start(f32[4,2,128,128]{3,2,1,0:T(8,128)} %get-tuple-element.76), channel_id=1, source_target_pairs={{0,24},{8,16},{16,8},{24,0},{1,25},{9,17},{17,9},{25,1},{2,26},{10... | collective-permute-start | bytes 1572872 | tf_op jit(solution)/shard_map/ppermute | solution.py:615
  129.2 32.8 %collective-permute-start.2 = (f32[8,2,128,128]{3,2,1,0:T(8,128)}, f32[8,2,128,128]{3,2,1,0:T(8,128)S(1)}, u32[]{:S(2)}, u32[]{:S(2)}) collective-permute-start(f32[8,2,128,128]{3,2,1,0:T(8,128)} %get-tuple-element.68), channel_id=1, source_target_pairs={{0,1},{1,0},{2,3},{3,2},{4,5},{5,4},{6,7},{7,6},{8,9},{9,8},{10,11... | collective-permute-start | bytes 3145736 | tf_op jit(solution)/shard_map/ppermute | solution.py:615
  129.2 1.0 copy-start.3
  132.6 10.1 %copy-start.18 = (f32[2,2,128,128]{3,2,1,0:T(8,128)S(1)}, f32[2,2,128,128]{3,2,1,0:T(8,128)}, u32[]{:S(2)}) copy-start(f32[2,2,128,128]{3,2,1,0:T(8,128)} %get-tuple-element.88) | copy-start | bytes 786436
  132.6 10.6 %copy-start.17 = (f32[2,2,128,128]{3,2,1,0:T(8,128)S(1)}, f32[2,2,128,128]{3,2,1,0:T(8,128)}, u32[]{:S(2)}) copy-start(f32[2,2,128,128]{3,2,1,0:T(8,128)} %get-tuple-element.89) | copy-start | bytes 786436
  132.6 12.1 %copy-start.16 = (f32[2,2,128,128]{3,2,1,0:T(8,128)S(1)}, f32[2,2,128,128]{3,2,1,0:T(8,128)}, u32[]{:S(2)}) copy-start(f32[2,2,128,128]{3,2,1,0:T(8,128)} %get-tuple-element.90) | copy-start | bytes 786436
  132.6 5.4 %copy-start.4 = (f32[4,2,128,128]{3,2,1,0:T(8,128)}, f32[4,2,128,128]{3,2,1,0:T(8,128)S(1)}, u32[]{:S(2)}) copy-start(f32[4,2,128,128]{3,2,1,0:T(8,128)S(1)} %collective-permute-done.6) | copy-start | bytes 1572868
  138.0 0.8 copy-start.5
  141.0 15.4 %collective-permute-start.10 = (f32[4,2,128,128]{3,2,1,0:T(8,128)}, f32[4,2,128,128]{3,2,1,0:T(8,128)S(1)}, u32[]{:S(2)}, u32[]{:S(2)}) collective-permute-start(f32[4,2,128,128]{3,2,1,0:T(8,128)} %sum_of.2), channel_id=1, source_target_pairs={{0,2},{1,3},{2,0},{3,1},{4,6},{5,7},{6,4},{7,5},{8,10},{9,11},{10,... | collective-permute-start | bytes 1572872 | tf_op jit(solution)/shard_map/ppermute | solution.py:615
  142.6 9.2 %collective-permute-start.11 = (f32[2,2,128,128]{3,2,1,0:T(8,128)S(1)}, f32[2,2,128,128]{3,2,1,0:T(8,128)S(1)}, u32[]{:S(2)}, u32[]{:S(2)}) collective-permute-start(f32[2,2,128,128]{3,2,1,0:T(8,128)S(1)} %copy-done.18), channel_id=1, source_target_pairs={{0,8},{8,0},{16,24},{24,16},{1,9},{9,1},{17,25},{25,17},{2,10},{10... | collective-permute-start | bytes 786440 | tf_op jit(solution)/shard_map/ppermute | solution.py:615
  143.2 11.5 %collective-permute-start.12 = (f32[2,2,128,128]{3,2,1,0:T(8,128)S(1)}, f32[2,2,128,128]{3,2,1,0:T(8,128)S(1)}, u32[]{:S(2)}, u32[]{:S(2)}) collective-permute-start(f32[2,2,128,128]{3,2,1,0:T(8,128)S(1)} %copy-done.17), channel_id=1, source_target_pairs={{0,16},{8,24},{16,0},{24,8},{1,17},{9,25},{17,1},{25,9},{2,18},{10... | collective-permute-start | bytes 786440 | tf_op jit(solution)/shard_map/ppermute | solution.py:615
  144.7 11.8 %collective-permute-start.13 = (f32[2,2,128,128]{3,2,1,0:T(8,128)S(1)}, f32[2,2,128,128]{3,2,1,0:T(8,128)S(1)}, u32[]{:S(2)}, u32[]{:S(2)}) collective-permute-start(f32[2,2,128,128]{3,2,1,0:T(8,128)S(1)} %copy-done.16), channel_id=1, source_target_pairs={{0,24},{8,16},{16,8},{24,0},{1,25},{9,17},{17,9},{25,1},{2,26},{10... | collective-permute-start | bytes 786440 | tf_op jit(solution)/shard_map/ppermute | solution.py:615
  151.8 4.7 %copy-start.9 = (f32[2,2,128,128]{3,2,1,0:T(8,128)}, f32[2,2,128,128]{3,2,1,0:T(8,128)S(1)}, u32[]{:S(2)}) copy-start(f32[2,2,128,128]{3,2,1,0:T(8,128)S(1)} %collective-permute-done.11) | copy-start | bytes 786436
  154.6 1.9 copy-start.11
  156.5 0.9 copy-start
  159.4 13.0 %collective-permute-start.14 = (f32[2,2,128,128]{3,2,1,0:T(8,128)}, f32[2,2,128,128]{3,2,1,0:T(8,128)S(1)}, u32[]{:S(2)}, u32[]{:S(2)}) collective-permute-start(f32[2,2,128,128]{3,2,1,0:T(8,128)} %sum_of.3), channel_id=1, source_target_pairs={{0,4},{1,5},{2,6},{3,7},{4,0},{5,1},{6,2},{7,3},{8,12},{9,13},{10,... | collective-permute-start | bytes 786440 | tf_op jit(solution)/shard_map/ppermute | solution.py:615
  162.0 1.0 copy-start.2
  165.4 9.2 %collective-permute-start.3 = (f32[2,2,128,128]{3,2,1,0:T(8,128)}, f32[2,2,128,128]{3,2,1,0:T(8,128)S(1)}, u32[]{:S(2)}, u32[]{:S(2)}) collective-permute-start(f32[2,2,128,128]{3,2,1,0:T(8,128)} %get-tuple-element.70), channel_id=1, source_target_pairs={{0,8},{8,0},{16,24},{24,16},{1,9},{9,1},{17,25},{25,17},{2,10},{10... | collective-permute-start | bytes 786440 | tf_op jit(solution)/shard_map/ppermute | solution.py:615
  166.0 11.4 %collective-permute-start.4 = (f32[2,2,128,128]{3,2,1,0:T(8,128)}, f32[2,2,128,128]{3,2,1,0:T(8,128)S(1)}, u32[]{:S(2)}, u32[]{:S(2)}) collective-permute-start(f32[2,2,128,128]{3,2,1,0:T(8,128)} %get-tuple-element.71), channel_id=1, source_target_pairs={{0,16},{8,24},{16,0},{24,8},{1,17},{9,25},{17,1},{25,9},{2,18},{10... | collective-permute-start | bytes 786440 | tf_op jit(solution)/shard_map/ppermute | solution.py:615
  167.8 9.6 %collective-permute-start.5 = (f32[2,2,128,128]{3,2,1,0:T(8,128)}, f32[2,2,128,128]{3,2,1,0:T(8,128)S(1)}, u32[]{:S(2)}, u32[]{:S(2)}) collective-permute-start(f32[2,2,128,128]{3,2,1,0:T(8,128)} %get-tuple-element.72), channel_id=1, source_target_pairs={{0,24},{8,16},{16,8},{24,0},{1,25},{9,17},{17,9},{25,1},{2,26},{10... | collective-permute-start | bytes 786440 | tf_op jit(solution)/shard_map/ppermute | solution.py:615
  172.5 5.0 %copy-start.6 = (f32[2,2,128,128]{3,2,1,0:T(8,128)}, f32[2,2,128,128]{3,2,1,0:T(8,128)S(1)}, u32[]{:S(2)}) copy-start(f32[2,2,128,128]{3,2,1,0:T(8,128)S(1)} %collective-permute-done.14) | copy-start | bytes 786436
  174.5 2.9 %copy-start.7 = (f32[2,2,128,128]{3,2,1,0:T(8,128)}, f32[2,2,128,128]{3,2,1,0:T(8,128)S(1)}, u32[]{:S(2)}) copy-start(f32[2,2,128,128]{3,2,1,0:T(8,128)S(1)} %collective-permute-done.3) | copy-start | bytes 786436
  177.4 0.8 copy-start.10
  (2 other events, 1.4 us)

commit v5 on v4

--- a/solution.py
+++ b/solution.py
@@ -697,7 +697,10 @@
     odd_terms = [(array, 0, 1) for array in odd_arrays]
     upper_terms = over_waves(pieces)
     near = flip(sum_of(odd_terms, False), "row", 2)
-    lower_terms = over_waves(spread_sum(keep_lower, arrived_lower, wave_count))
+    pieces = spread_sum(keep_lower, arrived_lower, wave_count)
+    arrays, pieces = later([term[0] for term in upper_terms], pieces)
+    upper_terms = [(array, 0, 1) for array in arrays]
+    lower_terms = over_waves(pieces)
 
     bit = row_count // 2
     send = sum_of(upper_terms + [(near, 0, 2)], False)

time: 193 us -> 189 us (0.979)
  waiting for transfers between devices: 24.3 us -> 20.8 us
    ppermute x15, waiting for transfers between devices: 24.3 us -> 20.8 us  [flip(): return lax.ppermute(block, axis, [(i, i ^ bit) for i in range(count)])]
  transfers between devices with their start and end apart: 15 -> 15, of which waited for: 7 -> 6; matrix products, arithmetic and copies ran while one was open for 2% -> 2% of each run, Pallas kernels for 32% -> 32%
where the time goes in v5:
time: 189 us; the launch traced here: 188 us
  Pallas kernels  129 us (68%)
  waiting for transfers between devices  20.8 us (11%)
  starting transfers between devices  16.2 us (9%)
  local copies, waits for them, and re-layouts  10.8 us (6%)
  blocking collectives  8.02 us (4%)
  other arithmetic  1.9 us (1%)
    pallas_call x2, Pallas kernels, inverse(): pl.pallas_call(functools.partial(inverse_kernel, layout, cuts, base), out...  64.1 us
    ppermute x15, waiting for transfers between devices, flip(): return lax.ppermute(block, axis, [(i, i ^ bit) for i in range(count)])  20.8 us
    pallas_call x1, Pallas kernels, row_forward(): pl.pallas_call(row_forward_kernel, out_shape=(out, out), grid_spec=pltpu....  17.9 us
    ppermute x15, starting transfers between devices, flip(): return lax.ppermute(block, axis, [(i, i ^ bit) for i in range(count)])  16.2 us
    pallas_call x1, Pallas kernels, column_inverse(): pl.pallas_call(functools.partial(column_inverse_kernel, layout), out_shap...  15.2 us
    pallas_call x1, Pallas kernels, split_columns(): pl.pallas_call(split_kernel, out_shape=(out, out), grid_spec=pltpu.Prefet...  8.56 us
    pallas_call x3, Pallas kernels, spread_sum(): pl.pallas_call(spread_kernel, out_shape=[out] * count, grid=(size // step...  8.1 us
    all_to_all x1, blocking collectives, shards(): lax.all_to_all(power, 'wave', split_axis=1, concat_axis=0, tiled=True)  8.02 us
  transfers between devices with their start and end apart: 15, of which 6 were waited for; matrix products, arithmetic and copies ran while one was open for 2% of the time, Pallas kernels for 32%

profile of v5, /device:TPU:0, one launch (start us, length us, event | category | flops | bytes accessed | tf_op | source)
XLA Modules:
  0.0 187.8 jit_solution(4996055914219684874)
XLA Ops:
  0.6 8.6 %split_columns.1 = (f32[2,256,1024]{2,1,0:T(8,128)}, f32[2,256,1024]{2,1,0:T(8,128)}) custom-call(s32[7]{0:T(128)} %stack.33.info_ref, f32[2,1,256,2048]{3,2,1,0:T(8,128)} %wave_ref.1, f32[1,2,256,2048]{3,2,1,0:T(8,128)} %trans_ref.1), custom_call_target="tpu_custom_call" | custom-call | flops 10485760 | bytes 12582912 | tf_op jit(solution)/shard_map/split_columns/pallas_call | solution.py:96
  12.3 1.3 fusion.4
  14.3 7.1 %column_forward.1.mine_ref = f32[2,256,768]{2,1,0:T(8,128)} custom-call(s32[7]{0:T(128)} %stack.33.info_ref, f32[2,256,1024]{2,1,0:T(8,128)} %get-tuple-element.56.field_ref, bf16[2,1024,768]{2,1,0:T(8,128)(2,1)} %constant.228.clone.table_hi.col_hi, bf16[2,1024,768]{2,1,0:T(8,128)(2,1)} %constant.229.clone.table_lo.col_lo), custom_call_target="tpu_custom_call" | custom-call | flops 2415919104 | bytes 3670016 | tf_op jit(solution)/shard_map/column_forward/pallas_call | solution.py:136
  21.4 1.3 copy-done.15
  22.7 17.9 %row_forward.1 = (bf16[2,1536,768]{2,1,0:T(8,128)(2,1)}, bf16[2,1536,768]{2,1,0:T(8,128)(2,1)}) custom-call(s32[7]{0:T(128)} %stack.33.info_ref, f32[2,256,768]{2,1,0:T(8,128)} %column_forward.1.mine_ref, f32[2,256,1024]{2,1,0:T(8,128)} %copy-done.15, bf16[2,1024,768]{2,1,0:T(8,128)(2,1)} %constant.228.clone.table_hi.col_hi, ...), custom_call_target="tpu_custom_call" | custom-call | flops 7247757312 | bytes 12582912 | tf_op jit(solution)/shard_map/row_forward/pallas_call | solution.py:227
  40.6 36.8 %inverse.2 = (f32[16,2,128,128]{3,2,1,0:T(8,128)}, f32[16,2,128,128]{3,2,1,0:T(8,128)}) custom-call(s32[7]{0:T(128)} %stack.33.info_ref, s32[4,32]{1,0:T(4,128)} %constant.236.clone.slot_ref, s32[64,2]{1,0:T(8,128)} %copy.35.pos_ref, f32[2,64]{1,0:T(2,128)} %maximum_multiply_fusion.weight_ref, bf16[2,1536,768]{2,1,0:T(8,128)(2,1)} %get-tuple-element.63.spec_hi, ...), custom_call_target="tpu_custom_call" | custom-call | flops 21139292160 | bytes 17301504 | tf_op jit(solution)/shard_map/inverse/pallas_call | solution.py:396
  77.4 27.4 %inverse.3 = (f32[8,2,128,128]{3,2,1,0:T(8,128)}, f32[8,2,128,128]{3,2,1,0:T(8,128)}, bf16[2,640,768]{2,1,0:T(8,128)(2,1)}, bf16[2,640,768]{2,1,0:T(8,128)(2,1)}) custom-call(s32[7]{0:T(128)} %stack.33.info_ref, s32[4,16]{1,0:T(4,128)} %constant.241.clone.slot_ref, s32[64,2]{1,0:T(8,128)} %copy.35.pos_ref, f32[2,64]{1,0:T(2,128)} %maximum_multiply_fusion.weight_ref, ...), custom_call_target="tpu_custom_call" | custom-call | flops 15099494400 | bytes 17301504 | tf_op jit(solution)/shard_map/inverse/pallas_call | solution.py:396
  105.3 1.4 copy-done.1
  106.7 3.3 %spread_sum.3 = (f32[4,2,128,128]{3,2,1,0:T(8,128)}, f32[4,2,128,128]{3,2,1,0:T(8,128)}, f32[4,2,128,128]{3,2,1,0:T(8,128)}, f32[4,2,128,128]{3,2,1,0:T(8,128)}) custom-call(f32[4,4,2,128,128]{4,3,2,1,0:T(8,128)} %bitcast.41, f32[4,4,2,128,128]{4,3,2,1,0:T(8,128)} %bitcast.42), custom_call_target="tpu_custom_call" | custom-call | flops 524288 | bytes 6291456 | tf_op jit(solution)/shard_map/spread_sum/pallas_call | solution.py:551
  110.0 2.5 %collective-permute-start.2 = (f32[4,2,128,128]{3,2,1,0:T(8,128)}, f32[4,2,128,128]{3,2,1,0:T(8,128)S(1)}, u32[]{:S(2)}, u32[]{:S(2)}) collective-permute-start(f32[4,2,128,128]{3,2,1,0:T(8,128)} %get-tuple-element.74), channel_id=1, source_target_pairs={{0,8},{8,0},{16,24},{24,16},{1,9},{9,1},{17,25},{25,17},{2,10},{10... | collective-permute-start | bytes 1572872 | tf_op jit(solution)/shard_map/ppermute | solution.py:615
  112.5 1.5 collective-permute-start.3
  114.0 15.2 %column_inverse.1 = (f32[8,2,128,128]{3,2,1,0:T(8,128)}, f32[8,2,128,128]{3,2,1,0:T(8,128)}) custom-call(s32[7]{0:T(128)} %stack.33.info_ref, s32[4,16]{1,0:T(4,128)} %constant.242.clone.slot_ref, s32[64,2]{1,0:T(8,128)} %copy.35.pos_ref, f32[2,64]{1,0:T(2,128)} %maximum_multiply_fusion.weight_ref, bf16[2,640,768]{2,1,0:T(8,128)(2,1)} %get-tuple-element.87.rows_hi, ...), custom_call_target="tpu_custom_call" | custom-call | flops 6039797760 | bytes 6029312 | tf_op jit(solution)/shard_map/column_inverse/pallas_call | solution.py:467
  129.2 1.0 copy-done.3
  130.2 2.4 %spread_sum.4 = (f32[2,2,128,128]{3,2,1,0:T(8,128)}, f32[2,2,128,128]{3,2,1,0:T(8,128)}, f32[2,2,128,128]{3,2,1,0:T(8,128)}, f32[2,2,128,128]{3,2,1,0:T(8,128)}) custom-call(f32[4,2,2,128,128]{4,3,2,1,0:T(8,128)} %bitcast.44, f32[4,2,2,128,128]{4,3,2,1,0:T(8,128)} %bitcast.46), custom_call_target="tpu_custom_call" | custom-call | flops 262144 | bytes 3145728 | tf_op jit(solution)/shard_map/spread_sum/pallas_call | solution.py:551
  132.6 5.4 %collective-permute-done.3 = f32[4,2,128,128]{3,2,1,0:T(8,128)S(1)} collective-permute-done((f32[4,2,128,128]{3,2,1,0:T(8,128)}, f32[4,2,128,128]{3,2,1,0:T(8,128)S(1)}, u32[]{:S(2)}, u32[]{:S(2)}) %collective-permute-start.3) | collective-permute-done | bytes 524320 | tf_op jit(solution)/shard_map/ppermute | solution.py:615
  138.8 2.3 %sum_of.2 = f32[4,2,128,128]{3,2,1,0:T(8,128)} custom-call(f32[1,4,2,128,128]{4,3,2,1,0:T(8,128)} %bitcast.47, f32[1,4,2,128,128]{4,3,2,1,0:T(8,128)} %bitcast.48, f32[1,4,2,128,128]{4,3,2,1,0:T(8,128)} %bitcast.49, f32[1,4,2,128,128]{4,3,2,1,0:T(8,128)} %bitcast.24.refs_3_), custom_call_target="tpu_custom_call" | custom-call | flops 524288 | bytes 2621440 | tf_op jit(solution)/shard_map/sum_of/pallas_call | solution.py:526
  141.0 1.6 collective-permute-start.13
  143.2 1.5 collective-permute-start.7
  144.7 1.4 collective-permute-start.8
  147.1 2.4 %spread_sum.5 = (f32[2,2,128,128]{3,2,1,0:T(8,128)}, f32[2,2,128,128]{3,2,1,0:T(8,128)}, f32[2,2,128,128]{3,2,1,0:T(8,128)}, f32[2,2,128,128]{3,2,1,0:T(8,128)}) custom-call(f32[4,2,2,128,128]{4,3,2,1,0:T(8,128)} %bitcast.43, f32[4,2,2,128,128]{4,3,2,1,0:T(8,128)} %bitcast.45), custom_call_target="tpu_custom_call" | custom-call | flops 262144 | bytes 3145728 | tf_op jit(solution)/shard_map/spread_sum/pallas_call | solution.py:551
  149.5 2.3 %collective-permute-done.6 = f32[2,2,128,128]{3,2,1,0:T(8,128)S(1)} collective-permute-done((f32[2,2,128,128]{3,2,1,0:T(8,128)S(1)}, f32[2,2,128,128]{3,2,1,0:T(8,128)S(1)}, u32[]{:S(2)}, u32[]{:S(2)}) %collective-permute-start.6) | collective-permute-done | bytes 262176 | tf_op jit(solution)/shard_map/ppermute | solution.py:615
  151.8 2.8 %collective-permute-done.7 = f32[2,2,128,128]{3,2,1,0:T(8,128)S(1)} collective-permute-done((f32[2,2,128,128]{3,2,1,0:T(8,128)S(1)}, f32[2,2,128,128]{3,2,1,0:T(8,128)S(1)}, u32[]{:S(2)}, u32[]{:S(2)}) %collective-permute-start.7) | collective-permute-done | bytes 262176 | tf_op jit(solution)/shard_map/ppermute | solution.py:615
  154.6 1.8 collective-permute-done.8
  157.3 2.0 %sum_of.3 = f32[2,2,128,128]{3,2,1,0:T(8,128)} custom-call(f32[1,2,2,128,128]{4,3,2,1,0:T(8,128)} %bitcast.51, f32[1,2,2,128,128]{4,3,2,1,0:T(8,128)} %bitcast.53, f32[1,2,2,128,128]{4,3,2,1,0:T(8,128)} %bitcast.54, f32[1,2,2,128,128]{4,3,2,1,0:T(8,128)} %bitcast.55, f32[2,2,2,128,128]{4,3,2,1,0:T(8,128)} %bitcast.39), custom_call_target="tpu_custom_call" | custom-call | flops 262144 | bytes 1572864 | tf_op jit(solution)/shard_map/sum_of/pallas_call | solution.py:526
  159.4 2.6 %collective-permute-start.14 = (f32[2,2,128,128]{3,2,1,0:T(8,128)}, f32[2,2,128,128]{3,2,1,0:T(8,128)S(1)}, u32[]{:S(2)}, u32[]{:S(2)}) collective-permute-start(f32[2,2,128,128]{3,2,1,0:T(8,128)} %sum_of.3), channel_id=1, source_target_pairs={{0,4},{1,5},{2,6},{3,7},{4,0},{5,1},{6,2},{7,3},{8,12},{9,13},{10,... | collective-permute-start | bytes 786440 | tf_op jit(solution)/shard_map/ppermute | solution.py:615
  162.6 1.7 collective-permute-start.11
  164.4 1.1 collective-permute-start.12
  165.5 7.0 %collective-permute-done.14 = f32[2,2,128,128]{3,2,1,0:T(8,128)S(1)} collective-permute-done((f32[2,2,128,128]{3,2,1,0:T(8,128)}, f32[2,2,128,128]{3,2,1,0:T(8,128)S(1)}, u32[]{:S(2)}, u32[]{:S(2)}) %collective-permute-start.14) | collective-permute-done | bytes 262176 | tf_op jit(solution)/shard_map/ppermute | solution.py:615
  172.4 1.5 collective-permute-done.11
  174.7 3.3 %power_of.1 = f32[2,128,128]{2,1,0:T(8,128)} custom-call(f32[1,2,2,128,128]{4,3,2,1,0:T(8,128)} %bitcast.52, f32[1,2,2,128,128]{4,3,2,1,0:T(8,128)} %bitcast.57, f32[1,2,2,128,128]{4,3,2,1,0:T(8,128)} %bitcast.58, f32[1,2,2,128,128]{4,3,2,1,0:T(8,128)} %bitcast.59, f32[2,2,2,128,128]{4,3,2,1,0:T(8,128)} %bitcast.40, f32[1,2,2,128,128]{4,3,2,1,0:T(8,128)} %bitcast.56, ...), custom_call_target="tpu_custom_call" | custom-call | tf_op jit(solution)/shard_map/power_of/pallas_call | solution.py:585
  178.1 1.0 copy.37
  179.1 8.0 %all_to_all.18 = f32[2,128,128]{2,0,1:T(2,128)S(1)} all-to-all(f32[2,128,128]{2,0,1:T(2,128)S(1)} %copy.37), channel_id=1, replica_groups=mesh['wave'=4,'row'=8] {'wave'}, dimensions={1} | all-to-all | bytes 262144 | tf_op jit(solution)/shard_map/all_to_all | solution.py:714
  (57 shorter events, 8.9 us)
Async XLA Ops:
  0.6 10.4 %copy-start.13 = (s32[64,2]{0,1:T(2,128)S(1)}, s32[64,2]{0,1:T(2,128)}, u32[]{:S(2)}) copy-start(s32[64,2]{0,1:T(2,128)} %param.34) | copy-start | bytes 1540
  0.6 11.1 %copy-start.14 = (s32[1,2]{1,0:T(1,128)S(1)}, s32[1,2]{1,0:T(1,128)}, u32[]{:S(2)}) copy-start(s32[1,2]{1,0:T(1,128)} %param.31) | copy-start | bytes 28
  9.2 12.2 %collective-permute-start = (f32[2,256,1024]{2,1,0:T(8,128)}, f32[2,256,1024]{2,1,0:T(8,128)S(1)}, u32[]{:S(2)}, u32[]{:S(2)}) collective-permute-start(f32[2,256,1024]{2,1,0:T(8,128)} %get-tuple-element.57), channel_id=1, source_target_pairs={{0,1},{1,0},{2,3},{3,2},{4,5},{5,4},{6,7},{7,6},{8,9},{9,8},{10,11... | collective-permute-start | bytes 6291464 | tf_op jit(solution)/shard_map/ppermute | solution.py:615
  21.4 1.3 copy-start.15
  77.4 27.9 %collective-permute-start.1 = (f32[16,2,128,128]{3,2,1,0:T(8,128)}, f32[16,2,128,128]{3,2,1,0:T(8,128)S(1)}, u32[]{:S(2)}, u32[]{:S(2)}) collective-permute-start(f32[16,2,128,128]{3,2,1,0:T(8,128)} %get-tuple-element.68), channel_id=1, source_target_pairs={{0,1},{1,0},{2,3},{3,2},{4,5},{5,4},{6,7},{7,6},{8,9},{9,8},{10,11... | collective-permute-start | bytes 6291464 | tf_op jit(solution)/shard_map/ppermute | solution.py:615
  104.8 24.4 %collective-permute-start.5 = (f32[8,2,128,128]{3,2,1,0:T(8,128)}, f32[8,2,128,128]{3,2,1,0:T(8,128)S(1)}, u32[]{:S(2)}, u32[]{:S(2)}) collective-permute-start(f32[8,2,128,128]{3,2,1,0:T(8,128)} %get-tuple-element.78), channel_id=1, source_target_pairs={{0,1},{1,0},{2,3},{3,2},{4,5},{5,4},{6,7},{7,6},{8,9},{9,8},{10,11... | collective-permute-start | bytes 3145736 | tf_op jit(solution)/shard_map/ppermute | solution.py:615
  105.3 1.4 copy-start.1
  110.0 22.6 %collective-permute-start.2 = (f32[4,2,128,128]{3,2,1,0:T(8,128)}, f32[4,2,128,128]{3,2,1,0:T(8,128)S(1)}, u32[]{:S(2)}, u32[]{:S(2)}) collective-permute-start(f32[4,2,128,128]{3,2,1,0:T(8,128)} %get-tuple-element.74), channel_id=1, source_target_pairs={{0,8},{8,0},{16,24},{24,16},{1,9},{9,1},{17,25},{25,17},{2,10},{10... | collective-permute-start | bytes 1572872 | tf_op jit(solution)/shard_map/ppermute | solution.py:615
  112.5 25.5 %collective-permute-start.3 = (f32[4,2,128,128]{3,2,1,0:T(8,128)}, f32[4,2,128,128]{3,2,1,0:T(8,128)S(1)}, u32[]{:S(2)}, u32[]{:S(2)}) collective-permute-start(f32[4,2,128,128]{3,2,1,0:T(8,128)} %get-tuple-element.75), channel_id=1, source_target_pairs={{0,16},{8,24},{16,0},{24,8},{1,17},{9,25},{17,1},{25,9},{2,18},{10... | collective-permute-start | bytes 1572872 | tf_op jit(solution)/shard_map/ppermute | solution.py:615
  114.0 24.0 %collective-permute-start.4 = (f32[4,2,128,128]{3,2,1,0:T(8,128)}, f32[4,2,128,128]{3,2,1,0:T(8,128)}, u32[]{:S(2)}, u32[]{:S(2)}) collective-permute-start(f32[4,2,128,128]{3,2,1,0:T(8,128)} %get-tuple-element.76), channel_id=1, source_target_pairs={{0,24},{8,16},{16,8},{24,0},{1,25},{9,17},{17,9},{25,1},{2,26},{10... | collective-permute-start | bytes 1572872 | tf_op jit(solution)/shard_map/ppermute | solution.py:615
  129.2 16.9 %collective-permute-start.9 = (f32[8,2,128,128]{3,2,1,0:T(8,128)}, f32[8,2,128,128]{3,2,1,0:T(8,128)S(1)}, u32[]{:S(2)}, u32[]{:S(2)}) collective-permute-start(f32[8,2,128,128]{3,2,1,0:T(8,128)} %get-tuple-element.90), channel_id=1, source_target_pairs={{0,1},{1,0},{2,3},{3,2},{4,5},{5,4},{6,7},{7,6},{8,9},{9,8},{10,11... | collective-permute-start | bytes 3145736 | tf_op jit(solution)/shard_map/ppermute | solution.py:615
  129.2 1.0 copy-start.3
  132.6 10.1 %copy-start.18 = (f32[2,2,128,128]{3,2,1,0:T(8,128)S(1)}, f32[2,2,128,128]{3,2,1,0:T(8,128)}, u32[]{:S(2)}) copy-start(f32[2,2,128,128]{3,2,1,0:T(8,128)} %get-tuple-element.84) | copy-start | bytes 786436
  132.6 10.6 %copy-start.17 = (f32[2,2,128,128]{3,2,1,0:T(8,128)S(1)}, f32[2,2,128,128]{3,2,1,0:T(8,128)}, u32[]{:S(2)}) copy-start(f32[2,2,128,128]{3,2,1,0:T(8,128)} %get-tuple-element.85) | copy-start | bytes 786436
  132.6 12.1 %copy-start.16 = (f32[2,2,128,128]{3,2,1,0:T(8,128)S(1)}, f32[2,2,128,128]{3,2,1,0:T(8,128)}, u32[]{:S(2)}) copy-start(f32[2,2,128,128]{3,2,1,0:T(8,128)} %get-tuple-element.86) | copy-start | bytes 786436
  132.6 5.4 %copy-start.4 = (f32[4,2,128,128]{3,2,1,0:T(8,128)}, f32[4,2,128,128]{3,2,1,0:T(8,128)S(1)}, u32[]{:S(2)}) copy-start(f32[4,2,128,128]{3,2,1,0:T(8,128)S(1)} %collective-permute-done.2) | copy-start | bytes 1572868
  138.0 0.8 copy-start.5
  141.0 15.4 %collective-permute-start.13 = (f32[4,2,128,128]{3,2,1,0:T(8,128)}, f32[4,2,128,128]{3,2,1,0:T(8,128)S(1)}, u32[]{:S(2)}, u32[]{:S(2)}) collective-permute-start(f32[4,2,128,128]{3,2,1,0:T(8,128)} %sum_of.2), channel_id=1, source_target_pairs={{0,2},{1,3},{2,0},{3,1},{4,6},{5,7},{6,4},{7,5},{8,10},{9,11},{10,... | collective-permute-start | bytes 1572872 | tf_op jit(solution)/shard_map/ppermute | solution.py:615
  142.6 9.2 %collective-permute-start.6 = (f32[2,2,128,128]{3,2,1,0:T(8,128)S(1)}, f32[2,2,128,128]{3,2,1,0:T(8,128)S(1)}, u32[]{:S(2)}, u32[]{:S(2)}) collective-permute-start(f32[2,2,128,128]{3,2,1,0:T(8,128)S(1)} %copy-done.18), channel_id=1, source_target_pairs={{0,8},{8,0},{16,24},{24,16},{1,9},{9,1},{17,25},{25,17},{2,10},{10... | collective-permute-start | bytes 786440 | tf_op jit(solution)/shard_map/ppermute | solution.py:615
  143.2 11.5 %collective-permute-start.7 = (f32[2,2,128,128]{3,2,1,0:T(8,128)S(1)}, f32[2,2,128,128]{3,2,1,0:T(8,128)S(1)}, u32[]{:S(2)}, u32[]{:S(2)}) collective-permute-start(f32[2,2,128,128]{3,2,1,0:T(8,128)S(1)} %copy-done.17), channel_id=1, source_target_pairs={{0,16},{8,24},{16,0},{24,8},{1,17},{9,25},{17,1},{25,9},{2,18},{10... | collective-permute-start | bytes 786440 | tf_op jit(solution)/shard_map/ppermute | solution.py:615
  144.7 11.8 %collective-permute-start.8 = (f32[2,2,128,128]{3,2,1,0:T(8,128)S(1)}, f32[2,2,128,128]{3,2,1,0:T(8,128)S(1)}, u32[]{:S(2)}, u32[]{:S(2)}) collective-permute-start(f32[2,2,128,128]{3,2,1,0:T(8,128)S(1)} %copy-done.16), channel_id=1, source_target_pairs={{0,24},{8,16},{16,8},{24,0},{1,25},{9,17},{17,9},{25,1},{2,26},{10... | collective-permute-start | bytes 786440 | tf_op jit(solution)/shard_map/ppermute | solution.py:615
  146.1 1.0 copy-start.2
  151.8 4.7 %copy-start.6 = (f32[2,2,128,128]{3,2,1,0:T(8,128)}, f32[2,2,128,128]{3,2,1,0:T(8,128)S(1)}, u32[]{:S(2)}) copy-start(f32[2,2,128,128]{3,2,1,0:T(8,128)S(1)} %collective-permute-done.6) | copy-start | bytes 786436
  154.6 1.9 copy-start.7
  156.5 0.9 copy-start
  159.4 13.0 %collective-permute-start.14 = (f32[2,2,128,128]{3,2,1,0:T(8,128)}, f32[2,2,128,128]{3,2,1,0:T(8,128)S(1)}, u32[]{:S(2)}, u32[]{:S(2)}) collective-permute-start(f32[2,2,128,128]{3,2,1,0:T(8,128)} %sum_of.3), channel_id=1, source_target_pairs={{0,4},{1,5},{2,6},{3,7},{4,0},{5,1},{6,2},{7,3},{8,12},{9,13},{10,... | collective-permute-start | bytes 786440 | tf_op jit(solution)/shard_map/ppermute | solution.py:615
  162.0 10.5 %collective-permute-start.10 = (f32[2,2,128,128]{3,2,1,0:T(8,128)}, f32[2,2,128,128]{3,2,1,0:T(8,128)S(1)}, u32[]{:S(2)}, u32[]{:S(2)}) collective-permute-start(f32[2,2,128,128]{3,2,1,0:T(8,128)} %get-tuple-element.96), channel_id=1, source_target_pairs={{0,8},{8,0},{16,24},{24,16},{1,9},{9,1},{17,25},{25,17},{2,10},{10... | collective-permute-start | bytes 786440 | tf_op jit(solution)/shard_map/ppermute | solution.py:615
  162.6 11.3 %collective-permute-start.11 = (f32[2,2,128,128]{3,2,1,0:T(8,128)}, f32[2,2,128,128]{3,2,1,0:T(8,128)S(1)}, u32[]{:S(2)}, u32[]{:S(2)}) collective-permute-start(f32[2,2,128,128]{3,2,1,0:T(8,128)} %get-tuple-element.97), channel_id=1, source_target_pairs={{0,16},{8,24},{16,0},{24,8},{1,17},{9,25},{17,1},{25,9},{2,18},{10... | collective-permute-start | bytes 786440 | tf_op jit(solution)/shard_map/ppermute | solution.py:615
  164.4 9.6 %collective-permute-start.12 = (f32[2,2,128,128]{3,2,1,0:T(8,128)}, f32[2,2,128,128]{3,2,1,0:T(8,128)S(1)}, u32[]{:S(2)}, u32[]{:S(2)}) collective-permute-start(f32[2,2,128,128]{3,2,1,0:T(8,128)} %get-tuple-element.98), channel_id=1, source_target_pairs={{0,24},{8,16},{16,8},{24,0},{1,25},{9,17},{17,9},{25,1},{2,26},{10... | collective-permute-start | bytes 786440 | tf_op jit(solution)/shard_map/ppermute | solution.py:615
  172.4 1.5 copy-start.9
  172.4 1.5 copy-start.10
  173.9 0.8 copy-start.12
  (2 other events, 1.4 us)

commit v6 on v5

--- a/solution.py
+++ b/solution.py
@@ -24,6 +24,7 @@
 FREQS = BLOCKS * LANES
 COL_TILES = FOLD // PAIR
 CUT_STEPS = 4
+VMEM_BYTES = 67043328
 
 
 def angles_of(first, second):
@@ -152,6 +153,7 @@
             bytes_accessed=8 * rows * (FOLD + DEPTH),
             transcendentals=0,
         ),
+        compiler_params=pltpu.CompilerParams(vmem_limit_bytes=VMEM_BYTES),
         name="column_forward",
     )(info, field, *table)
 
@@ -251,6 +253,7 @@
             bytes_accessed=16 * rows * DEPTH + 16 * DEPTH * DEPTH,
             transcendentals=0,
         ),
+        compiler_params=pltpu.CompilerParams(vmem_limit_bytes=VMEM_BYTES),
         name="row_forward",
     )(
         info, mine, theirs, *column_forward_table(), *table, jnp.asarray(down),
@@ -486,6 +489,7 @@
             bytes_accessed=8 * segments * height * DEPTH + 16 * count * WINDOW * WINDOW,
             transcendentals=0,
         ),
+        compiler_params=pltpu.CompilerParams(vmem_limit_bytes=VMEM_BYTES),
         name="column_inverse",
     )(
         info, jnp.asarray(slots), positions, weights, *rows, *table,
@@ -532,6 +536,7 @@
         cost_estimate=pl.CostEstimate(
             flops=size, bytes_accessed=(len(terms) + 1) * size, transcendentals=0
         ),
+        compiler_params=pltpu.CompilerParams(vmem_limit_bytes=VMEM_BYTES),
         name="sum_of",
     )(*arrays)
 
@@ -557,6 +562,7 @@
         cost_estimate=pl.CostEstimate(
             flops=first.size, bytes_accessed=12 * first.size, transcendentals=0
         ),
+        compiler_params=pltpu.CompilerParams(vmem_limit_bytes=VMEM_BYTES),
         name="spread_sum",
     )(*(value.reshape((count, size) + tail) for value in (first, second)))
 
@@ -595,6 +601,7 @@
             pl.BlockSpec(along.shape, lambda i: (0, 0)),
         ],
         out_specs=pl.BlockSpec((1, WINDOW, WINDOW), lambda i: (i, 0, 0)),
+        compiler_params=pltpu.CompilerParams(vmem_limit_bytes=VMEM_BYTES),
         name="power_of",
     )(
         *(array.reshape((parts, count) + tail) for array, _, parts in terms),

time: 189 us -> 185 us (0.979)
  local copies, waits for them, and re-layouts: 10.8 us -> 3.71 us
  waiting for transfers between devices: 20.8 us -> 23.8 us
    unnamed x39 -> x5, local copies, waits for them, and re-layouts: 7.82 us -> 0.72 us
    ppermute x15, waiting for transfers between devices: 20.8 us -> 23.8 us  [flip(): return lax.ppermute(block, axis, [(i, i ^ bit) for i in range(count)])]
  transfers between devices with their start and end apart: 15 -> 15, of which waited for: 6 -> 5; matrix products, arithmetic and copies ran while one was open for 2% -> 2% of each run, Pallas kernels for 32% -> 33%
where the time goes in v6:
time: 185 us; the launch traced here: 184 us
  Pallas kernels  129 us (70%)
  waiting for transfers between devices  23.8 us (13%)
  starting transfers between devices  16.2 us (9%)
  blocking collectives  7.75 us (4%)
  local copies, waits for them, and re-layouts  3.71 us (2%)
  other arithmetic  1.97 us (1%)
    pallas_call x2, Pallas kernels, inverse(): pl.pallas_call(functools.partial(inverse_kernel, layout, cuts, base), out...  64.1 us
    ppermute x15, waiting for transfers between devices, flip(): return lax.ppermute(block, axis, [(i, i ^ bit) for i in range(count)])  23.8 us
    pallas_call x1, Pallas kernels, row_forward(): pl.pallas_call(row_forward_kernel, out_shape=(out, out), grid_spec=pltpu....  17.9 us
    ppermute x15, starting transfers between devices, flip(): return lax.ppermute(block, axis, [(i, i ^ bit) for i in range(count)])  16.2 us
    pallas_call x1, Pallas kernels, column_inverse(): pl.pallas_call(functools.partial(column_inverse_kernel, layout), out_shap...  15.1 us
    pallas_call x1, Pallas kernels, split_columns(): pl.pallas_call(split_kernel, out_shape=(out, out), grid_spec=pltpu.Prefet...  8.68 us
    pallas_call x3, Pallas kernels, spread_sum(): pl.pallas_call(spread_kernel, out_shape=[out] * count, grid=(size // step...  8.14 us
    all_to_all x1, blocking collectives, shards(): lax.all_to_all(power, 'wave', split_axis=1, concat_axis=0, tiled=True)  7.75 us
  transfers between devices with their start and end apart: 15, of which 5 were waited for; matrix products, arithmetic and copies ran while one was open for 2% of the time, Pallas kernels for 33%

profile of v6, /device:TPU:0, one launch (start us, length us, event | category | flops | bytes accessed | tf_op | source)
XLA Modules:
  0.0 183.6 jit_solution(9448866528615868347)
XLA Ops:
  0.6 8.7 %split_columns.1 = (f32[2,256,1024]{2,1,0:T(8,128)}, f32[2,256,1024]{2,1,0:T(8,128)}) custom-call(s32[7]{0:T(128)} %stack.33.info_ref, f32[2,1,256,2048]{3,2,1,0:T(8,128)} %wave_ref.1, f32[1,2,256,2048]{3,2,1,0:T(8,128)} %trans_ref.1), custom_call_target="tpu_custom_call" | custom-call | flops 10485760 | bytes 12582912 | tf_op jit(solution)/shard_map/split_columns/pallas_call | solution.py:97
  11.1 0.7 copy.35.pos_ref
  11.8 0.7 fusion.6
  12.5 1.4 fusion.4
  14.5 7.1 %column_forward.1.mine_ref = f32[2,256,768]{2,1,0:T(8,128)} custom-call(s32[7]{0:T(128)} %stack.33.info_ref, f32[2,256,1024]{2,1,0:T(8,128)} %get-tuple-element.56.field_ref, bf16[2,1024,768]{2,1,0:T(8,128)(2,1)} %constant.228.clone.table_hi.col_hi, bf16[2,1024,768]{2,1,0:T(8,128)(2,1)} %constant.229.clone.table_lo.col_lo), custom_call_target="tpu_custom_call" | custom-call | flops 2415919104 | bytes 3670016 | tf_op jit(solution)/shard_map/column_forward/pallas_call | solution.py:137
  21.6 17.9 %row_forward.1 = (bf16[2,1536,768]{2,1,0:T(8,128)(2,1)}, bf16[2,1536,768]{2,1,0:T(8,128)(2,1)}) custom-call(s32[7]{0:T(128)} %stack.33.info_ref, f32[2,256,768]{2,1,0:T(8,128)} %column_forward.1.mine_ref, f32[2,256,1024]{2,1,0:T(8,128)} %collective-permute-done.theirs_ref, bf16[2,1024,768]{2,1,0:T(8,128)(2,1)} %constant.228.clone.table_hi.col_hi, ...), custom_call_target="tpu_custom_call" | custom-call | flops 7247757312 | bytes 12582912 | tf_op jit(solution)/shard_map/row_forward/pallas_call | solution.py:229
  39.6 36.8 %inverse.2 = (f32[16,2,128,128]{3,2,1,0:T(8,128)}, f32[16,2,128,128]{3,2,1,0:T(8,128)}) custom-call(s32[7]{0:T(128)} %stack.33.info_ref, s32[4,32]{1,0:T(4,128)} %constant.236.clone.slot_ref, s32[64,2]{1,0:T(8,128)} %copy.35.pos_ref, f32[2,64]{1,0:T(2,128)} %maximum_multiply_fusion.weight_ref, bf16[2,1536,768]{2,1,0:T(8,128)(2,1)} %get-tuple-element.63.spec_hi, ...), custom_call_target="tpu_custom_call" | custom-call | flops 21139292160 | bytes 17301504 | tf_op jit(solution)/shard_map/inverse/pallas_call | solution.py:399
  76.4 27.4 %inverse.3 = (f32[8,2,128,128]{3,2,1,0:T(8,128)}, f32[8,2,128,128]{3,2,1,0:T(8,128)}, bf16[2,640,768]{2,1,0:T(8,128)(2,1)}, bf16[2,640,768]{2,1,0:T(8,128)(2,1)}) custom-call(s32[7]{0:T(128)} %stack.33.info_ref, s32[4,16]{1,0:T(4,128)} %constant.241.clone.slot_ref, s32[64,2]{1,0:T(8,128)} %copy.35.pos_ref, f32[2,64]{1,0:T(2,128)} %maximum_multiply_fusion.weight_ref, ...), custom_call_target="tpu_custom_call" | custom-call | flops 15099494400 | bytes 17301504 | tf_op jit(solution)/shard_map/inverse/pallas_call | solution.py:399
  104.2 3.3 %spread_sum.3 = (f32[4,2,128,128]{3,2,1,0:T(8,128)}, f32[4,2,128,128]{3,2,1,0:T(8,128)}, f32[4,2,128,128]{3,2,1,0:T(8,128)}, f32[4,2,128,128]{3,2,1,0:T(8,128)}) custom-call(f32[4,4,2,128,128]{4,3,2,1,0:T(8,128)} %bitcast.39, f32[4,4,2,128,128]{4,3,2,1,0:T(8,128)} %bitcast.12.second_ref), custom_call_target="tpu_custom_call" | custom-call | flops 524288 | bytes 6291456 | tf_op jit(solution)/shard_map/spread_sum/pallas_call | solution.py:556
  107.6 2.5 %collective-permute-start.2 = (f32[4,2,128,128]{3,2,1,0:T(8,128)}, f32[4,2,128,128]{3,2,1,0:T(8,128)}, u32[]{:S(2)}, u32[]{:S(2)}) collective-permute-start(f32[4,2,128,128]{3,2,1,0:T(8,128)} %get-tuple-element.74), channel_id=1, source_target_pairs={{0,8},{8,0},{16,24},{24,16},{1,9},{9,1},{17,25},{25,17},{2,10},{10... | collective-permute-start | bytes 1572872 | tf_op jit(solution)/shard_map/ppermute | solution.py:622
  110.1 1.5 collective-permute-start.3
  111.6 15.1 %column_inverse.1 = (f32[8,2,128,128]{3,2,1,0:T(8,128)}, f32[8,2,128,128]{3,2,1,0:T(8,128)}) custom-call(s32[7]{0:T(128)} %stack.33.info_ref, s32[4,16]{1,0:T(4,128)} %constant.242.clone.slot_ref, s32[64,2]{1,0:T(8,128)} %copy.35.pos_ref, f32[2,64]{1,0:T(2,128)} %maximum_multiply_fusion.weight_ref, bf16[2,640,768]{2,1,0:T(8,128)(2,1)} %get-tuple-element.87.rows_hi, ...), custom_call_target="tpu_custom_call" | custom-call | flops 6039797760 | bytes 6029312 | tf_op jit(solution)/shard_map/column_inverse/pallas_call | solution.py:470
  126.7 2.4 %spread_sum.4 = (f32[2,2,128,128]{3,2,1,0:T(8,128)}, f32[2,2,128,128]{3,2,1,0:T(8,128)}, f32[2,2,128,128]{3,2,1,0:T(8,128)}, f32[2,2,128,128]{3,2,1,0:T(8,128)}) custom-call(f32[4,2,2,128,128]{4,3,2,1,0:T(8,128)} %bitcast.41, f32[4,2,2,128,128]{4,3,2,1,0:T(8,128)} %bitcast.14.second_ref), custom_call_target="tpu_custom_call" | custom-call | flops 262144 | bytes 3145728 | tf_op jit(solution)/shard_map/spread_sum/pallas_call | solution.py:556
  129.1 6.5 %collective-permute-done.3 = f32[4,2,128,128]{3,2,1,0:T(8,128)} collective-permute-done((f32[4,2,128,128]{3,2,1,0:T(8,128)}, f32[4,2,128,128]{3,2,1,0:T(8,128)}, u32[]{:S(2)}, u32[]{:S(2)}) %collective-permute-start.3) | collective-permute-done | bytes 524320 | tf_op jit(solution)/shard_map/ppermute | solution.py:622
  135.6 2.3 %sum_of.2 = f32[4,2,128,128]{3,2,1,0:T(8,128)} custom-call(f32[1,4,2,128,128]{4,3,2,1,0:T(8,128)} %bitcast.42, f32[1,4,2,128,128]{4,3,2,1,0:T(8,128)} %bitcast.22.refs_1_, f32[1,4,2,128,128]{4,3,2,1,0:T(8,128)} %bitcast.23.refs_2_, f32[1,4,2,128,128]{4,3,2,1,0:T(8,128)} %bitcast.24.refs_3_), custom_call_target="tpu_custom_call" | custom-call | flops 524288 | bytes 2621440 | tf_op jit(solution)/shard_map/sum_of/pallas_call | solution.py:530
  137.9 1.6 collective-permute-start.13
  139.5 1.2 collective-permute-start.6
  140.7 0.8 collective-permute-start.7
  141.5 1.4 collective-permute-start.8
  143.0 2.4 %spread_sum.5 = (f32[2,2,128,128]{3,2,1,0:T(8,128)}, f32[2,2,128,128]{3,2,1,0:T(8,128)}, f32[2,2,128,128]{3,2,1,0:T(8,128)}, f32[2,2,128,128]{3,2,1,0:T(8,128)}) custom-call(f32[4,2,2,128,128]{4,3,2,1,0:T(8,128)} %bitcast.40, f32[4,2,2,128,128]{4,3,2,1,0:T(8,128)} %bitcast.16.second_ref), custom_call_target="tpu_custom_call" | custom-call | flops 262144 | bytes 3145728 | tf_op jit(solution)/shard_map/spread_sum/pallas_call | solution.py:556
  145.4 3.6 %collective-permute-done.6 = f32[2,2,128,128]{3,2,1,0:T(8,128)} collective-permute-done((f32[2,2,128,128]{3,2,1,0:T(8,128)}, f32[2,2,128,128]{3,2,1,0:T(8,128)}, u32[]{:S(2)}, u32[]{:S(2)}) %collective-permute-start.6) | collective-permute-done | bytes 262176 | tf_op jit(solution)/shard_map/ppermute | solution.py:622
  149.0 4.9 %collective-permute-done.7 = f32[2,2,128,128]{3,2,1,0:T(8,128)} collective-permute-done((f32[2,2,128,128]{3,2,1,0:T(8,128)}, f32[2,2,128,128]{3,2,1,0:T(8,128)}, u32[]{:S(2)}, u32[]{:S(2)}) %collective-permute-start.7) | collective-permute-done | bytes 262176 | tf_op jit(solution)/shard_map/ppermute | solution.py:622
  153.9 2.1 %sum_of.3 = f32[2,2,128,128]{3,2,1,0:T(8,128)} custom-call(f32[1,2,2,128,128]{4,3,2,1,0:T(8,128)} %bitcast.44, f32[1,2,2,128,128]{4,3,2,1,0:T(8,128)} %bitcast.27.refs_1_, f32[1,2,2,128,128]{4,3,2,1,0:T(8,128)} %bitcast.28.refs_2_, f32[1,2,2,128,128]{4,3,2,1,0:T(8,128)} %bitcast.29.refs_3_, f32[2,2,2,128,128]{4,3,2,1,0:T(8,128)} %bitcast.25.refs_4_), custom_call_target="tpu_custom_call" | custom-call | flops 262144 | bytes 1572864 | tf_op jit(solution)/shard_map/sum_of/pallas_call | solution.py:530
  156.0 2.6 %collective-permute-start.14 = (f32[2,2,128,128]{3,2,1,0:T(8,128)}, f32[2,2,128,128]{3,2,1,0:T(8,128)}, u32[]{:S(2)}, u32[]{:S(2)}) collective-permute-start(f32[2,2,128,128]{3,2,1,0:T(8,128)} %sum_of.3), channel_id=1, source_target_pairs={{0,4},{1,5},{2,6},{3,7},{4,0},{5,1},{6,2},{7,3},{8,12},{9,13},{10,... | collective-permute-start | bytes 786440 | tf_op jit(solution)/shard_map/ppermute | solution.py:622
  159.2 1.5 collective-permute-start.11
  160.6 1.4 collective-permute-start.12
  162.1 6.8 %collective-permute-done.14 = f32[2,2,128,128]{3,2,1,0:T(8,128)} collective-permute-done((f32[2,2,128,128]{3,2,1,0:T(8,128)}, f32[2,2,128,128]{3,2,1,0:T(8,128)}, u32[]{:S(2)}, u32[]{:S(2)}) %collective-permute-start.14) | collective-permute-done | bytes 262176 | tf_op jit(solution)/shard_map/ppermute | solution.py:622
  168.9 1.9 %collective-permute-done.11 = f32[2,2,128,128]{3,2,1,0:T(8,128)} collective-permute-done((f32[2,2,128,128]{3,2,1,0:T(8,128)}, f32[2,2,128,128]{3,2,1,0:T(8,128)}, u32[]{:S(2)}, u32[]{:S(2)}) %collective-permute-start.11) | collective-permute-done | bytes 262176 | tf_op jit(solution)/shard_map/ppermute | solution.py:622
  170.8 3.4 %power_of.1 = f32[2,128,128]{2,1,0:T(8,128)} custom-call(f32[1,2,2,128,128]{4,3,2,1,0:T(8,128)} %bitcast.45, f32[1,2,2,128,128]{4,3,2,1,0:T(8,128)} %bitcast.18.refs_1_, f32[1,2,2,128,128]{4,3,2,1,0:T(8,128)} %bitcast.19.refs_2_, f32[1,2,2,128,128]{4,3,2,1,0:T(8,128)} %bitcast.20.refs_3_, f32[2,2,2,128,128]{4,3,2,1,0:T(8,128)} %bitcast.25.refs_4_, ...), custom_call_target="tpu_custom_call" | custom-call | tf_op jit(solution)/shard_map/power_of/pallas_call | solution.py:591
  174.1 1.0 copy.37
  175.1 7.8 %all_to_all.18 = f32[2,128,128]{2,0,1:T(2,128)S(1)} all-to-all(f32[2,128,128]{2,0,1:T(2,128)S(1)} %copy.37), channel_id=1, replica_groups=mesh['wave'=4,'row'=8] {'wave'}, dimensions={1} | all-to-all | bytes 262144 | tf_op jit(solution)/shard_map/all_to_all | solution.py:721
  182.9 0.7 copy.38
  (23 shorter events, 2.9 us)
Async XLA Ops:
  0.6 10.5 %copy-start = (s32[64,2]{0,1:T(2,128)S(1)}, s32[64,2]{0,1:T(2,128)}, u32[]{:S(2)}) copy-start(s32[64,2]{0,1:T(2,128)} %param.34) | copy-start | bytes 1540
  0.6 11.2 %copy-start.1 = (s32[1,2]{1,0:T(1,128)S(1)}, s32[1,2]{1,0:T(1,128)}, u32[]{:S(2)}) copy-start(s32[1,2]{1,0:T(1,128)} %param.31) | copy-start | bytes 28
  9.3 12.3 %collective-permute-start = (f32[2,256,1024]{2,1,0:T(8,128)}, f32[2,256,1024]{2,1,0:T(8,128)}, u32[]{:S(2)}, u32[]{:S(2)}) collective-permute-start(f32[2,256,1024]{2,1,0:T(8,128)} %get-tuple-element.57), channel_id=1, source_target_pairs={{0,1},{1,0},{2,3},{3,2},{4,5},{5,4},{6,7},{7,6},{8,9},{9,8},{10,11... | collective-permute-start | bytes 6291464 | tf_op jit(solution)/shard_map/ppermute | solution.py:622
  76.4 27.9 %collective-permute-start.1 = (f32[16,2,128,128]{3,2,1,0:T(8,128)}, f32[16,2,128,128]{3,2,1,0:T(8,128)}, u32[]{:S(2)}, u32[]{:S(2)}) collective-permute-start(f32[16,2,128,128]{3,2,1,0:T(8,128)} %get-tuple-element.68), channel_id=1, source_target_pairs={{0,1},{1,0},{2,3},{3,2},{4,5},{5,4},{6,7},{7,6},{8,9},{9,8},{10,11... | collective-permute-start | bytes 6291464 | tf_op jit(solution)/shard_map/ppermute | solution.py:622
  103.7 23.0 %collective-permute-start.5 = (f32[8,2,128,128]{3,2,1,0:T(8,128)}, f32[8,2,128,128]{3,2,1,0:T(8,128)}, u32[]{:S(2)}, u32[]{:S(2)}) collective-permute-start(f32[8,2,128,128]{3,2,1,0:T(8,128)} %get-tuple-element.78), channel_id=1, source_target_pairs={{0,1},{1,0},{2,3},{3,2},{4,5},{5,4},{6,7},{7,6},{8,9},{9,8},{10,11... | collective-permute-start | bytes 3145736 | tf_op jit(solution)/shard_map/ppermute | solution.py:622
  107.6 21.6 %collective-permute-start.2 = (f32[4,2,128,128]{3,2,1,0:T(8,128)}, f32[4,2,128,128]{3,2,1,0:T(8,128)}, u32[]{:S(2)}, u32[]{:S(2)}) collective-permute-start(f32[4,2,128,128]{3,2,1,0:T(8,128)} %get-tuple-element.74), channel_id=1, source_target_pairs={{0,8},{8,0},{16,24},{24,16},{1,9},{9,1},{17,25},{25,17},{2,10},{10... | collective-permute-start | bytes 1572872 | tf_op jit(solution)/shard_map/ppermute | solution.py:622
  110.1 25.6 %collective-permute-start.3 = (f32[4,2,128,128]{3,2,1,0:T(8,128)}, f32[4,2,128,128]{3,2,1,0:T(8,128)}, u32[]{:S(2)}, u32[]{:S(2)}) collective-permute-start(f32[4,2,128,128]{3,2,1,0:T(8,128)} %get-tuple-element.75), channel_id=1, source_target_pairs={{0,16},{8,24},{16,0},{24,8},{1,17},{9,25},{17,1},{25,9},{2,18},{10... | collective-permute-start | bytes 1572872 | tf_op jit(solution)/shard_map/ppermute | solution.py:622
  111.6 24.1 %collective-permute-start.4 = (f32[4,2,128,128]{3,2,1,0:T(8,128)}, f32[4,2,128,128]{3,2,1,0:T(8,128)}, u32[]{:S(2)}, u32[]{:S(2)}) collective-permute-start(f32[4,2,128,128]{3,2,1,0:T(8,128)} %get-tuple-element.76), channel_id=1, source_target_pairs={{0,24},{8,16},{16,8},{24,0},{1,25},{9,17},{17,9},{25,1},{2,26},{10... | collective-permute-start | bytes 1572872 | tf_op jit(solution)/shard_map/ppermute | solution.py:622
  126.7 16.3 %collective-permute-start.9 = (f32[8,2,128,128]{3,2,1,0:T(8,128)}, f32[8,2,128,128]{3,2,1,0:T(8,128)}, u32[]{:S(2)}, u32[]{:S(2)}) collective-permute-start(f32[8,2,128,128]{3,2,1,0:T(8,128)} %get-tuple-element.90), channel_id=1, source_target_pairs={{0,1},{1,0},{2,3},{3,2},{4,5},{5,4},{6,7},{7,6},{8,9},{9,8},{10,11... | collective-permute-start | bytes 3145736 | tf_op jit(solution)/shard_map/ppermute | solution.py:622
  137.9 16.0 %collective-permute-start.13 = (f32[4,2,128,128]{3,2,1,0:T(8,128)}, f32[4,2,128,128]{3,2,1,0:T(8,128)}, u32[]{:S(2)}, u32[]{:S(2)}) collective-permute-start(f32[4,2,128,128]{3,2,1,0:T(8,128)} %sum_of.2), channel_id=1, source_target_pairs={{0,2},{1,3},{2,0},{3,1},{4,6},{5,7},{6,4},{7,5},{8,10},{9,11},{10,... | collective-permute-start | bytes 1572872 | tf_op jit(solution)/shard_map/ppermute | solution.py:622
  139.5 9.5 %collective-permute-start.6 = (f32[2,2,128,128]{3,2,1,0:T(8,128)}, f32[2,2,128,128]{3,2,1,0:T(8,128)}, u32[]{:S(2)}, u32[]{:S(2)}) collective-permute-start(f32[2,2,128,128]{3,2,1,0:T(8,128)} %get-tuple-element.84), channel_id=1, source_target_pairs={{0,8},{8,0},{16,24},{24,16},{1,9},{9,1},{17,25},{25,17},{2,10},{10... | collective-permute-start | bytes 786440 | tf_op jit(solution)/shard_map/ppermute | solution.py:622
  140.7 13.2 %collective-permute-start.7 = (f32[2,2,128,128]{3,2,1,0:T(8,128)}, f32[2,2,128,128]{3,2,1,0:T(8,128)}, u32[]{:S(2)}, u32[]{:S(2)}) collective-permute-start(f32[2,2,128,128]{3,2,1,0:T(8,128)} %get-tuple-element.85), channel_id=1, source_target_pairs={{0,16},{8,24},{16,0},{24,8},{1,17},{9,25},{17,1},{25,9},{2,18},{10... | collective-permute-start | bytes 786440 | tf_op jit(solution)/shard_map/ppermute | solution.py:622
  141.5 12.4 %collective-permute-start.8 = (f32[2,2,128,128]{3,2,1,0:T(8,128)}, f32[2,2,128,128]{3,2,1,0:T(8,128)}, u32[]{:S(2)}, u32[]{:S(2)}) collective-permute-start(f32[2,2,128,128]{3,2,1,0:T(8,128)} %get-tuple-element.86), channel_id=1, source_target_pairs={{0,24},{8,16},{16,8},{24,0},{1,25},{9,17},{17,9},{25,1},{2,26},{10... | collective-permute-start | bytes 786440 | tf_op jit(solution)/shard_map/ppermute | solution.py:622
  156.0 12.9 %collective-permute-start.14 = (f32[2,2,128,128]{3,2,1,0:T(8,128)}, f32[2,2,128,128]{3,2,1,0:T(8,128)}, u32[]{:S(2)}, u32[]{:S(2)}) collective-permute-start(f32[2,2,128,128]{3,2,1,0:T(8,128)} %sum_of.3), channel_id=1, source_target_pairs={{0,4},{1,5},{2,6},{3,7},{4,0},{5,1},{6,2},{7,3},{8,12},{9,13},{10,... | collective-permute-start | bytes 786440 | tf_op jit(solution)/shard_map/ppermute | solution.py:622
  158.6 10.3 %collective-permute-start.10 = (f32[2,2,128,128]{3,2,1,0:T(8,128)}, f32[2,2,128,128]{3,2,1,0:T(8,128)}, u32[]{:S(2)}, u32[]{:S(2)}) collective-permute-start(f32[2,2,128,128]{3,2,1,0:T(8,128)} %get-tuple-element.96), channel_id=1, source_target_pairs={{0,8},{8,0},{16,24},{24,16},{1,9},{9,1},{17,25},{25,17},{2,10},{10... | collective-permute-start | bytes 786440 | tf_op jit(solution)/shard_map/ppermute | solution.py:622
  159.2 11.6 %collective-permute-start.11 = (f32[2,2,128,128]{3,2,1,0:T(8,128)}, f32[2,2,128,128]{3,2,1,0:T(8,128)}, u32[]{:S(2)}, u32[]{:S(2)}) collective-permute-start(f32[2,2,128,128]{3,2,1,0:T(8,128)} %get-tuple-element.97), channel_id=1, source_target_pairs={{0,16},{8,24},{16,0},{24,8},{1,17},{9,25},{17,1},{25,9},{2,18},{10... | collective-permute-start | bytes 786440 | tf_op jit(solution)/shard_map/ppermute | solution.py:622
  160.6 10.2 %collective-permute-start.12 = (f32[2,2,128,128]{3,2,1,0:T(8,128)}, f32[2,2,128,128]{3,2,1,0:T(8,128)}, u32[]{:S(2)}, u32[]{:S(2)}) collective-permute-start(f32[2,2,128,128]{3,2,1,0:T(8,128)} %get-tuple-element.98), channel_id=1, source_target_pairs={{0,24},{8,16},{16,8},{24,0},{1,25},{9,17},{17,9},{25,1},{2,26},{10... | collective-permute-start | bytes 786440 | tf_op jit(solution)/shard_map/ppermute | solution.py:622

commit v7 on v6

--- a/solution.py
+++ b/solution.py
@@ -9,13 +9,13 @@
 from jax.experimental.pallas import tpu as pltpu
 from jax.sharding import PartitionSpec as P
 
+
 GRID = 2048
 FACTOR = 16
 WINDOW = 128
 HALF = 64
 FRESNEL = 0.1
 
-BAND = math.isqrt(GRID * GRID // 9)
 FOLD = GRID // 2
 BLOCKS = 3
 LANES = 128
@@ -622,7 +622,7 @@
     return lax.ppermute(block, axis, [(i, i ^ bit) for i in range(count)])
 
 
-def shards(plane_waves, transmission, wave_index, wave_weight, wave_phase, probe_pos):
+def diffraction(plane_waves, transmission, wave_index, wave_weight, wave_phase, probe_pos):
     rows_here = plane_waves.shape[2]
     row_count = lax.axis_size("row")
     wave_count = lax.axis_size("wave")
@@ -678,9 +678,11 @@
         return lax.optimization_barrier((value,) + before)
 
     def over_waves(pieces):
-        return [(pieces[0], 0, 1)] + [
-            (flip(piece, "wave", bits), 0, 1) for bits, piece in enumerate(pieces) if bits
-        ]
+        terms = [(pieces[0], 0, 1)]
+        for bits, piece in enumerate(pieces):
+            if bits:
+                terms.append((flip(piece, "wave", bits), 0, 1))
+        return terms
 
     common = (info, probe_pos, weights)
     keep, send = inverse(
@@ -695,19 +697,17 @@
     pieces = spread_sum(keep, arrived, wave_count)
     (rows_hi, rows_lo), pieces = later((rows_hi, rows_lo), pieces)
     odd_terms = over_waves(pieces)
-    keep_lower, send = column_inverse(
-        layout, (rows_hi, rows_lo), slots_of(0, (lower,)), *common
-    )
+    keep_lower, send = column_inverse(layout, (rows_hi, rows_lo), slots_of(0, (lower,)), *common)
     arrived_lower = flip(send, "row", 1)
     pieces = spread_sum(keep_upper, arrived_upper, wave_count)
-    odd_arrays, pieces = later([term[0] for term in odd_terms], pieces)
+    lower_pieces = spread_sum(keep_lower, arrived_lower, wave_count)
+    odd_arrays, pieces, lower_pieces = later(
+        [term[0] for term in odd_terms], pieces, lower_pieces
+    )
     odd_terms = [(array, 0, 1) for array in odd_arrays]
     upper_terms = over_waves(pieces)
     near = flip(sum_of(odd_terms, False), "row", 2)
-    pieces = spread_sum(keep_lower, arrived_lower, wave_count)
-    arrays, pieces = later([term[0] for term in upper_terms], pieces)
-    upper_terms = [(array, 0, 1) for array in arrays]
-    lower_terms = over_waves(pieces)
+    lower_terms = over_waves(lower_pieces)
 
     bit = row_count // 2
     send = sum_of(upper_terms + [(near, 0, 2)], False)
@@ -723,7 +723,7 @@
 
 def solution(mesh):
     return jax.shard_map(
-        shards,
+        diffraction,
         mesh=mesh,
         in_specs=(
             P(None, "wave", "row", None),

time: 185 us -> 199 us (1.076)
  waiting for transfers between devices: 23.8 us -> 36.7 us
    ppermute x15, waiting for transfers between devices: 23.8 us -> 36.7 us  [flip(): return lax.ppermute(block, axis, [(i, i ^ bit) for i in range(count)])]
  transfers between devices with their start and end apart: 15 -> 15, of which waited for: 5 -> 6; matrix products, arithmetic and copies ran while one was open for 2% -> 2% of each run, Pallas kernels for 33% -> 30%
where the time goes in v7:
time: 199 us; the launch traced here: 197 us
  Pallas kernels  129 us (65%)
  waiting for transfers between devices  36.7 us (18%)
  starting transfers between devices  15.9 us (8%)
  blocking collectives  8.56 us (4%)
  local copies, waits for them, and re-layouts  3.7 us (2%)
    pallas_call x2, Pallas kernels, inverse(): pl.pallas_call(functools.partial(inverse_kernel, layout, cuts, base), out...  64.1 us
    ppermute x15, waiting for transfers between devices, flip(): return lax.ppermute(block, axis, [(i, i ^ bit) for i in range(count)])  36.7 us
    pallas_call x1, Pallas kernels, row_forward(): pl.pallas_call(row_forward_kernel, out_shape=(out, out), grid_spec=pltpu....  17.9 us
    ppermute x15, starting transfers between devices, flip(): return lax.ppermute(block, axis, [(i, i ^ bit) for i in range(count)])  15.9 us
    pallas_call x1, Pallas kernels, column_inverse(): pl.pallas_call(functools.partial(column_inverse_kernel, layout), out_shap...  15.3 us
    pallas_call x1, Pallas kernels, split_columns(): pl.pallas_call(split_kernel, out_shape=(out, out), grid_spec=pltpu.Prefet...  8.68 us
    all_to_all x1, blocking collectives, diffraction(): lax.all_to_all(power, 'wave', split_axis=1, concat_axis=0, tiled=True)  8.56 us
    pallas_call x3, Pallas kernels, spread_sum(): pl.pallas_call(spread_kernel, out_shape=[out] * count, grid=(size // step...  8.16 us
  transfers between devices with their start and end apart: 15, of which 6 were waited for; matrix products, arithmetic and copies ran while one was open for 2% of the time, Pallas kernels for 30%

profile of v7, /device:TPU:0, one launch (start us, length us, event | category | flops | bytes accessed | tf_op | source)
XLA Modules:
  0.0 197.2 jit_solution(6582290840008737198)
XLA Ops:
  0.6 8.7 %split_columns.1 = (f32[2,256,1024]{2,1,0:T(8,128)}, f32[2,256,1024]{2,1,0:T(8,128)}) custom-call(s32[7]{0:T(128)} %stack.33.info_ref, f32[2,1,256,2048]{3,2,1,0:T(8,128)} %wave_ref.1, f32[1,2,256,2048]{3,2,1,0:T(8,128)} %trans_ref.1), custom_call_target="tpu_custom_call" | custom-call | flops 10485760 | bytes 12582912 | tf_op jit(solution)/shard_map/split_columns/pallas_call | solution.py:97
  10.5 0.7 copy.35.pos_ref
  11.8 1.3 fusion.4
  14.4 7.1 %column_forward.1.mine_ref = f32[2,256,768]{2,1,0:T(8,128)} custom-call(s32[7]{0:T(128)} %stack.33.info_ref, f32[2,256,1024]{2,1,0:T(8,128)} %get-tuple-element.52.field_ref, bf16[2,1024,768]{2,1,0:T(8,128)(2,1)} %constant.228.clone.table_hi.col_hi, bf16[2,1024,768]{2,1,0:T(8,128)(2,1)} %constant.229.clone.table_lo.col_lo), custom_call_target="tpu_custom_call" | custom-call | flops 2415919104 | bytes 3670016 | tf_op jit(solution)/shard_map/column_forward/pallas_call | solution.py:137
  21.6 17.9 %row_forward.1 = (bf16[2,1536,768]{2,1,0:T(8,128)(2,1)}, bf16[2,1536,768]{2,1,0:T(8,128)(2,1)}) custom-call(s32[7]{0:T(128)} %stack.33.info_ref, f32[2,256,768]{2,1,0:T(8,128)} %column_forward.1.mine_ref, f32[2,256,1024]{2,1,0:T(8,128)} %collective-permute-done.theirs_ref, bf16[2,1024,768]{2,1,0:T(8,128)(2,1)} %constant.228.clone.table_hi.col_hi, ...), custom_call_target="tpu_custom_call" | custom-call | flops 7247757312 | bytes 12582912 | tf_op jit(solution)/shard_map/row_forward/pallas_call | solution.py:229
  39.5 36.8 %inverse.2 = (f32[16,2,128,128]{3,2,1,0:T(8,128)}, f32[16,2,128,128]{3,2,1,0:T(8,128)}) custom-call(s32[7]{0:T(128)} %stack.33.info_ref, s32[4,32]{1,0:T(4,128)} %constant.236.clone.slot_ref, s32[64,2]{1,0:T(8,128)} %copy.35.pos_ref, f32[2,64]{1,0:T(2,128)} %maximum_multiply_fusion.weight_ref, bf16[2,1536,768]{2,1,0:T(8,128)(2,1)} %get-tuple-element.59.spec_hi, ...), custom_call_target="tpu_custom_call" | custom-call | flops 21139292160 | bytes 17301504 | tf_op jit(solution)/shard_map/inverse/pallas_call | solution.py:399
  76.3 27.4 %inverse.3 = (f32[8,2,128,128]{3,2,1,0:T(8,128)}, f32[8,2,128,128]{3,2,1,0:T(8,128)}, bf16[2,640,768]{2,1,0:T(8,128)(2,1)}, bf16[2,640,768]{2,1,0:T(8,128)(2,1)}) custom-call(s32[7]{0:T(128)} %stack.33.info_ref, s32[4,16]{1,0:T(4,128)} %constant.241.clone.slot_ref, s32[64,2]{1,0:T(8,128)} %copy.35.pos_ref, f32[2,64]{1,0:T(2,128)} %maximum_multiply_fusion.weight_ref, ...), custom_call_target="tpu_custom_call" | custom-call | flops 15099494400 | bytes 17301504 | tf_op jit(solution)/shard_map/inverse/pallas_call | solution.py:399
  104.2 3.3 %spread_sum.3 = (f32[4,2,128,128]{3,2,1,0:T(8,128)}, f32[4,2,128,128]{3,2,1,0:T(8,128)}, f32[4,2,128,128]{3,2,1,0:T(8,128)}, f32[4,2,128,128]{3,2,1,0:T(8,128)}) custom-call(f32[4,4,2,128,128]{4,3,2,1,0:T(8,128)} %bitcast.39, f32[4,4,2,128,128]{4,3,2,1,0:T(8,128)} %bitcast.12.second_ref), custom_call_target="tpu_custom_call" | custom-call | flops 524288 | bytes 6291456 | tf_op jit(solution)/shard_map/spread_sum/pallas_call | solution.py:556
  107.5 15.3 %column_inverse.1 = (f32[8,2,128,128]{3,2,1,0:T(8,128)}, f32[8,2,128,128]{3,2,1,0:T(8,128)}) custom-call(s32[7]{0:T(128)} %stack.33.info_ref, s32[4,16]{1,0:T(4,128)} %constant.242.clone.slot_ref, s32[64,2]{1,0:T(8,128)} %copy.35.pos_ref, f32[2,64]{1,0:T(2,128)} %maximum_multiply_fusion.weight_ref, bf16[2,640,768]{2,1,0:T(8,128)(2,1)} %get-tuple-element.79.rows_hi, ...), custom_call_target="tpu_custom_call" | custom-call | flops 6039797760 | bytes 6029312 | tf_op jit(solution)/shard_map/column_inverse/pallas_call | solution.py:470
  122.8 3.0 %collective-permute-start.2 = (f32[4,2,128,128]{3,2,1,0:T(8,128)}, f32[4,2,128,128]{3,2,1,0:T(8,128)}, u32[]{:S(2)}, u32[]{:S(2)}) collective-permute-start(f32[4,2,128,128]{3,2,1,0:T(8,128)} %get-tuple-element.70), channel_id=1, source_target_pairs={{0,8},{8,0},{16,24},{24,16},{1,9},{9,1},{17,25},{25,17},{2,10},{10... | collective-permute-start | bytes 1572872 | tf_op jit(solution)/shard_map/ppermute | solution.py:622
  125.8 1.5 collective-permute-start.3
  127.3 2.4 %spread_sum.4 = (f32[2,2,128,128]{3,2,1,0:T(8,128)}, f32[2,2,128,128]{3,2,1,0:T(8,128)}, f32[2,2,128,128]{3,2,1,0:T(8,128)}, f32[2,2,128,128]{3,2,1,0:T(8,128)}) custom-call(f32[4,2,2,128,128]{4,3,2,1,0:T(8,128)} %bitcast.40, f32[4,2,2,128,128]{4,3,2,1,0:T(8,128)} %bitcast.14.second_ref), custom_call_target="tpu_custom_call" | custom-call | flops 262144 | bytes 3145728 | tf_op jit(solution)/shard_map/spread_sum/pallas_call | solution.py:556
  129.8 2.4 %spread_sum.5 = (f32[2,2,128,128]{3,2,1,0:T(8,128)}, f32[2,2,128,128]{3,2,1,0:T(8,128)}, f32[2,2,128,128]{3,2,1,0:T(8,128)}, f32[2,2,128,128]{3,2,1,0:T(8,128)}) custom-call(f32[4,2,2,128,128]{4,3,2,1,0:T(8,128)} %bitcast.41, f32[4,2,2,128,128]{4,3,2,1,0:T(8,128)} %bitcast.16.second_ref), custom_call_target="tpu_custom_call" | custom-call | flops 262144 | bytes 3145728 | tf_op jit(solution)/shard_map/spread_sum/pallas_call | solution.py:556
  132.2 6.7 %collective-permute-done.2 = f32[4,2,128,128]{3,2,1,0:T(8,128)} collective-permute-done((f32[4,2,128,128]{3,2,1,0:T(8,128)}, f32[4,2,128,128]{3,2,1,0:T(8,128)}, u32[]{:S(2)}, u32[]{:S(2)}) %collective-permute-start.2) | collective-permute-done | bytes 524320 | tf_op jit(solution)/shard_map/ppermute | solution.py:622
  138.9 12.1 %collective-permute-done.3 = f32[4,2,128,128]{3,2,1,0:T(8,128)} collective-permute-done((f32[4,2,128,128]{3,2,1,0:T(8,128)}, f32[4,2,128,128]{3,2,1,0:T(8,128)}, u32[]{:S(2)}, u32[]{:S(2)}) %collective-permute-start.3) | collective-permute-done | bytes 524320 | tf_op jit(solution)/shard_map/ppermute | solution.py:622
  151.0 2.3 %sum_of.2 = f32[4,2,128,128]{3,2,1,0:T(8,128)} custom-call(f32[1,4,2,128,128]{4,3,2,1,0:T(8,128)} %bitcast.42, f32[1,4,2,128,128]{4,3,2,1,0:T(8,128)} %bitcast.22.refs_1_, f32[1,4,2,128,128]{4,3,2,1,0:T(8,128)} %bitcast.23.refs_2_, f32[1,4,2,128,128]{4,3,2,1,0:T(8,128)} %bitcast.24.refs_3_), custom_call_target="tpu_custom_call" | custom-call | flops 524288 | bytes 2621440 | tf_op jit(solution)/shard_map/sum_of/pallas_call | solution.py:530
  153.2 1.6 collective-permute-start.10
  154.8 1.2 collective-permute-start.11
  156.0 0.8 collective-permute-start.12
  156.9 1.4 collective-permute-start.13
  158.3 1.2 collective-permute-start.7
  159.5 4.8 %collective-permute-done.11 = f32[2,2,128,128]{3,2,1,0:T(8,128)} collective-permute-done((f32[2,2,128,128]{3,2,1,0:T(8,128)}, f32[2,2,128,128]{3,2,1,0:T(8,128)}, u32[]{:S(2)}, u32[]{:S(2)}) %collective-permute-start.11) | collective-permute-done | bytes 262176 | tf_op jit(solution)/shard_map/ppermute | solution.py:622
  164.3 1.5 collective-permute-start.8
  165.8 5.3 %collective-permute-done.12 = f32[2,2,128,128]{3,2,1,0:T(8,128)} collective-permute-done((f32[2,2,128,128]{3,2,1,0:T(8,128)}, f32[2,2,128,128]{3,2,1,0:T(8,128)}, u32[]{:S(2)}, u32[]{:S(2)}) %collective-permute-start.12) | collective-permute-done | bytes 262176 | tf_op jit(solution)/shard_map/ppermute | solution.py:622
  171.1 2.1 %sum_of.3 = f32[2,2,128,128]{3,2,1,0:T(8,128)} custom-call(f32[1,2,2,128,128]{4,3,2,1,0:T(8,128)} %bitcast.45, f32[1,2,2,128,128]{4,3,2,1,0:T(8,128)} %bitcast.27.refs_1_, f32[1,2,2,128,128]{4,3,2,1,0:T(8,128)} %bitcast.28.refs_2_, f32[1,2,2,128,128]{4,3,2,1,0:T(8,128)} %bitcast.29.refs_3_, f32[2,2,2,128,128]{4,3,2,1,0:T(8,128)} %bitcast.25.refs_4_), custom_call_target="tpu_custom_call" | custom-call | flops 262144 | bytes 1572864 | tf_op jit(solution)/shard_map/sum_of/pallas_call | solution.py:530
  173.2 2.6 %collective-permute-start.14 = (f32[2,2,128,128]{3,2,1,0:T(8,128)}, f32[2,2,128,128]{3,2,1,0:T(8,128)}, u32[]{:S(2)}, u32[]{:S(2)}) collective-permute-start(f32[2,2,128,128]{3,2,1,0:T(8,128)} %sum_of.3), channel_id=1, source_target_pairs={{0,4},{1,5},{2,6},{3,7},{4,0},{5,1},{6,2},{7,3},{8,12},{9,13},{10,... | collective-permute-start | bytes 786440 | tf_op jit(solution)/shard_map/ppermute | solution.py:622
  175.8 4.3 %collective-permute-done.8 = f32[2,2,128,128]{3,2,1,0:T(8,128)} collective-permute-done((f32[2,2,128,128]{3,2,1,0:T(8,128)}, f32[2,2,128,128]{3,2,1,0:T(8,128)}, u32[]{:S(2)}, u32[]{:S(2)}) %collective-permute-start.8) | collective-permute-done | bytes 262176 | tf_op jit(solution)/shard_map/ppermute | solution.py:622
  180.1 3.5 %collective-permute-done.14 = f32[2,2,128,128]{3,2,1,0:T(8,128)} collective-permute-done((f32[2,2,128,128]{3,2,1,0:T(8,128)}, f32[2,2,128,128]{3,2,1,0:T(8,128)}, u32[]{:S(2)}, u32[]{:S(2)}) %collective-permute-start.14) | collective-permute-done | bytes 262176 | tf_op jit(solution)/shard_map/ppermute | solution.py:622
  183.6 3.3 %power_of.1 = f32[2,128,128]{2,1,0:T(8,128)} custom-call(f32[1,2,2,128,128]{4,3,2,1,0:T(8,128)} %bitcast.44, f32[1,2,2,128,128]{4,3,2,1,0:T(8,128)} %bitcast.18.refs_1_, f32[1,2,2,128,128]{4,3,2,1,0:T(8,128)} %bitcast.19.refs_2_, f32[1,2,2,128,128]{4,3,2,1,0:T(8,128)} %bitcast.20.refs_3_, f32[2,2,2,128,128]{4,3,2,1,0:T(8,128)} %bitcast.25.refs_4_, ...), custom_call_target="tpu_custom_call" | custom-call | tf_op jit(solution)/shard_map/power_of/pallas_call | solution.py:591
  186.9 1.0 copy.37
  187.9 8.6 %all_to_all.18 = f32[2,128,128]{2,0,1:T(2,128)S(1)} all-to-all(f32[2,128,128]{2,0,1:T(2,128)S(1)} %copy.37), channel_id=1, replica_groups=mesh['wave'=4,'row'=8] {'wave'}, dimensions={1} | all-to-all | bytes 262144 | tf_op jit(solution)/shard_map/all_to_all | solution.py:721
  196.5 0.7 copy.38
  (23 shorter events, 3.0 us)
Async XLA Ops:
  0.6 9.8 %copy-start = (s32[64,2]{0,1:T(2,128)S(1)}, s32[64,2]{0,1:T(2,128)}, u32[]{:S(2)}) copy-start(s32[64,2]{0,1:T(2,128)} %param.34) | copy-start | bytes 1540
  0.6 10.6 %copy-start.1 = (s32[1,2]{1,0:T(1,128)S(1)}, s32[1,2]{1,0:T(1,128)}, u32[]{:S(2)}) copy-start(s32[1,2]{1,0:T(1,128)} %param.31) | copy-start | bytes 28
  9.3 12.3 %collective-permute-start = (f32[2,256,1024]{2,1,0:T(8,128)}, f32[2,256,1024]{2,1,0:T(8,128)}, u32[]{:S(2)}, u32[]{:S(2)}) collective-permute-start(f32[2,256,1024]{2,1,0:T(8,128)} %get-tuple-element.53), channel_id=1, source_target_pairs={{0,1},{1,0},{2,3},{3,2},{4,5},{5,4},{6,7},{7,6},{8,9},{9,8},{10,11... | collective-permute-start | bytes 6291464 | tf_op jit(solution)/shard_map/ppermute | solution.py:622
  76.3 27.9 %collective-permute-start.1 = (f32[16,2,128,128]{3,2,1,0:T(8,128)}, f32[16,2,128,128]{3,2,1,0:T(8,128)}, u32[]{:S(2)}, u32[]{:S(2)}) collective-permute-start(f32[16,2,128,128]{3,2,1,0:T(8,128)} %get-tuple-element.64), channel_id=1, source_target_pairs={{0,1},{1,0},{2,3},{3,2},{4,5},{5,4},{6,7},{7,6},{8,9},{9,8},{10,11... | collective-permute-start | bytes 6291464 | tf_op jit(solution)/shard_map/ppermute | solution.py:622
  103.7 23.6 %collective-permute-start.5 = (f32[8,2,128,128]{3,2,1,0:T(8,128)}, f32[8,2,128,128]{3,2,1,0:T(8,128)}, u32[]{:S(2)}, u32[]{:S(2)}) collective-permute-start(f32[8,2,128,128]{3,2,1,0:T(8,128)} %get-tuple-element.74), channel_id=1, source_target_pairs={{0,1},{1,0},{2,3},{3,2},{4,5},{5,4},{6,7},{7,6},{8,9},{9,8},{10,11... | collective-permute-start | bytes 3145736 | tf_op jit(solution)/shard_map/ppermute | solution.py:622
  122.8 7.0 %collective-permute-start.6 = (f32[8,2,128,128]{3,2,1,0:T(8,128)}, f32[8,2,128,128]{3,2,1,0:T(8,128)}, u32[]{:S(2)}, u32[]{:S(2)}) collective-permute-start(f32[8,2,128,128]{3,2,1,0:T(8,128)} %get-tuple-element.82), channel_id=1, source_target_pairs={{0,1},{1,0},{2,3},{3,2},{4,5},{5,4},{6,7},{7,6},{8,9},{9,8},{10,11... | collective-permute-start | bytes 3145736 | tf_op jit(solution)/shard_map/ppermute | solution.py:622
  122.8 16.1 %collective-permute-start.2 = (f32[4,2,128,128]{3,2,1,0:T(8,128)}, f32[4,2,128,128]{3,2,1,0:T(8,128)}, u32[]{:S(2)}, u32[]{:S(2)}) collective-permute-start(f32[4,2,128,128]{3,2,1,0:T(8,128)} %get-tuple-element.70), channel_id=1, source_target_pairs={{0,8},{8,0},{16,24},{24,16},{1,9},{9,1},{17,25},{25,17},{2,10},{10... | collective-permute-start | bytes 1572872 | tf_op jit(solution)/shard_map/ppermute | solution.py:622
  125.8 25.2 %collective-permute-start.3 = (f32[4,2,128,128]{3,2,1,0:T(8,128)}, f32[4,2,128,128]{3,2,1,0:T(8,128)}, u32[]{:S(2)}, u32[]{:S(2)}) collective-permute-start(f32[4,2,128,128]{3,2,1,0:T(8,128)} %get-tuple-element.71), channel_id=1, source_target_pairs={{0,16},{8,24},{16,0},{24,8},{1,17},{9,25},{17,1},{25,9},{2,18},{10... | collective-permute-start | bytes 1572872 | tf_op jit(solution)/shard_map/ppermute | solution.py:622
  127.3 23.6 %collective-permute-start.4 = (f32[4,2,128,128]{3,2,1,0:T(8,128)}, f32[4,2,128,128]{3,2,1,0:T(8,128)}, u32[]{:S(2)}, u32[]{:S(2)}) collective-permute-start(f32[4,2,128,128]{3,2,1,0:T(8,128)} %get-tuple-element.72), channel_id=1, source_target_pairs={{0,24},{8,16},{16,8},{24,0},{1,25},{9,17},{17,9},{25,1},{2,26},{10... | collective-permute-start | bytes 1572872 | tf_op jit(solution)/shard_map/ppermute | solution.py:622
  153.2 17.9 %collective-permute-start.10 = (f32[4,2,128,128]{3,2,1,0:T(8,128)}, f32[4,2,128,128]{3,2,1,0:T(8,128)}, u32[]{:S(2)}, u32[]{:S(2)}) collective-permute-start(f32[4,2,128,128]{3,2,1,0:T(8,128)} %sum_of.2), channel_id=1, source_target_pairs={{0,2},{1,3},{2,0},{3,1},{4,6},{5,7},{6,4},{7,5},{8,10},{9,11},{10,... | collective-permute-start | bytes 1572872 | tf_op jit(solution)/shard_map/ppermute | solution.py:622
  154.8 9.5 %collective-permute-start.11 = (f32[2,2,128,128]{3,2,1,0:T(8,128)}, f32[2,2,128,128]{3,2,1,0:T(8,128)}, u32[]{:S(2)}, u32[]{:S(2)}) collective-permute-start(f32[2,2,128,128]{3,2,1,0:T(8,128)} %get-tuple-element.96), channel_id=1, source_target_pairs={{0,8},{8,0},{16,24},{24,16},{1,9},{9,1},{17,25},{25,17},{2,10},{10... | collective-permute-start | bytes 786440 | tf_op jit(solution)/shard_map/ppermute | solution.py:622
  156.0 15.1 %collective-permute-start.12 = (f32[2,2,128,128]{3,2,1,0:T(8,128)}, f32[2,2,128,128]{3,2,1,0:T(8,128)}, u32[]{:S(2)}, u32[]{:S(2)}) collective-permute-start(f32[2,2,128,128]{3,2,1,0:T(8,128)} %get-tuple-element.97), channel_id=1, source_target_pairs={{0,16},{8,24},{16,0},{24,8},{1,17},{9,25},{17,1},{25,9},{2,18},{10... | collective-permute-start | bytes 786440 | tf_op jit(solution)/shard_map/ppermute | solution.py:622
  156.9 14.2 %collective-permute-start.13 = (f32[2,2,128,128]{3,2,1,0:T(8,128)}, f32[2,2,128,128]{3,2,1,0:T(8,128)}, u32[]{:S(2)}, u32[]{:S(2)}) collective-permute-start(f32[2,2,128,128]{3,2,1,0:T(8,128)} %get-tuple-element.98), channel_id=1, source_target_pairs={{0,24},{8,16},{16,8},{24,0},{1,25},{9,17},{17,9},{25,1},{2,26},{10... | collective-permute-start | bytes 786440 | tf_op jit(solution)/shard_map/ppermute | solution.py:622
  158.3 17.5 %collective-permute-start.7 = (f32[2,2,128,128]{3,2,1,0:T(8,128)}, f32[2,2,128,128]{3,2,1,0:T(8,128)}, u32[]{:S(2)}, u32[]{:S(2)}) collective-permute-start(f32[2,2,128,128]{3,2,1,0:T(8,128)} %get-tuple-element.88), channel_id=1, source_target_pairs={{0,8},{8,0},{16,24},{24,16},{1,9},{9,1},{17,25},{25,17},{2,10},{10... | collective-permute-start | bytes 786440 | tf_op jit(solution)/shard_map/ppermute | solution.py:622
  164.3 15.7 %collective-permute-start.8 = (f32[2,2,128,128]{3,2,1,0:T(8,128)}, f32[2,2,128,128]{3,2,1,0:T(8,128)}, u32[]{:S(2)}, u32[]{:S(2)}) collective-permute-start(f32[2,2,128,128]{3,2,1,0:T(8,128)} %get-tuple-element.89), channel_id=1, source_target_pairs={{0,16},{8,24},{16,0},{24,8},{1,17},{9,25},{17,1},{25,9},{2,18},{10... | collective-permute-start | bytes 786440 | tf_op jit(solution)/shard_map/ppermute | solution.py:622
  171.1 9.0 %collective-permute-start.9 = (f32[2,2,128,128]{3,2,1,0:T(8,128)}, f32[2,2,128,128]{3,2,1,0:T(8,128)}, u32[]{:S(2)}, u32[]{:S(2)}) collective-permute-start(f32[2,2,128,128]{3,2,1,0:T(8,128)} %get-tuple-element.90), channel_id=1, source_target_pairs={{0,24},{8,16},{16,8},{24,0},{1,25},{9,17},{17,9},{25,1},{2,26},{10... | collective-permute-start | bytes 786440 | tf_op jit(solution)/shard_map/ppermute | solution.py:622
  173.2 10.4 %collective-permute-start.14 = (f32[2,2,128,128]{3,2,1,0:T(8,128)}, f32[2,2,128,128]{3,2,1,0:T(8,128)}, u32[]{:S(2)}, u32[]{:S(2)}) collective-permute-start(f32[2,2,128,128]{3,2,1,0:T(8,128)} %sum_of.3), channel_id=1, source_target_pairs={{0,4},{1,5},{2,6},{3,7},{4,0},{5,1},{6,2},{7,3},{8,12},{9,13},{10,... | collective-permute-start | bytes 786440 | tf_op jit(solution)/shard_map/ppermute | solution.py:622
